TPU v7x, 32 devices: a whole 2x2x4 slice. The times are simulated.
32 devices in a mesh: dp: 4 (over y, core), tm: 8 (over z, x).
Axes of the slice: x: 2, y: 2, z: 4, core: 2. Of those that a mesh axis runs over, the one named last changes fastest.
Arguments:
- latents: bfloat16 [4, 64, 64, 1280], P('dp', 'tm'), may hold values from -6 to 6
- conv_weight: bfloat16 [1280, 3840], replicated, may hold values from -0.09375 to 0.09375
- qkv_weight: bfloat16 [1280, 1920], replicated, may hold values from -2 to 2
- out_weight: bfloat16 [640, 1280], replicated, may hold values from -0.25 to 0.25
- out_cotangent: bfloat16 [4, 32, 64, 1280], P('dp', 'tm'), may hold values from -6 to 6
Outputs:
- input_grad: bfloat16 [4, 64, 64, 1280], P('dp', 'tm')
- conv_grad: bfloat16 [1280, 3840], P('tm')
- qkv_grad: bfloat16 [1280, 1920], P('tm')
- proj_grad: bfloat16 [640, 1280], P('tm')
All inputs are finite; a program needn't handle non-finite values.
Results may differ from a plain program's by a relative error of at most 0.04.
Values may be sent and summed in bfloat16 or wider, within the bound.
A program may use at most 192 MiB of HBM per device.

v0:
```python
import math

import jax
import jax.numpy as jnp
from jax import lax
from jax.sharding import PartitionSpec as P

HEADS = 10
HEAD = 64


EPSILON = 1e-05


def from_behind(shard, axis, by):
    devices = lax.axis_size(axis)
    pairs = [(i, i + by) for i in range(devices) if 0 <= i + by < devices]
    return lax.ppermute(shard, axis, pairs)


def dot_rows(left_side, right_side):
    return jnp.dot(left_side, right_side, preferred_element_type=jnp.float32)


def column_term(lefts, right_side):
    pieces = [
        lax.dot_general(
            operand, right_side, (((0,), (0,)), ((), ())), preferred_element_type=jnp.float32
        )
        for operand in lefts
    ]
    return jnp.concatenate(pieces, axis=1)


def head_shape(packed):
    return packed.shape[:3] + (HEADS, HEAD)


def attend_forward(qkv_loc):
    width = qkv_loc.shape[-1] // 3
    shape = head_shape(qkv_loc)
    queries = qkv_loc[..., :width].reshape(shape)
    keys = qkv_loc[..., width : 2 * width].reshape(shape)
    values = qkv_loc[..., 2 * width :].reshape(shape)
    scores = jnp.einsum(
        "vqlhd,vklhd->vlhqk", queries, keys, preferred_element_type=jnp.float32
    ) / math.sqrt(HEAD)
    highest = jnp.max(scores, axis=-1, keepdims=True)
    expo = jnp.exp(scores - highest)
    probs = expo / jnp.sum(expo, axis=-1, keepdims=True)
    probs_b = probs.astype(jnp.bfloat16)
    attended = jnp.einsum(
        "vlhqk,vklhd->vqlhd", probs_b, values, preferred_element_type=jnp.float32
    ).astype(jnp.bfloat16)
    return (attended.reshape(qkv_loc.shape[:3] + (width,)), probs, probs_b)


def attend_backward(qkv_loc, attended, probs, probs_b, grad_att):
    width = qkv_loc.shape[-1] // 3
    shape = head_shape(qkv_loc)
    queries = qkv_loc[..., :width].reshape(shape)
    keys = qkv_loc[..., width : 2 * width].reshape(shape)
    values = qkv_loc[..., 2 * width :].reshape(shape)
    grad_heads = grad_att.reshape(shape)
    grad_values = jnp.einsum(
        "vlhqk,vqlhd->vklhd", probs_b, grad_heads, preferred_element_type=jnp.float32
    ).astype(jnp.bfloat16)
    grad_probs = jnp.einsum(
        "vqlhd,vklhd->vlhqk", grad_heads, values, preferred_element_type=jnp.float32
    )
    row_delta = jnp.sum(
        grad_heads.astype(jnp.float32) * attended.reshape(shape).astype(jnp.float32), axis=-1
    )
    row_delta = jnp.transpose(row_delta, (0, 2, 3, 1))[..., None]
    grad_scores = (probs * (grad_probs - row_delta) / math.sqrt(HEAD)).astype(jnp.bfloat16)
    grad_queries = jnp.einsum(
        "vlhqk,vklhd->vqlhd", grad_scores, keys, preferred_element_type=jnp.float32
    ).astype(jnp.bfloat16)
    grad_keys = jnp.einsum(
        "vlhqk,vqlhd->vklhd", grad_scores, queries, preferred_element_type=jnp.float32
    ).astype(jnp.bfloat16)
    flat_shape = qkv_loc.shape[:3] + (width,)
    return jnp.concatenate(
        [
            grad_queries.reshape(flat_shape),
            grad_keys.reshape(flat_shape),
            grad_values.reshape(flat_shape),
        ],
        axis=-1,
    )


def local(latents, conv_weight, qkv_weight, out_weight, out_cotangent):
    videos, frames, places, width = latents.shape
    half = frames // 2
    attn_width = out_weight.shape[0]
    split = latents.reshape(videos, half, 2, places, width)
    even_frames = split[:, :, 0]
    odd_frames = split[:, :, 1]
    rim_input = from_behind(odd_frames[:, half - 1 :], "tm", 1)
    prev_frames = jnp.concatenate([rim_input, odd_frames[:, : half - 1]], axis=1)
    local_rows = videos * half * places

    def as_rows(values):
        return values.reshape(local_rows, values.shape[-1])

    tap_zero = conv_weight[:, :width]
    tap_one = conv_weight[:, width : 2 * width]
    tap_two = conv_weight[:, 2 * width :]
    prev_rows = as_rows(prev_frames)
    even_rows = as_rows(even_frames)
    odd_rows = as_rows(odd_frames)
    hidden = (
        dot_rows(prev_rows, tap_zero) + dot_rows(even_rows, tap_one) + dot_rows(odd_rows, tap_two)
    ).astype(jnp.bfloat16)
    hidden_f = hidden.astype(jnp.float32)
    centred = hidden_f - jnp.mean(hidden_f, axis=-1, keepdims=True)
    inv_std = lax.rsqrt(jnp.mean(centred * centred, axis=-1, keepdims=True) + EPSILON)
    unit_rows = centred * inv_std
    normed = unit_rows.astype(jnp.bfloat16)
    qkv_rows = (
        dot_rows(normed, qkv_weight)
        .astype(jnp.bfloat16)
        .reshape(videos, half, places, 3 * attn_width)
    )
    qkv_loc = lax.all_to_all(qkv_rows, "tm", split_axis=2, concat_axis=1, tiled=True)
    attended, probs, probs_b = attend_forward(qkv_loc)
    cotangent_rows = as_rows(out_cotangent)
    attended_time = lax.all_to_all(attended, "tm", split_axis=1, concat_axis=2, tiled=True)
    grad_time = (
        dot_rows(cotangent_rows, out_weight.T)
        .astype(jnp.bfloat16)
        .reshape(videos, half, places, attn_width)
    )
    grad_att = lax.all_to_all(grad_time, "tm", split_axis=2, concat_axis=1, tiled=True)
    proj_left = as_rows(attended_time)
    grad_qkv_loc = attend_backward(qkv_loc, attended, probs, probs_b, grad_att)
    grad_qkv = as_rows(lax.all_to_all(grad_qkv_loc, "tm", split_axis=1, concat_axis=2, tiled=True))
    grad_normed = dot_rows(grad_qkv, qkv_weight.T)
    correction = (
        grad_normed
        - jnp.mean(grad_normed, axis=-1, keepdims=True)
        - unit_rows * jnp.mean(grad_normed * unit_rows, axis=-1, keepdims=True)
    )
    grad_hidden = (cotangent_rows.astype(jnp.float32) + inv_std * correction).astype(jnp.bfloat16)
    grad_four = grad_hidden.reshape(videos, half, places, width)
    rim_after = from_behind(grad_four[:, :1], "tm", -1)
    grad_next = jnp.concatenate([grad_four[:, 1:], rim_after], axis=1)
    grad_even = dot_rows(grad_hidden, tap_one.T).astype(jnp.bfloat16)
    grad_odd = (dot_rows(grad_hidden, tap_two.T) + dot_rows(as_rows(grad_next), tap_zero.T)).astype(
        jnp.bfloat16
    )
    input_grad = jnp.stack(
        [
            grad_even.reshape(videos, half, places, width),
            grad_odd.reshape(videos, half, places, width),
        ],
        axis=2,
    ).reshape(latents.shape)
    dp_count = lax.axis_size("dp")
    tm_count = lax.axis_size("tm")
    grad_scale = 1.0 / math.sqrt(dp_count * tm_count * local_rows)
    conv_part = lax.psum_scatter(
        column_term((prev_rows, even_rows, odd_rows), grad_hidden).astype(jnp.bfloat16),
        "tm",
        scatter_dimension=0,
        tiled=True,
    )
    qkv_part = lax.psum_scatter(
        column_term((normed,), grad_qkv).astype(jnp.bfloat16), "tm", scatter_dimension=0, tiled=True
    )
    proj_part = lax.psum_scatter(
        column_term((proj_left,), cotangent_rows).astype(jnp.bfloat16),
        "tm",
        scatter_dimension=0,
        tiled=True,
    )
    conv_total, qkv_total, proj_total = (
        lax.psum(conv_part, "dp").astype(jnp.float32),
        lax.psum(qkv_part, "dp").astype(jnp.float32),
        lax.psum(proj_part, "dp").astype(jnp.float32),
    )
    conv_grad = (conv_total * grad_scale).astype(jnp.bfloat16)
    qkv_grad = (qkv_total * grad_scale).astype(jnp.bfloat16)
    proj_grad = (proj_total * grad_scale).astype(jnp.bfloat16)
    return (input_grad, conv_grad, qkv_grad, proj_grad)


def solution(mesh):
    return jax.shard_map(
        local,
        mesh=mesh,
        in_specs=(P("dp", "tm", None, None), P(), P(), P(), P("dp", "tm", None, None)),
        out_specs=(P("dp", "tm", None, None), P("tm", None), P("tm", None), P("tm", None)),
        check_vma=False,
    )
```

profile of v0, /device:TPU:17, one launch (start us, length us, event | category | flops | bytes accessed | tf_op | source)
XLA Modules:
  0.0 574.3 jit_solution(3840173619625434894)
XLA Ops:
  8.6 1.8 convolution_convert_fusion.10
  11.4 5.6 all-to-all-start.1
  17.2 3.5 collective-permute-start
  20.7 2.9 fusion.5
  24.7 4.9 collective-permute-done
  35.4 4.2 all-to-all-start
  43.3 17.2 %all-to-all-done = bf16[1,4,64,1920]{3,1,0,2:T(4,128)(2,1)} async-done(((bf16[1,4,64,1920]{3,1,0,2:T(4,128)(2,1)}), bf16[1,4,64,1920]{3,1,0,2:T(4,128)(2,1)}, u32[]{:S(2)}, u32[]{:S(2)}) %all-to-all-start) | async-done | bytes 983072 | tf_op jit(solution)/shard_map/all_to_all | solution.py:126
  66.6 3.7 fusion.74
  70.4 3.2 fusion.45
  73.6 2.1 fusion.41
  80.1 1.8 reshape.168
  83.2 1.8 reshape.169
  85.1 2.4 copy.105
  87.5 1.8 reshape.170
  89.4 29.1 %all_to_all.63 = bf16[1,32,8,1920]{3,2,0,1:T(8,128)(2,1)S(1)} all-to-all(bf16[1,32,8,1920]{3,2,0,1:T(8,128)(2,1)S(1)} %maximum_bitcast_fusion), channel_id=1, replica_groups=mesh['dp'=4,'tm'=8] {'tm'}, dimensions={1} | all-to-all | bytes 1966080 | tf_op jit(solution)/shard_map/all_to_all | solution.py:138
  118.6 4.5 fusion.71
  127.4 4.4 pad_maximum_fusion
  131.8 13.7 %copy.116 = bf16[1280,3840]{1,0:T(8,128)(2,1)} copy(bf16[1280,3840]{0,1:T(8,128)(2,1)} %pad_maximum_fusion) | data formatting | bytes 19660800
  147.7 22.8 %all_to_all.64 = bf16[1,32,8,640]{3,2,0,1:T(8,128)(2,1)S(1)} all-to-all(bf16[1,32,8,640]{3,2,0,1:T(8,128)(2,1)S(1)} %bitcast.115), channel_id=1, replica_groups=mesh['dp'=4,'tm'=8] {'tm'}, dimensions={1} | all-to-all | bytes 655360 | tf_op jit(solution)/shard_map/all_to_all | solution.py:129
  170.5 1.8 convolution_convert_fusion.4
  173.5 4.0 convolution_convert_fusion
  177.6 2.2 collective-permute-start.1
  179.8 3.0 fusion.24
  182.8 140.9 %reduce-scatter.10.cloned.1.call-done = bf16[160,3840]{1,0:T(8,128)(2,1)} async-done(((bf16[1280,3840]{1,0:T(8,128)(2,1)}), bf16[160,3840]{1,0:T(8,128)(2,1)}) %reduce-scatter.10.cloned.1.call-update) | async-done | bytes 1228816
  323.7 3.6 copy.117
  327.3 62.7 %reduce-scatter.8.cloned.1.call-done = bf16[80,1280]{1,0:T(8,128)(2,1)} async-done(((bf16[640,1280]{1,0:T(8,128)(2,1)}), bf16[80,1280]{1,0:T(8,128)(2,1)}) %reduce-scatter.8.cloned.1.call-update) | async-done | bytes 204816 | tf_op jit(solution)/shard_map/reduce_scatter | solution.py:172
  390.0 103.9 %reduce-scatter.6.cloned.1.call-done = bf16[160,1920]{1,0:T(8,128)(2,1)} async-done(((bf16[1280,1920]{1,0:T(8,128)(2,1)}), bf16[160,1920]{1,0:T(8,128)(2,1)}) %reduce-scatter.6.cloned.1.call-update) | async-done | bytes 614416 | tf_op jit(solution)/shard_map/reduce_scatter | solution.py:169
  494.0 3.0 fusion.3
  497.1 3.0 fusion.27
  501.3 57.8 %all-reduce.3.cloned.1.call-done = (bf16[160,3840]{0,1:T(8,128)(2,1)}, bf16[160,1920]{1,0:T(8,128)(2,1)}, bf16[80,1280]{1,0:T(8,128)(2,1)}) async-done(((bf16[160,3840]{0,1:T(8,128)(2,1)}, bf16[160,1920]{1,0:T(8,128)(2,1)}, bf16[80,1280]{1,0:T(8,128)(2,1)}), (bf16[160,3840]{0,1:T(8,128)(2,1)}, bf16[160,1920]{1,0:T(8,128)(2,1)}, bf16[80,1280]{1,0:T(8,128)(2,1)})) %all-reduce.3.cloned.1.call-update) | async-done | bytes 2048016 | tf_op jit(solution)/shard_map/psum | solution.py:179
  559.1 3.2 multiply_convert_fusion
  562.3 3.8 copy.112
  (100 shorter events, 35.7 us)
Async XLA Ops:
  7.2 1.4 copy-start
  10.4 6.6 %copy-start.13 = (bf16[1,8,64,1280]{3,2,1,0:T(8,128)(2,1)S(1)}, bf16[1,8,64,1280]{3,2,1,0:T(8,128)(2,1)}, u32[]{:S(2)}) copy-start(bf16[1,8,64,1280]{3,2,1,0:T(8,128)(2,1)} %param.5) | copy-start | bytes 3932164
  11.4 24.0 %all-to-all-start.1 = ((bf16[1,4,64,640]{3,1,0,2:T(4,128)(2,1)}), bf16[1,4,64,640]{3,1,0,2:T(4,128)(2,1)S(1)}, u32[]{:S(2)}, u32[]{:S(2)}) async-start(bf16[1,4,64,640]{3,1,0,2:T(4,128)(2,1)} %copy.89), calls=%async_computation.1 | async-start | bytes 655360 | tf_op jit(solution)/shard_map/all_to_all | solution.py:135
  17.0 6.7 %copy-start.14 = (bf16[1280,3840]{1,0:T(8,128)(2,1)S(1)}, bf16[1280,3840]{1,0:T(8,128)(2,1)}, u32[]{:S(2)}) copy-start(bf16[1280,3840]{1,0:T(8,128)(2,1)} %param.6) | copy-start | bytes 29491204
  17.1 6.5 %copy-start.10 = (bf16[1,4,1,64,1280]{4,3,2,1,0:T(8,128)(2,1)}, bf16[1,4,1,64,1280]{4,3,2,1,0:T(8,128)(2,1)S(1)}, u32[]{:S(2)}) copy-start(bf16[1,4,1,64,1280]{4,3,2,1,0:T(8,128)(2,1)S(1)} %get-tuple-element.31) | copy-start | bytes 1966084
  17.1 6.5 %copy-start.8 = (bf16[1,4,1,64,1280]{4,3,2,1,0:T(8,128)(2,1)}, bf16[1,4,1,64,1280]{4,3,2,1,0:T(8,128)(2,1)S(1)}, u32[]{:S(2)}) copy-start(bf16[1,4,1,64,1280]{4,3,2,1,0:T(8,128)(2,1)S(1)} %get-tuple-element.30) | copy-start | bytes 1966084
  17.2 12.5 %collective-permute-start = (bf16[1,1,64,1280]{3,2,1,0:T(8,128)(2,1)S(1)}, bf16[1,1,64,1280]{3,2,1,0:T(8,128)(2,1)S(1)}, u32[]{:S(2)}, u32[]{:S(2)}) collective-permute-start(bf16[1,1,64,1280]{3,2,1,0:T(8,128)(2,1)S(1)} %slice.52), channel_id=1, source_target_pairs={{0,1},{1,2},{2,3},{3,4},{4,5},{5,6},{6,7},{8,9},{9,10},{10,11},{11... | collective-permute-start | bytes 491528 | tf_op jit(solution)/shard_map/ppermute | solution.py:18
  29.7 2.2 slice-start
  29.7 2.4 slice-start.1
  35.4 25.1 %all-to-all-start = ((bf16[1,4,64,1920]{3,1,0,2:T(4,128)(2,1)}), bf16[1,4,64,1920]{3,1,0,2:T(4,128)(2,1)}, u32[]{:S(2)}, u32[]{:S(2)}) async-start(bf16[1,4,64,1920]{3,1,0,2:T(4,128)(2,1)} %copy.84), calls=%async_computation | async-start | bytes 1966080 | tf_op jit(solution)/shard_map/all_to_all | solution.py:126
  39.6 284.0 %reduce-scatter.10.cloned.1.call-start = ((), (), s32[]{:S(2)}) async-start(), calls=%async_computation.9 | async-start | bytes 11059200
  70.4 3.2 copy-start.12
  70.4 3.2 copy-start.16
  70.4 3.2 copy-start.19
  73.6 2.1 copy-start.15
  75.7 1.2 copy-start.4
  76.9 1.2 copy-start.5
  118.6 4.5 copy-start.2
  118.6 4.5 copy-start.6
  123.1 1.1 copy-start.11
  124.2 1.1 copy-start.9
  145.6 244.4 %reduce-scatter.8.cloned.1.call-start = ((), (), s32[]{:S(2)}) async-start(), calls=%async_computation.8 | async-start | bytes 1843200 | tf_op jit(solution)/shard_map/reduce_scatter | solution.py:172
  147.7 22.8 %copy-start.7 = (bf16[1,4,64,1280]{3,2,1,0:T(8,128)(2,1)S(1)}, bf16[1,4,64,1280]{3,2,1,0:T(8,128)(2,1)}, u32[]{:S(2)}) copy-start(bf16[1,4,64,1280]{3,2,1,0:T(8,128)(2,1)} %param.9) | copy-start | bytes 1966084
  172.3 1.2 copy-start.3
  172.4 321.6 %reduce-scatter.6.cloned.1.call-start = ((), (), s32[]{:S(2)}) async-start(), calls=%async_computation.7 | async-start | bytes 5529600 | tf_op jit(solution)/shard_map/reduce_scatter | solution.py:169
  177.6 381.6 %all-reduce.3.cloned.1.call-start = ((), (), s32[]{:S(2)}) async-start(), calls=%async_computation.10 | async-start | bytes 5570560 | tf_op jit(solution)/shard_map/psum | solution.py:179
  177.6 319.4 %collective-permute-start.1 = (bf16[1,1,64,1280]{3,2,1,0:T(8,128)(2,1)S(1)}, bf16[1,1,64,1280]{3,2,1,0:T(8,128)(2,1)S(1)}, u32[]{:S(2)}, u32[]{:S(2)}) collective-permute-start(bf16[1,1,64,1280]{3,2,1,0:T(8,128)(2,1)S(1)} %slice.59), channel_id=1, source_target_pairs={{1,0},{2,1},{3,2},{4,3},{5,4},{6,5},{7,6},{9,8},{10,9},{11,10},{12... | collective-permute-start | bytes 491528 | tf_op jit(solution)/shard_map/ppermute | solution.py:18
  562.3 3.8 copy-start.18
  562.3 4.5 copy-start.17
  562.3 5.5 copy-start.1
Sparse Core Ops, SparseCore 0:
  145.7 177.8 reduce-scatter.9
  327.1 62.8 reduce-scatter.7
  394.2 99.7 reduce-scatter.5
  496.3 62.7 all-reduce.2
where the time goes:
time: 578 us; the launch traced here: 574 us
  waiting for transfers between devices  387 us (67%)
  local copies, waits for them, and re-layouts  52.3 us (9%)
  blocking collectives  51.8 us (9%)
  matrix products  42.2 us (7%)
  starting transfers between devices  15.8 us (3%)
  between operations  14.2 us (2%)
  other arithmetic  10.5 us (2%)
    unnamed x5, waiting for transfers between devices  141 us
    reduce_scatter x1, waiting for transfers between devices, local(): lax.psum_scatter(column_term((normed,), grad_qkv).astype(jnp.bfloat16), '...  104 us
    reduce_scatter x1, waiting for transfers between devices, local(): lax.psum_scatter(column_term((proj_left,), cotangent_rows).astype(jnp.bfl...  62.7 us
    psum x1, waiting for transfers between devices, local(): lax.psum(conv_part, 'dp').astype(jnp.float32)  57.8 us
    all_to_all x1, blocking collectives, local(): lax.all_to_all(grad_qkv_loc, 'tm', split_axis=1, concat_axis=2, tiled=True)  29.1 us
    unnamed x47, local copies, waits for them, and re-layouts  26.2 us
    all_to_all x1, blocking collectives, local(): lax.all_to_all(attended, 'tm', split_axis=1, concat_axis=2, tiled=True)  22.8 us
    dot_general x9, matrix products, dot_rows(): return jnp.dot(left_side, right_side, preferred_element_type=jnp.float32)  22 us
  transfers between devices with their start and end apart: 8, of which 6 were waited for; matrix products, arithmetic and copies ran while one was open for 6% of the time, Pallas kernels for 0%

commit v1 on v0

v1 whole, which is shorter than its diff:
```python
import functools
import math

import jax
import jax.numpy as jnp
from jax import lax
from jax.experimental import pallas as pl
from jax.experimental.pallas import tpu as pltpu
from jax.sharding import PartitionSpec as P

HEADS = 10
HEAD = 64


EPSILON = 1e-05


def from_behind(shard, axis, by):
    devices = lax.axis_size(axis)
    pairs = [(i, i + by) for i in range(devices) if 0 <= i + by < devices]
    return lax.ppermute(shard, axis, pairs)


def swap(shard, axis, bit):
    devices = lax.axis_size(axis)
    return lax.ppermute(shard, axis, [(i, i ^ (1 << bit)) for i in range(devices)])


def bit_of(axis, bit):
    return (lax.axis_index(axis) >> bit) & 1


def dot_rows(left_side, right_side):
    return jnp.dot(left_side, right_side, preferred_element_type=jnp.float32)


def dot_rows_t(left_side, right_side):
    return lax.dot_general(
        left_side, right_side, (((1,), (1,)), ((), ())), preferred_element_type=jnp.float32
    )


def dot_columns(left_side, right_side):
    return lax.dot_general(
        left_side, right_side, (((0,), (0,)), ((), ())), preferred_element_type=jnp.float32
    )


def attention_kernel(loc, width, packed_ref, result_ref):
    rows = packed_ref.shape[0]
    row_at = lax.broadcasted_iota(jnp.int32, (rows, rows), 0)
    column_at = lax.broadcasted_iota(jnp.int32, (rows, rows), 1)
    same = (row_at % loc) == (column_at % loc)
    lane = lax.broadcasted_iota(jnp.int32, (rows, 2 * HEAD), 1)
    scale = 1.0 / math.sqrt(HEAD)
    for pair in range(width // (2 * HEAD)):
        first = pair * 2 * HEAD
        q = packed_ref[:, first : first + 2 * HEAD]
        k = packed_ref[:, width + first : width + first + 2 * HEAD]
        v = packed_ref[:, 2 * width + first : 2 * width + first + 2 * HEAD]
        g = packed_ref[:, 3 * width + first : 3 * width + first + 2 * HEAD]
        zero = jnp.zeros_like(q)
        grad_q = grad_k = grad_v = attended = None
        kept = []
        for head in range(2):
            mine = (lane >= HEAD) if head else (lane < HEAD)
            q_h = jnp.where(mine, q, zero)
            v_h = jnp.where(mine, v, zero)
            g_h = jnp.where(mine, g, zero)
            scores = jnp.where(same, dot_rows_t(q_h, k) * scale, -1e30)
            expo = jnp.exp(scores - jnp.max(scores, axis=1, keepdims=True))
            probs = expo * (1.0 / jnp.sum(expo, axis=1, keepdims=True))
            probs_b = probs.astype(jnp.bfloat16)
            part = dot_rows(probs_b, v_h)
            attended = part if attended is None else attended + part
            part = dot_columns(probs_b, g_h)
            grad_v = part if grad_v is None else grad_v + part
            grad_probs = dot_rows_t(g_h, v)
            kept.append((mine, q_h, probs, grad_probs))
        attended_b = attended.astype(jnp.bfloat16)
        product = g.astype(jnp.float32) * attended_b.astype(jnp.float32)
        for mine, q_h, probs, grad_probs in kept:
            k_h = jnp.where(mine, k, zero)
            delta = jnp.sum(jnp.where(mine, product, 0.0), axis=1, keepdims=True)
            grad_scores = (probs * (grad_probs - delta) * scale).astype(jnp.bfloat16)
            part = dot_rows(grad_scores, k_h)
            grad_q = part if grad_q is None else grad_q + part
            part = dot_columns(grad_scores, q_h)
            grad_k = part if grad_k is None else grad_k + part
        result_ref[:, first : first + 2 * HEAD] = grad_q.astype(jnp.bfloat16)
        result_ref[:, width + first : width + first + 2 * HEAD] = grad_k.astype(jnp.bfloat16)
        result_ref[:, 2 * width + first : 2 * width + first + 2 * HEAD] = grad_v.astype(
            jnp.bfloat16
        )
        result_ref[:, 3 * width + first : 3 * width + first + 2 * HEAD] = attended_b


def attention(packed, loc, width):
    rows = packed.shape[0]
    return pl.pallas_call(
        functools.partial(attention_kernel, loc, width),
        out_shape=jax.ShapeDtypeStruct(packed.shape, jnp.bfloat16),
        in_specs=[pl.BlockSpec(memory_space=pltpu.VMEM)],
        out_specs=pl.BlockSpec(memory_space=pltpu.VMEM),
        compiler_params=pltpu.CompilerParams(vmem_limit_bytes=40 * 1024 * 1024),
        cost_estimate=pl.CostEstimate(
            flops=14 * HEADS * rows * rows * 2 * HEAD,
            bytes_accessed=2 * packed.size * 2,
            transcendentals=HEADS * rows * rows,
        ),
    )(packed)


def halve(array, position, axis, bit):
    mine = bit_of(axis, bit)
    away = lax.dynamic_index_in_dim(array, 1 - mine, position, keepdims=False)
    stay = lax.dynamic_index_in_dim(array, mine, position, keepdims=False)
    came = swap(away, axis, bit)
    return (stay.astype(jnp.float32) + came.astype(jnp.float32)).astype(jnp.bfloat16)


def join(array, axis, bit, position):
    came = swap(array, axis, bit)
    first = bit_of(axis, bit) == 0
    return jnp.concatenate(
        [jnp.where(first, array, came), jnp.where(first, came, array)], axis=position
    )


def sum_over_devices(share, bits, y_first, scale):
    if y_first:
        share = halve(share, bits + 1, "dp", 1)
        share = halve(share, bits, "tm", 0)
    else:
        share = halve(share, bits, "tm", 0)
        share = halve(share, bits, "dp", 1)
    for bit in range(1, bits):
        share = halve(share, bits - bit, "tm", bit)
    share = (share.astype(jnp.float32) * scale).astype(jnp.bfloat16)
    return join(share, "dp", 1, 1)


def local(latents, conv_weight, qkv_weight, out_weight, out_cotangent):
    videos, frames, places, width = latents.shape
    half = frames // 2
    attn_width = out_weight.shape[0]
    dp_count = lax.axis_size("dp")
    tm_count = lax.axis_size("tm")
    bits = tm_count.bit_length() - 1
    loc = places // tm_count
    rows = half * places
    core = bit_of("dp", 0)

    def as_rows(values):
        return values.reshape(rows, values.shape[-1])

    def own_half(values, which):
        size = values.shape[-1] // 2
        return lax.dynamic_slice_in_dim(values, which * size, size, axis=values.ndim - 1)

    split = latents.reshape(half, 2, tm_count, loc, width)
    rim_input = from_behind(split[half - 1, 1], "tm", 1)
    split = jnp.transpose(split, (1, 2, 0, 3, 4))
    even_frames, odd_frames = split[0], split[1]
    prev_frames = jnp.concatenate([rim_input[:, None], odd_frames[:, : half - 1]], axis=1)
    cotangent_rows = as_rows(
        jnp.transpose(out_cotangent.reshape(half, tm_count, loc, width), (1, 0, 2, 3))
    )

    tap_zero = conv_weight[:, :width]
    tap_one = conv_weight[:, width : 2 * width]
    tap_two = conv_weight[:, 2 * width :]
    prev_rows = as_rows(prev_frames)
    even_rows = as_rows(even_frames)
    odd_rows = as_rows(odd_frames)
    conv_left = jnp.concatenate([prev_rows, even_rows, odd_rows], axis=1)
    conv_left_other = swap(conv_left, "dp", 0)
    cot_half = own_half(cotangent_rows, core)
    cot_half_other = swap(own_half(cotangent_rows, 1 - core), "dp", 0)

    grad_att = dot_rows_t(cotangent_rows, out_weight).astype(jnp.bfloat16)
    hidden = (
        dot_rows(prev_rows, tap_zero) + dot_rows(even_rows, tap_one) + dot_rows(odd_rows, tap_two)
    ).astype(jnp.bfloat16)
    hidden_f = hidden.astype(jnp.float32)
    centred = hidden_f - jnp.mean(hidden_f, axis=-1, keepdims=True)
    inv_std = lax.rsqrt(jnp.mean(centred * centred, axis=-1, keepdims=True) + EPSILON)
    unit_rows = centred * inv_std
    normed = unit_rows.astype(jnp.bfloat16)
    normed_other = swap(normed, "dp", 0)
    qkv_rows = dot_rows(normed, qkv_weight).astype(jnp.bfloat16)

    outgoing = jnp.concatenate([qkv_rows, grad_att], axis=1).reshape(tm_count, half * loc, -1)
    packed = lax.all_to_all(outgoing, "tm", split_axis=0, concat_axis=0, tiled=True)
    result = attention(packed.reshape(rows, 4 * attn_width), loc, attn_width)
    result = lax.all_to_all(
        result.reshape(tm_count, half * loc, 4 * attn_width),
        "tm",
        split_axis=0,
        concat_axis=0,
        tiled=True,
    ).reshape(rows, 4 * attn_width)
    grad_qkv = result[:, : 3 * attn_width]
    attended = result[:, 3 * attn_width :]

    grad_scale = 1.0 / math.sqrt(dp_count * tm_count * rows)

    def by_bits(share, taps, parts):
        channels = share.shape[0] // taps
        size = channels // tm_count // math.prod(parts)
        return share.reshape((taps,) + (2,) * bits + parts + (size, share.shape[1]))

    def summed(share, taps):
        share = by_bits(share, taps, (2, 2))
        ahead = lax.index_in_dim(share, 0, bits + 1, keepdims=False)
        behind = lax.index_in_dim(share, 1, bits + 1, keepdims=False)
        return jnp.concatenate(
            [
                sum_over_devices(ahead, bits, False, grad_scale),
                sum_over_devices(behind, bits, True, grad_scale),
            ],
            axis=1,
        )

    attended_other = swap(attended, "dp", 0)
    proj_share = (
        dot_columns(attended, cot_half) + dot_columns(attended_other, cot_half_other)
    ).astype(jnp.bfloat16)
    gq_half = own_half(grad_qkv, core)
    gq_half_other = swap(own_half(grad_qkv, 1 - core), "dp", 0)
    qkv_share = (dot_columns(normed, gq_half) + dot_columns(normed_other, gq_half_other)).astype(
        jnp.bfloat16
    )

    grad_normed = dot_rows_t(grad_qkv, qkv_weight)
    correction = (
        grad_normed
        - jnp.mean(grad_normed, axis=-1, keepdims=True)
        - unit_rows * jnp.mean(grad_normed * unit_rows, axis=-1, keepdims=True)
    )
    grad_hidden = (cotangent_rows.astype(jnp.float32) + inv_std * correction).astype(jnp.bfloat16)
    gh_half = own_half(grad_hidden, core)
    gh_half_other = swap(own_half(grad_hidden, 1 - core), "dp", 0)
    conv_share = (
        dot_columns(conv_left, gh_half) + dot_columns(conv_left_other, gh_half_other)
    ).astype(jnp.bfloat16)

    proj_sum = sum_over_devices(by_bits(proj_share, 1, (2,)), bits, True, grad_scale)
    qkv_sum = summed(qkv_share, 1)
    conv_sum = summed(conv_share, 3)

    grad_four = grad_hidden.reshape(tm_count, half, loc, width)
    rim_after = from_behind(grad_four[:, 0], "tm", -1)
    grad_next = jnp.concatenate([grad_four[:, 1:], rim_after[:, None]], axis=1)
    grad_even = dot_rows_t(grad_hidden, tap_one).astype(jnp.bfloat16)
    grad_odd = (dot_rows_t(grad_hidden, tap_two) + dot_rows_t(as_rows(grad_next), tap_zero)).astype(
        jnp.bfloat16
    )
    by_frame = (tm_count, half, loc, width)
    input_grad = jnp.transpose(
        jnp.stack([grad_even.reshape(by_frame), grad_odd.reshape(by_frame)], axis=0),
        (2, 0, 1, 3, 4),
    ).reshape(latents.shape)

    proj_grad = join(proj_sum[0], "dp", 0, 1)
    qkv_grad = join(qkv_sum[0], "dp", 0, 1)
    conv_both = join(conv_sum[:, :, None], "dp", 0, 2)
    conv_grad = jnp.transpose(conv_both, (1, 0, 2, 3)).reshape(conv_both.shape[1], 3 * width)
    return (input_grad, conv_grad, qkv_grad, proj_grad)


def solution(mesh):
    return jax.shard_map(
        local,
        mesh=mesh,
        in_specs=(P("dp", "tm", None, None), P(), P(), P(), P("dp", "tm", None, None)),
        out_specs=(P("dp", "tm", None, None), P("tm", None), P("tm", None), P("tm", None)),
        check_vma=False,
    )
```

time: 578 us -> 262 us (0.45)
  waiting for transfers between devices: 387 us -> 102 us
  starting transfers between devices: 15.8 us -> 49.8 us
  local copies, waits for them, and re-layouts: 52.3 us -> 20.7 us
  blocking collectives: 51.8 us -> 33.5 us
  between operations: 14.2 us -> 1.48 us
  matrix products: 42.2 us -> 32.2 us
  Pallas kernels: 0 us -> 5.86 us
    reduce_scatter x2 -> x0, waiting for transfers between devices: 167 us -> none  [the longest x1 104 us: local(): lax.psum_scatter(column_term((normed,), grad_qkv).astype(jnp.bfloat16), '...]
    unnamed x5 -> x0, waiting for transfers between devices: 141 us -> none
    ppermute x0 -> x34, waiting for transfers between devices: none -> 81.3 us  [swap(): lax.ppermute(shard, axis, [(i, i ^ 1 << bit) for i in range(devices)])]
    psum x1 -> x0, waiting for transfers between devices: 57.8 us -> none  [local(): lax.psum(conv_part, 'dp').astype(jnp.float32)]
    ppermute x0 -> x34, starting transfers between devices: none -> 36.4 us  [swap(): lax.ppermute(shard, axis, [(i, i ^ 1 << bit) for i in range(devices)])]
    unnamed x47 -> x36, local copies, waits for them, and re-layouts: 26.2 us -> 4.17 us
    all_to_all x2 -> x1, blocking collectives: 51.8 us -> 33.5 us  [local(): lax.all_to_all(outgoing, 'tm', split_axis=0, concat_axis=0, tiled=True)]
    dot_general x9 -> x4, matrix products: 22 us -> 6.91 us  [dot_rows(): return jnp.dot(left_side, right_side, preferred_element_type=jnp.float32)]
  transfers between devices with their start and end apart: 8 -> 37, of which waited for: 6 -> 16; matrix products, arithmetic and copies ran while one was open for 6% -> 21% of each run, Pallas kernels for 0% -> 0%
where the time goes in v1:
time: 262 us; the launch traced here: 257 us
  waiting for transfers between devices  102 us (39%)
  starting transfers between devices  49.8 us (19%)
  blocking collectives  33.5 us (13%)
  matrix products  32.2 us (12%)
  local copies, waits for them, and re-layouts  20.7 us (8%)
  other arithmetic  11.4 us (4%)
  Pallas kernels  5.86 us (2%)
    ppermute x34, waiting for transfers between devices, swap(): lax.ppermute(shard, axis, [(i, i ^ 1 << bit) for i in range(devices)])  81.3 us
    ppermute x34, starting transfers between devices, swap(): lax.ppermute(shard, axis, [(i, i ^ 1 << bit) for i in range(devices)])  36.4 us
    all_to_all x1, blocking collectives, local(): lax.all_to_all(outgoing, 'tm', split_axis=0, concat_axis=0, tiled=True)  33.5 us
    all_to_all x1, waiting for transfers between devices, local(): lax.all_to_all(result.reshape(tm_count, half * loc, 4 * attn_width), 'tm'...  20.7 us
    dot_general x5, matrix products, dot_rows_t(): lax.dot_general(left_side, right_side, (((1,), (1,)), ((), ())), preferre...  13.8 us
    dot_general x6, matrix products, dot_columns(): lax.dot_general(left_side, right_side, (((0,), (0,)), ((), ())), preferre...  11.5 us
    ppermute x2, starting transfers between devices, from_behind(): return lax.ppermute(shard, axis, pairs)  7.84 us
    dot_general x4, matrix products, dot_rows(): return jnp.dot(left_side, right_side, preferred_element_type=jnp.float32)  6.91 us
  transfers between devices with their start and end apart: 37, of which 16 were waited for; matrix products, arithmetic and copies ran while one was open for 21% of the time, Pallas kernels for 0%

profile of v1, /device:TPU:17, one launch (start us, length us, event | category | flops | bytes accessed | tf_op | source)
XLA Modules:
  0.0 256.9 jit_solution(9704164319966077714)
XLA Ops:
  1.7 3.1 %collective-permute-start = (bf16[8,8,1280]{2,1,0:T(8,128)(2,1)S(1)}, bf16[8,8,1280]{2,1,0:T(8,128)(2,1)S(1)}, u32[]{:S(2)}, u32[]{:S(2)}) collective-permute-start(bf16[8,8,1280]{2,1,0:T(8,128)(2,1)S(1)} %slice_bitcast_fusion.1), channel_id=1, source_target_pairs={{0,1},{1,2},{2,3},{3,4},{4,5},{5,6},{6,7},{8,9},{9,10},{10,11},{11... | collective-permute-start | bytes 491528 | tf_op jit(solution)/shard_map/ppermute | solution.py:21
  7.7 3.2 %fusion.6 = f32[256,1280]{1,0:T(8,128)S(1)} fusion(bf16[256,1280]{1,0:T(8,128)(2,1)S(1)} %bitcast.189, bf16[1280,3840]{1,0:T(8,128)(2,1)} %param.6), kind=kOutput, calls=%fused_computation.8 | convolution fusion | flops 838860800 | bytes 5242880 | tf_op jit(solution)/shard_map/dot_general | solution.py:34
  17.9 33.5 %all_to_all.10 = bf16[8,32,2560]{2,1,0:T(8,128)(2,1)S(1)} all-to-all(bf16[8,32,2560]{2,1,0:T(8,128)(2,1)S(1)} %bitcast.203), channel_id=1, replica_groups=mesh['dp'=4,'tm'=8] {'tm'}, dimensions={0} | all-to-all | bytes 2621440 | tf_op jit(solution)/shard_map/all_to_all | solution.py:194
  51.3 5.9 %shard_map.84 = bf16[256,2560]{1,0:T(8,128)(2,1)} custom-call(bf16[256,2560]{1,0:T(8,128)(2,1)S(1)} %bitcast.182), custom_call_target="tpu_custom_call" | custom-call | flops 1174405120 | bytes 2621440 | tf_op jit(solution)/shard_map/pallas_call | solution.py:100
  57.2 5.5 %all-to-all-start.1 = ((bf16[8,32,2560]{2,1,0:T(8,128)(2,1)}), bf16[8,32,2560]{2,1,0:T(8,128)(2,1)S(1)}, u32[]{:S(2)}, u32[]{:S(2)}) async-start(bf16[8,32,2560]{2,1,0:T(8,128)(2,1)} %bitcast.15), calls=%async_computation.1 | async-start | bytes 2621440 | tf_op jit(solution)/shard_map/all_to_all | solution.py:196
  66.1 2.7 %pad_maximum_fusion = bf16[256,3840]{1,0:T(8,128)(2,1)} fusion(bf16[256,1280]{1,0:T(8,128)(2,1)} %bitcast.193, bf16[256,1280]{1,0:T(8,128)(2,1)S(1)} %bitcast.190, bf16[256,1280]{1,0:T(8,128)(2,1)} %bitcast.196), kind=kLoop, calls=%fused_computation.26 | loop fusion | flops 5898240 | bytes 3932160 | tf_op jit(solution)/shard_map/concatenate | solution.py:176
  69.4 20.7 %all-to-all-done.1 = bf16[8,32,2560]{2,1,0:T(8,128)(2,1)S(1)} async-done(((bf16[8,32,2560]{2,1,0:T(8,128)(2,1)}), bf16[8,32,2560]{2,1,0:T(8,128)(2,1)S(1)}, u32[]{:S(2)}, u32[]{:S(2)}) %all-to-all-start.1) | async-done | bytes 1310752 | tf_op jit(solution)/shard_map/all_to_all | solution.py:196
  90.1 4.1 %fusion.66 = (f32[256]{0:T(256)S(1)}, f32[256]{0:T(256)S(1)}, f32[256,1280]{1,0:T(8,128)S(1)}) fusion(f32[256]{0:T(256)S(1)} %add_rsqrt_fusion, f32[256,1280]{1,0:T(8,128)S(1)} %get-tuple-element.36, f32[256]{0:T(256)S(1)} %broadcast_multiply_fusion.2, bf16[1280,1920]{1,0:T(8,128)(2,1)} %param.7, bf16[256,2560]{1,0:T(8,128)(2,1)S(1)} %bitcast.186), kind=kOutput, calls=%fused_computation.152 | convolution fusion | flops 1259929088 | bytes 8523776 | tf_op jit(solution)/shard_map/dot_general | solution.py:38
  94.8 3.0 %fusion = f32[256,1280]{1,0:T(8,128)S(1)} fusion(bf16[256,1280]{1,0:T(8,128)(2,1)S(1)} %add_convert_fusion.3, bf16[1280,3840]{1,0:T(8,128)(2,1)} %param.6), kind=kOutput, calls=%fused_computation.2 | convolution fusion | flops 838860800 | bytes 5242880 | tf_op jit(solution)/shard_map/dot_general | solution.py:38
  97.8 3.0 %fusion.21 = bf16[256,1280]{1,0:T(8,128)(2,1)S(1)} fusion(bf16[256,1280]{1,0:T(8,128)(2,1)S(1)} %add_convert_fusion.3, bf16[1280,3840]{1,0:T(8,128)(2,1)} %param.6), kind=kOutput, calls=%fused_computation.17 | convolution fusion | flops 839188480 | bytes 4587520 | tf_op jit(solution)/shard_map/dot_general | solution.py:38
  101.3 4.7 %collective-permute-start.1 = (bf16[8,8,1280]{2,1,0:T(8,128)(2,1)S(1)}, bf16[8,8,1280]{2,1,0:T(8,128)(2,1)S(1)}, u32[]{:S(2)}, u32[]{:S(2)}) collective-permute-start(bf16[8,8,1280]{2,1,0:T(8,128)(2,1)S(1)} %slice_bitcast_fusion), channel_id=1, source_target_pairs={{1,0},{2,1},{3,2},{4,3},{5,4},{6,5},{7,6},{9,8},{10,9},{11,10},{12... | collective-permute-start | bytes 491528 | tf_op jit(solution)/shard_map/ppermute | solution.py:21
  110.9 3.0 %fusion.30 = bf16[256,1280]{1,0:T(8,128)(2,1)S(1)} fusion(f32[256,1280]{1,0:T(8,128)S(1)} %fusion, bf16[256,1280]{1,0:T(8,128)(2,1)S(1)} %bitcast.212, bf16[1280,3840]{1,0:T(8,128)(2,1)} %param.6), kind=kOutput, calls=%fused_computation.20 | convolution fusion | flops 839516160 | bytes 5898240 | tf_op jit(solution)/shard_map/dot_general | solution.py:38
  118.8 3.3 %add_convert_fusion = bf16[3840,640]{1,0:T(8,128)(2,1)S(1)} fusion(f32[3840,640]{1,0:T(8,128)S(1)} %fusion.52, bf16[256,3840]{1,0:T(8,128)(2,1)} %collective-permute-done.2, bf16[256,640]{1,0:T(8,128)(2,1)S(1)} %collective-permute-done.3), kind=kOutput, calls=%fused_computation | convolution fusion | flops 1263206400 | bytes 17039360 | tf_op jit(solution)/shard_map/dot_general | solution.py:44
  125.4 2.0 collective-permute-start.4
  128.8 3.5 %add_convert_fusion.1 = bf16[1280,960]{0,1:T(8,128)(2,1)} fusion(f32[1280,960]{0,1:T(8,128)S(1)} %fusion.45, bf16[256,1280]{1,0:T(8,128)(2,1)} %collective-permute-done.15, bf16[256,960]{1,0:T(8,128)(2,1)S(1)} %collective-permute-done.16), kind=kOutput, calls=%fused_computation.1 | convolution fusion | flops 631603200 | bytes 8519680 | tf_op jit(solution)/shard_map/dot_general | solution.py:44
  132.3 3.0 %copy.36 = bf16[1280,960]{1,0:T(8,128)(2,1)S(1)} copy(bf16[1280,960]{0,1:T(8,128)(2,1)} %add_convert_fusion.1) | data formatting | bytes 4915200 | tf_op jit(solution)/shard_map/convert_element_type | solution.py:231
  135.8 22.9 %collective-permute-done.31 = bf16[1,2,2,40,640]{4,3,1,2,0:T(8,128)(2,1)S(1)} collective-permute-done((bf16[1,2,2,40,640]{4,3,1,2,0:T(8,128)(2,1)S(1)}, bf16[1,2,2,40,640]{4,3,1,2,0:T(8,128)(2,1)S(1)}, u32[]{:S(2)}, u32[]{:S(2)}) %collective-permute-start.31) | collective-permute-done | bytes 204832 | tf_op jit(solution)/shard_map/ppermute | solution.py:26
  162.4 2.9 %collective-permute-start.33 = (bf16[1,40,640]{2,1,0:T(8,128)(2,1)S(1)}, bf16[1,40,640]{2,1,0:T(8,128)(2,1)S(1)}, u32[]{:S(2)}, u32[]{:S(2)}) collective-permute-start(bf16[1,40,640]{2,1,0:T(8,128)(2,1)S(1)} %dynamic-slice_bitcast_fusion.16), channel_id=1, source_target_pairs={{0,4},{1,5},{2,6},{3,7},{4,0},{5,1},{6,2},{7,3},{8,12},{9,13},{10,... | collective-permute-start | bytes 153608 | tf_op jit(solution)/shard_map/ppermute | solution.py:26
  167.2 7.5 %collective-permute-done.17 = bf16[1,2,2,2,40,960]{5,4,1,2,3,0:T(8,128)(2,1)S(1)} collective-permute-done((bf16[1,2,2,2,40,960]{5,4,1,2,3,0:T(8,128)(2,1)S(1)}, bf16[1,2,2,2,40,960]{5,4,1,2,3,0:T(8,128)(2,1)S(1)}, u32[]{:S(2)}, u32[]{:S(2)}) %collective-permute-start.17) | collective-permute-done | bytes 614432 | tf_op jit(solution)/shard_map/ppermute | solution.py:26
  175.3 3.6 %collective-permute-done.22 = bf16[1,2,2,2,40,960]{5,4,3,2,1,0:T(8,128)(2,1)S(1)} collective-permute-done((bf16[1,2,2,2,40,960]{5,4,3,2,1,0:T(8,128)(2,1)S(1)}, bf16[1,2,2,2,40,960]{5,4,3,2,1,0:T(8,128)(2,1)S(1)}, u32[]{:S(2)}, u32[]{:S(2)}) %collective-permute-start.22) | collective-permute-done | bytes 614432 | tf_op jit(solution)/shard_map/ppermute | solution.py:26
  180.0 7.1 %collective-permute-start.35 = (bf16[80,640]{1,0:T(8,128)(2,1)S(1)}, bf16[80,640]{1,0:T(8,128)(2,1)S(1)}, u32[]{:S(2)}, u32[]{:S(2)}) collective-permute-start(bf16[80,640]{1,0:T(8,128)(2,1)S(1)} %maximum_bitcast_fusion.4), channel_id=1, source_target_pairs={{0,8},{8,0},{16,24},{24,16},{1,9},{9,1},{17,25},{25,17},{2,10},{10... | collective-permute-start | bytes 307208 | tf_op jit(solution)/shard_map/ppermute | solution.py:26
  188.8 7.6 %collective-permute-done.23 = bf16[1,2,2,40,960]{4,3,2,1,0:T(8,128)(2,1)S(1)} collective-permute-done((bf16[1,2,2,40,960]{4,3,2,1,0:T(8,128)(2,1)S(1)}, bf16[1,2,2,40,960]{4,3,2,1,0:T(8,128)(2,1)S(1)}, u32[]{:S(2)}, u32[]{:S(2)}) %collective-permute-start.23) | collective-permute-done | bytes 307232 | tf_op jit(solution)/shard_map/ppermute | solution.py:26
  197.2 1.8 fusion.34
  202.1 2.4 collective-permute-start.25
  204.5 1.7 collective-permute-done.20
  209.9 5.3 %collective-permute-done.21 = bf16[1,40,960]{2,1,0:T(8,128)(2,1)S(1)} collective-permute-done((bf16[1,40,960]{2,1,0:T(8,128)(2,1)S(1)}, bf16[1,40,960]{2,1,0:T(8,128)(2,1)S(1)}, u32[]{:S(2)}, u32[]{:S(2)}) %collective-permute-start.21) | collective-permute-done | bytes 76832 | tf_op jit(solution)/shard_map/ppermute | solution.py:26
  217.0 2.1 collective-permute-start.27
  221.0 7.1 %collective-permute-done.6 = bf16[3,2,40,640]{3,2,0,1:T(8,128)(2,1)S(1)} collective-permute-done((bf16[3,2,40,640]{3,2,0,1:T(8,128)(2,1)S(1)}, bf16[3,2,40,640]{3,2,0,1:T(8,128)(2,1)S(1)}, u32[]{:S(2)}, u32[]{:S(2)}) %collective-permute-start.6) | collective-permute-done | bytes 307232 | tf_op jit(solution)/shard_map/ppermute | solution.py:26
  228.6 7.8 %collective-permute-done.11 = bf16[3,2,40,640]{3,2,1,0:T(8,128)(2,1)S(1)} collective-permute-done((bf16[3,2,40,640]{3,2,1,0:T(8,128)(2,1)S(1)}, bf16[3,2,40,640]{3,2,1,0:T(8,128)(2,1)S(1)}, u32[]{:S(2)}, u32[]{:S(2)}) %collective-permute-start.11) | collective-permute-done | bytes 307232 | tf_op jit(solution)/shard_map/ppermute | solution.py:26
  236.5 1.9 collective-permute-start.12
  238.8 6.6 %collective-permute-done.12 = bf16[3,40,640]{2,1,0:T(8,128)(2,1)S(1)} collective-permute-done((bf16[3,40,640]{2,1,0:T(8,128)(2,1)S(1)}, bf16[3,40,640]{2,1,0:T(8,128)(2,1)S(1)}, u32[]{:S(2)}, u32[]{:S(2)}) %collective-permute-start.12) | collective-permute-done | bytes 153632 | tf_op jit(solution)/shard_map/ppermute | solution.py:26
  245.7 4.8 %collective-permute-done.13 = bf16[3,40,640]{2,1,0:T(8,128)(2,1)S(1)} collective-permute-done((bf16[3,40,640]{2,1,0:T(8,128)(2,1)S(1)}, bf16[3,40,640]{2,1,0:T(8,128)(2,1)S(1)}, u32[]{:S(2)}, u32[]{:S(2)}) %collective-permute-start.13) | collective-permute-done | bytes 153632 | tf_op jit(solution)/shard_map/ppermute | solution.py:26
  (182 shorter events, 58.1 us)
Async XLA Ops:
  1.7 9.9 %collective-permute-start = (bf16[8,8,1280]{2,1,0:T(8,128)(2,1)S(1)}, bf16[8,8,1280]{2,1,0:T(8,128)(2,1)S(1)}, u32[]{:S(2)}, u32[]{:S(2)}) collective-permute-start(bf16[8,8,1280]{2,1,0:T(8,128)(2,1)S(1)} %slice_bitcast_fusion.1), channel_id=1, source_target_pairs={{0,1},{1,2},{2,3},{3,4},{4,5},{5,6},{6,7},{8,9},{9,10},{10,11},{11... | collective-permute-start | bytes 491528 | tf_op jit(solution)/shard_map/ppermute | solution.py:21
  57.2 32.9 %all-to-all-start.1 = ((bf16[8,32,2560]{2,1,0:T(8,128)(2,1)}), bf16[8,32,2560]{2,1,0:T(8,128)(2,1)S(1)}, u32[]{:S(2)}, u32[]{:S(2)}) async-start(bf16[8,32,2560]{2,1,0:T(8,128)(2,1)} %bitcast.15), calls=%async_computation.1 | async-start | bytes 2621440 | tf_op jit(solution)/shard_map/all_to_all | solution.py:196
  64.5 50.7 %collective-permute-start.29 = (bf16[256,640]{1,0:T(8,128)(2,1)}, bf16[256,640]{1,0:T(8,128)(2,1)}, u32[]{:S(2)}, u32[]{:S(2)}) collective-permute-start(bf16[256,640]{1,0:T(8,128)(2,1)} %constant_dynamic-slice_fusion.2), channel_id=1, source_target_pairs={{0,8},{8,0},{16,24},{24,16},{1,9},{9,1},{17,25},{25,17},{2,10},{10... | collective-permute-start | bytes 983048 | tf_op jit(solution)/shard_map/ppermute | solution.py:26
  66.1 62.7 %collective-permute-start.15 = (bf16[256,1280]{1,0:T(8,128)(2,1)}, bf16[256,1280]{1,0:T(8,128)(2,1)}, u32[]{:S(2)}, u32[]{:S(2)}) collective-permute-start(bf16[256,1280]{1,0:T(8,128)(2,1)} %copy-done.11), channel_id=1, source_target_pairs={{0,8},{8,0},{16,24},{24,16},{1,9},{9,1},{17,25},{25,17},{2,10},{10... | collective-permute-start | bytes 1966088 | tf_op jit(solution)/shard_map/ppermute | solution.py:26
  68.9 49.9 %collective-permute-start.2 = (bf16[256,3840]{1,0:T(8,128)(2,1)}, bf16[256,3840]{1,0:T(8,128)(2,1)}, u32[]{:S(2)}, u32[]{:S(2)}) collective-permute-start(bf16[256,3840]{1,0:T(8,128)(2,1)} %pad_maximum_fusion), channel_id=1, source_target_pairs={{0,8},{8,0},{16,24},{24,16},{1,9},{9,1},{17,25},{25,17},{2,10},{10... | collective-permute-start | bytes 5898248 | tf_op jit(solution)/shard_map/ppermute | solution.py:26
  101.3 8.8 %collective-permute-start.1 = (bf16[8,8,1280]{2,1,0:T(8,128)(2,1)S(1)}, bf16[8,8,1280]{2,1,0:T(8,128)(2,1)S(1)}, u32[]{:S(2)}, u32[]{:S(2)}) collective-permute-start(bf16[8,8,1280]{2,1,0:T(8,128)(2,1)S(1)} %slice_bitcast_fusion), channel_id=1, source_target_pairs={{1,0},{2,1},{3,2},{4,3},{5,4},{6,5},{7,6},{9,8},{10,9},{11,10},{12... | collective-permute-start | bytes 491528 | tf_op jit(solution)/shard_map/ppermute | solution.py:21
  109.0 6.2 %collective-permute-start.28 = (bf16[256,640]{1,0:T(8,128)(2,1)S(1)}, bf16[256,640]{1,0:T(8,128)(2,1)S(1)}, u32[]{:S(2)}, u32[]{:S(2)}) collective-permute-start(bf16[256,640]{1,0:T(8,128)(2,1)S(1)} %slice.71), channel_id=1, source_target_pairs={{0,8},{8,0},{16,24},{24,16},{1,9},{9,1},{17,25},{25,17},{2,10},{10... | collective-permute-start | bytes 983048 | tf_op jit(solution)/shard_map/ppermute | solution.py:26
  110.1 18.7 %collective-permute-start.16 = (bf16[256,960]{1,0:T(8,128)(2,1)S(1)}, bf16[256,960]{1,0:T(8,128)(2,1)S(1)}, u32[]{:S(2)}, u32[]{:S(2)}) collective-permute-start(bf16[256,960]{1,0:T(8,128)(2,1)S(1)} %constant_dynamic-slice_fusion.5), channel_id=1, source_target_pairs={{0,8},{8,0},{16,24},{24,16},{1,9},{9,1},{17,25},{25,17},{2,10},{10... | collective-permute-start | bytes 1474568 | tf_op jit(solution)/shard_map/ppermute | solution.py:26
  117.5 17.7 %collective-permute-start.30 = (bf16[1,2,2,2,40,640]{5,4,1,2,3,0:T(8,128)(2,1)}, bf16[1,2,2,2,40,640]{5,4,1,2,3,0:T(8,128)(2,1)S(1)}, u32[]{:S(2)}, u32[]{:S(2)}) collective-permute-start(bf16[1,2,2,2,40,640]{5,4,1,2,3,0:T(8,128)(2,1)} %bitcast.181), channel_id=1, source_target_pairs={{0,16},{8,24},{16,0},{24,8},{1,17},{9,25},{17,1},{25,9},{2,18},{10... | collective-permute-start | bytes 1228808 | tf_op jit(solution)/shard_map/ppermute | solution.py:26
  125.4 71.8 %collective-permute-start.4 = (bf16[3,2,2,2,40,640]{5,4,0,1,2,3:T(8,128)(2,1)}, bf16[3,2,2,2,40,640]{5,4,0,1,2,3:T(8,128)(2,1)}, u32[]{:S(2)}, u32[]{:S(2)}) collective-permute-start(bf16[3,2,2,2,40,640]{5,4,0,1,2,3:T(8,128)(2,1)} %bitcast.179), channel_id=1, source_target_pairs={{0,1},{1,0},{2,3},{3,2},{4,5},{5,4},{6,7},{7,6},{8,9},{9,8},{10,11... | collective-permute-start | bytes 3686408 | tf_op jit(solution)/shard_map/ppermute | solution.py:26
  128.6 70.8 %collective-permute-start.9 = (bf16[3,2,2,2,40,640]{5,4,3,2,1,0:T(8,128)(2,1)}, bf16[3,2,2,2,40,640]{5,4,3,2,1,0:T(8,128)(2,1)}, u32[]{:S(2)}, u32[]{:S(2)}) collective-permute-start(bf16[3,2,2,2,40,640]{5,4,3,2,1,0:T(8,128)(2,1)} %dynamic-slice_bitcast_fusion), channel_id=1, source_target_pairs={{0,16},{8,24},{16,0},{24,8},{1,17},{9,25},{17,1},{25,9},{2,18},{10... | collective-permute-start | bytes 3686408 | tf_op jit(solution)/shard_map/ppermute | solution.py:26
  135.4 23.2 %collective-permute-start.31 = (bf16[1,2,2,40,640]{4,3,1,2,0:T(8,128)(2,1)S(1)}, bf16[1,2,2,40,640]{4,3,1,2,0:T(8,128)(2,1)S(1)}, u32[]{:S(2)}, u32[]{:S(2)}) collective-permute-start(bf16[1,2,2,40,640]{4,3,1,2,0:T(8,128)(2,1)S(1)} %dynamic-slice_bitcast_fusion.8), channel_id=1, source_target_pairs={{0,1},{1,0},{2,3},{3,2},{4,5},{5,4},{6,7},{7,6},{8,9},{9,8},{10,11... | collective-permute-start | bytes 614408 | tf_op jit(solution)/shard_map/ppermute | solution.py:26
  160.4 14.3 %collective-permute-start.17 = (bf16[1,2,2,2,40,960]{5,4,1,2,3,0:T(8,128)(2,1)S(1)}, bf16[1,2,2,2,40,960]{5,4,1,2,3,0:T(8,128)(2,1)S(1)}, u32[]{:S(2)}, u32[]{:S(2)}) collective-permute-start(bf16[1,2,2,2,40,960]{5,4,1,2,3,0:T(8,128)(2,1)S(1)} %bitcast.211), channel_id=1, source_target_pairs={{0,1},{1,0},{2,3},{3,2},{4,5},{5,4},{6,7},{7,6},{8,9},{9,8},{10,11... | collective-permute-start | bytes 1843208 | tf_op jit(solution)/shard_map/ppermute | solution.py:26
  165.3 13.5 %collective-permute-start.22 = (bf16[1,2,2,2,40,960]{5,4,3,2,1,0:T(8,128)(2,1)S(1)}, bf16[1,2,2,2,40,960]{5,4,3,2,1,0:T(8,128)(2,1)S(1)}, u32[]{:S(2)}, u32[]{:S(2)}) collective-permute-start(bf16[1,2,2,2,40,960]{5,4,3,2,1,0:T(8,128)(2,1)S(1)} %dynamic-slice_bitcast_fusion.1), channel_id=1, source_target_pairs={{0,16},{8,24},{16,0},{24,8},{1,17},{9,25},{17,1},{25,9},{2,18},{10... | collective-permute-start | bytes 1843208 | tf_op jit(solution)/shard_map/ppermute | solution.py:26
  166.9 13.0 %collective-permute-start.34 = (bf16[1,40,640]{2,1,0:T(8,128)(2,1)S(1)}, bf16[1,40,640]{2,1,0:T(8,128)(2,1)S(1)}, u32[]{:S(2)}, u32[]{:S(2)}) collective-permute-start(bf16[1,40,640]{2,1,0:T(8,128)(2,1)S(1)} %multiply_convert_fusion.4), channel_id=1, source_target_pairs={{0,16},{8,24},{16,0},{24,8},{1,17},{9,25},{17,1},{25,9},{2,18},{10... | collective-permute-start | bytes 153608 | tf_op jit(solution)/shard_map/ppermute | solution.py:26
  175.0 13.6 %collective-permute-start.18 = (bf16[1,2,2,40,960]{4,3,1,2,0:T(8,128)(2,1)S(1)}, bf16[1,2,2,40,960]{4,3,1,2,0:T(8,128)(2,1)S(1)}, u32[]{:S(2)}, u32[]{:S(2)}) collective-permute-start(bf16[1,2,2,40,960]{4,3,1,2,0:T(8,128)(2,1)S(1)} %dynamic-slice_bitcast_fusion.5), channel_id=1, source_target_pairs={{0,16},{8,24},{16,0},{24,8},{1,17},{9,25},{17,1},{25,9},{2,18},{10... | collective-permute-start | bytes 921608 | tf_op jit(solution)/shard_map/ppermute | solution.py:26
  180.0 8.5 %collective-permute-start.35 = (bf16[80,640]{1,0:T(8,128)(2,1)S(1)}, bf16[80,640]{1,0:T(8,128)(2,1)S(1)}, u32[]{:S(2)}, u32[]{:S(2)}) collective-permute-start(bf16[80,640]{1,0:T(8,128)(2,1)S(1)} %maximum_bitcast_fusion.4), channel_id=1, source_target_pairs={{0,8},{8,0},{16,24},{24,16},{1,9},{9,1},{17,25},{25,17},{2,10},{10... | collective-permute-start | bytes 307208 | tf_op jit(solution)/shard_map/ppermute | solution.py:26
  187.1 9.4 %collective-permute-start.23 = (bf16[1,2,2,40,960]{4,3,2,1,0:T(8,128)(2,1)S(1)}, bf16[1,2,2,40,960]{4,3,2,1,0:T(8,128)(2,1)S(1)}, u32[]{:S(2)}, u32[]{:S(2)}) collective-permute-start(bf16[1,2,2,40,960]{4,3,2,1,0:T(8,128)(2,1)S(1)} %dynamic-slice_bitcast_fusion.4), channel_id=1, source_target_pairs={{0,1},{1,0},{2,3},{3,2},{4,5},{5,4},{6,7},{7,6},{8,9},{9,8},{10,11... | collective-permute-start | bytes 921608 | tf_op jit(solution)/shard_map/ppermute | solution.py:26
  188.7 13.2 %collective-permute-start.19 = (bf16[1,2,40,960]{3,2,1,0:T(8,128)(2,1)S(1)}, bf16[1,2,40,960]{3,2,1,0:T(8,128)(2,1)S(1)}, u32[]{:S(2)}, u32[]{:S(2)}) collective-permute-start(bf16[1,2,40,960]{3,2,1,0:T(8,128)(2,1)S(1)} %dynamic-slice_bitcast_fusion.10), channel_id=1, source_target_pairs={{0,2},{1,3},{2,0},{3,1},{4,6},{5,7},{6,4},{7,5},{8,10},{9,11},{10,... | collective-permute-start | bytes 460808 | tf_op jit(solution)/shard_map/ppermute | solution.py:26
  196.6 5.5 %collective-permute-start.24 = (bf16[1,2,40,960]{3,2,1,0:T(8,128)(2,1)S(1)}, bf16[1,2,40,960]{3,2,1,0:T(8,128)(2,1)S(1)}, u32[]{:S(2)}, u32[]{:S(2)}) collective-permute-start(bf16[1,2,40,960]{3,2,1,0:T(8,128)(2,1)S(1)} %dynamic-slice_bitcast_fusion.9), channel_id=1, source_target_pairs={{0,2},{1,3},{2,0},{3,1},{4,6},{5,7},{6,4},{7,5},{8,10},{9,11},{10,... | collective-permute-start | bytes 460808 | tf_op jit(solution)/shard_map/ppermute | solution.py:26
  199.1 20.0 %collective-permute-start.5 = (bf16[3,2,2,40,640]{4,3,0,1,2:T(8,128)(2,1)S(1)}, bf16[3,2,2,40,640]{4,3,0,1,2:T(8,128)(2,1)S(1)}, u32[]{:S(2)}, u32[]{:S(2)}) collective-permute-start(bf16[3,2,2,40,640]{4,3,0,1,2:T(8,128)(2,1)S(1)} %dynamic-slice_bitcast_fusion.3), channel_id=1, source_target_pairs={{0,16},{8,24},{16,0},{24,8},{1,17},{9,25},{17,1},{25,9},{2,18},{10... | collective-permute-start | bytes 1843208 | tf_op jit(solution)/shard_map/ppermute | solution.py:26
  201.0 19.2 %collective-permute-start.10 = (bf16[3,2,2,40,640]{4,3,2,1,0:T(8,128)(2,1)S(1)}, bf16[3,2,2,40,640]{4,3,2,1,0:T(8,128)(2,1)S(1)}, u32[]{:S(2)}, u32[]{:S(2)}) collective-permute-start(bf16[3,2,2,40,640]{4,3,2,1,0:T(8,128)(2,1)S(1)} %dynamic-slice_bitcast_fusion.2), channel_id=1, source_target_pairs={{0,1},{1,0},{2,3},{3,2},{4,5},{5,4},{6,7},{7,6},{8,9},{9,8},{10,11... | collective-permute-start | bytes 1843208 | tf_op jit(solution)/shard_map/ppermute | solution.py:26
  202.1 6.4 %collective-permute-start.25 = (bf16[1,40,960]{2,1,0:T(8,128)(2,1)S(1)}, bf16[1,40,960]{2,1,0:T(8,128)(2,1)S(1)}, u32[]{:S(2)}, u32[]{:S(2)}) collective-permute-start(bf16[1,40,960]{2,1,0:T(8,128)(2,1)S(1)} %dynamic-slice_bitcast_fusion.14), channel_id=1, source_target_pairs={{0,4},{1,5},{2,6},{3,7},{4,0},{5,1},{6,2},{7,3},{8,12},{9,13},{10,... | collective-permute-start | bytes 230408 | tf_op jit(solution)/shard_map/ppermute | solution.py:26
  206.3 8.8 %collective-permute-start.21 = (bf16[1,40,960]{2,1,0:T(8,128)(2,1)S(1)}, bf16[1,40,960]{2,1,0:T(8,128)(2,1)S(1)}, u32[]{:S(2)}, u32[]{:S(2)}) collective-permute-start(bf16[1,40,960]{2,1,0:T(8,128)(2,1)S(1)} %multiply_convert_fusion.3), channel_id=1, source_target_pairs={{0,16},{8,24},{16,0},{24,8},{1,17},{9,25},{17,1},{25,9},{2,18},{10... | collective-permute-start | bytes 230408 | tf_op jit(solution)/shard_map/ppermute | solution.py:26
  208.5 8.4 %collective-permute-start.26 = (bf16[1,40,960]{2,1,0:T(8,128)(2,1)S(1)}, bf16[1,40,960]{2,1,0:T(8,128)(2,1)S(1)}, u32[]{:S(2)}, u32[]{:S(2)}) collective-permute-start(bf16[1,40,960]{2,1,0:T(8,128)(2,1)S(1)} %multiply_convert_fusion.2), channel_id=1, source_target_pairs={{0,16},{8,24},{16,0},{24,8},{1,17},{9,25},{17,1},{25,9},{2,18},{10... | collective-permute-start | bytes 230408 | tf_op jit(solution)/shard_map/ppermute | solution.py:26
  217.0 35.8 %collective-permute-start.27 = (bf16[160,960]{1,0:T(8,128)(2,1)S(1)}, bf16[160,960]{1,0:T(8,128)(2,1)S(1)}, u32[]{:S(2)}, u32[]{:S(2)}) collective-permute-start(bf16[160,960]{1,0:T(8,128)(2,1)S(1)} %maximum_bitcast_fusion.3), channel_id=1, source_target_pairs={{0,8},{8,0},{16,24},{24,16},{1,9},{9,1},{17,25},{25,17},{2,10},{10... | collective-permute-start | bytes 921608 | tf_op jit(solution)/shard_map/ppermute | solution.py:26
  219.2 8.9 %collective-permute-start.6 = (bf16[3,2,40,640]{3,2,0,1:T(8,128)(2,1)S(1)}, bf16[3,2,40,640]{3,2,0,1:T(8,128)(2,1)S(1)}, u32[]{:S(2)}, u32[]{:S(2)}) collective-permute-start(bf16[3,2,40,640]{3,2,0,1:T(8,128)(2,1)S(1)} %dynamic-slice_bitcast_fusion.7), channel_id=1, source_target_pairs={{0,2},{1,3},{2,0},{3,1},{4,6},{5,7},{6,4},{7,5},{8,10},{9,11},{10,... | collective-permute-start | bytes 921608 | tf_op jit(solution)/shard_map/ppermute | solution.py:26
  220.4 16.0 %collective-permute-start.11 = (bf16[3,2,40,640]{3,2,1,0:T(8,128)(2,1)S(1)}, bf16[3,2,40,640]{3,2,1,0:T(8,128)(2,1)S(1)}, u32[]{:S(2)}, u32[]{:S(2)}) collective-permute-start(bf16[3,2,40,640]{3,2,1,0:T(8,128)(2,1)S(1)} %dynamic-slice_bitcast_fusion.6), channel_id=1, source_target_pairs={{0,2},{1,3},{2,0},{3,1},{4,6},{5,7},{6,4},{7,5},{8,10},{9,11},{10,... | collective-permute-start | bytes 921608 | tf_op jit(solution)/shard_map/ppermute | solution.py:26
  228.3 10.1 %collective-permute-start.7 = (bf16[3,40,640]{2,1,0:T(8,128)(2,1)S(1)}, bf16[3,40,640]{2,1,0:T(8,128)(2,1)S(1)}, u32[]{:S(2)}, u32[]{:S(2)}) collective-permute-start(bf16[3,40,640]{2,1,0:T(8,128)(2,1)S(1)} %dynamic-slice_bitcast_fusion.12), channel_id=1, source_target_pairs={{0,4},{1,5},{2,6},{3,7},{4,0},{5,1},{6,2},{7,3},{8,12},{9,13},{10,... | collective-permute-start | bytes 460808 | tf_op jit(solution)/shard_map/ppermute | solution.py:26
  236.5 8.9 %collective-permute-start.12 = (bf16[3,40,640]{2,1,0:T(8,128)(2,1)S(1)}, bf16[3,40,640]{2,1,0:T(8,128)(2,1)S(1)}, u32[]{:S(2)}, u32[]{:S(2)}) collective-permute-start(bf16[3,40,640]{2,1,0:T(8,128)(2,1)S(1)} %dynamic-slice_bitcast_fusion.11), channel_id=1, source_target_pairs={{0,4},{1,5},{2,6},{3,7},{4,0},{5,1},{6,2},{7,3},{8,12},{9,13},{10,... | collective-permute-start | bytes 460808 | tf_op jit(solution)/shard_map/ppermute | solution.py:26
  238.5 7.2 %collective-permute-start.8 = (bf16[3,40,640]{2,1,0:T(8,128)(2,1)S(1)}, bf16[3,40,640]{2,1,0:T(8,128)(2,1)S(1)}, u32[]{:S(2)}, u32[]{:S(2)}) collective-permute-start(bf16[3,40,640]{2,1,0:T(8,128)(2,1)S(1)} %multiply_convert_fusion.1), channel_id=1, source_target_pairs={{0,16},{8,24},{16,0},{24,8},{1,17},{9,25},{17,1},{25,9},{2,18},{10... | collective-permute-start | bytes 460808 | tf_op jit(solution)/shard_map/ppermute | solution.py:26
  245.5 5.1 %collective-permute-start.13 = (bf16[3,40,640]{2,1,0:T(8,128)(2,1)S(1)}, bf16[3,40,640]{2,1,0:T(8,128)(2,1)S(1)}, u32[]{:S(2)}, u32[]{:S(2)}) collective-permute-start(bf16[3,40,640]{2,1,0:T(8,128)(2,1)S(1)} %multiply_convert_fusion), channel_id=1, source_target_pairs={{0,16},{8,24},{16,0},{24,8},{1,17},{9,25},{17,1},{25,9},{2,18},{10... | collective-permute-start | bytes 460808 | tf_op jit(solution)/shard_map/ppermute | solution.py:26
  (22 other events, 96.3 us)

commit v2 on v1

--- a/solution.py
+++ b/solution.py
@@ -21,9 +21,9 @@
     return lax.ppermute(shard, axis, pairs)
 
 
-def swap(shard, axis, bit):
+def swap(shard, axis, mask):
     devices = lax.axis_size(axis)
-    return lax.ppermute(shard, axis, [(i, i ^ (1 << bit)) for i in range(devices)])
+    return lax.ppermute(shard, axis, [(i, i ^ mask) for i in range(devices)])
 
 
 def bit_of(axis, bit):
@@ -111,33 +111,33 @@
     )(packed)
 
 
-def halve(array, position, axis, bit):
-    mine = bit_of(axis, bit)
-    away = lax.dynamic_index_in_dim(array, 1 - mine, position, keepdims=False)
-    stay = lax.dynamic_index_in_dim(array, mine, position, keepdims=False)
-    came = swap(away, axis, bit)
-    return (stay.astype(jnp.float32) + came.astype(jnp.float32)).astype(jnp.bfloat16)
-
-
-def join(array, axis, bit, position):
-    came = swap(array, axis, bit)
-    first = bit_of(axis, bit) == 0
+def add_rounded(terms, scale=None):
+    total = functools.reduce(jnp.add, [term.astype(jnp.float32) for term in terms])
+    return (total if scale is None else total * scale).astype(jnp.bfloat16)
+
+
+def halve(share):
+    mine = bit_of("tm", 0)
+    away = lax.dynamic_index_in_dim(share, 1 - mine, 1, keepdims=False)
+    stay = lax.dynamic_index_in_dim(share, mine, 1, keepdims=False)
+    return add_rounded([stay, swap(away, "tm", 1)])
+
+
+def scatter_high(share, scale):
+    mine = lax.axis_index("tm") >> 1
+    terms = [lax.dynamic_index_in_dim(share, mine, 0, keepdims=False)]
+    for mask in range(1, share.shape[0]):
+        away = lax.dynamic_index_in_dim(share, mine ^ mask, 0, keepdims=False)
+        terms.append(swap(away, "tm", 2 * mask))
+    return add_rounded(terms, scale)
+
+
+def join(array, bit):
+    came = swap(array, "dp", 1 << bit)
+    first = bit_of("dp", bit) == 0
     return jnp.concatenate(
-        [jnp.where(first, array, came), jnp.where(first, came, array)], axis=position
-    )
-
-
-def sum_over_devices(share, bits, y_first, scale):
-    if y_first:
-        share = halve(share, bits + 1, "dp", 1)
-        share = halve(share, bits, "tm", 0)
-    else:
-        share = halve(share, bits, "tm", 0)
-        share = halve(share, bits, "dp", 1)
-    for bit in range(1, bits):
-        share = halve(share, bits - bit, "tm", bit)
-    share = (share.astype(jnp.float32) * scale).astype(jnp.bfloat16)
-    return join(share, "dp", 1, 1)
+        [jnp.where(first, array, came), jnp.where(first, came, array)], axis=1
+    )
 
 
 def local(latents, conv_weight, qkv_weight, out_weight, out_cotangent):
@@ -146,17 +146,34 @@
     attn_width = out_weight.shape[0]
     dp_count = lax.axis_size("dp")
     tm_count = lax.axis_size("tm")
-    bits = tm_count.bit_length() - 1
+    high = tm_count // 2
     loc = places // tm_count
     rows = half * places
-    core = bit_of("dp", 0)
+    dp_at = lax.axis_index("dp")
 
     def as_rows(values):
         return values.reshape(rows, values.shape[-1])
 
-    def own_half(values, which):
-        size = values.shape[-1] // 2
+    def quarter(values, mask):
+        size = values.shape[-1] // dp_count
+        other = dp_at ^ mask
+        which = (other & 1) * (dp_count // 2) + (other >> 1)
         return lax.dynamic_slice_in_dim(values, which * size, size, axis=values.ndim - 1)
+
+    def all_rows(values):
+        own_core = swap(values, "dp", 1)
+        across = swap(values, "dp", 2)
+        return [values, own_core, across, swap(across, "dp", 1)]
+
+    def own_columns(values):
+        return [quarter(values, 0)] + [
+            swap(quarter(values, mask), "dp", mask) for mask in range(1, dp_count)
+        ]
+
+    def share_of(lefts, rights):
+        return functools.reduce(
+            jnp.add, [dot_columns(left, right) for left, right in zip(lefts, rights)]
+        ).astype(jnp.bfloat16)
 
     split = latents.reshape(half, 2, tm_count, loc, width)
     rim_input = from_behind(split[half - 1, 1], "tm", 1)
@@ -174,9 +191,8 @@
     even_rows = as_rows(even_frames)
     odd_rows = as_rows(odd_frames)
     conv_left = jnp.concatenate([prev_rows, even_rows, odd_rows], axis=1)
-    conv_left_other = swap(conv_left, "dp", 0)
-    cot_half = own_half(cotangent_rows, core)
-    cot_half_other = swap(own_half(cotangent_rows, 1 - core), "dp", 0)
+    conv_lefts = all_rows(conv_left)
+    cot_columns = own_columns(cotangent_rows)
 
     grad_att = dot_rows_t(cotangent_rows, out_weight).astype(jnp.bfloat16)
     hidden = (
@@ -187,7 +203,7 @@
     inv_std = lax.rsqrt(jnp.mean(centred * centred, axis=-1, keepdims=True) + EPSILON)
     unit_rows = centred * inv_std
     normed = unit_rows.astype(jnp.bfloat16)
-    normed_other = swap(normed, "dp", 0)
+    normeds = all_rows(normed)
     qkv_rows = dot_rows(normed, qkv_weight).astype(jnp.bfloat16)
 
     outgoing = jnp.concatenate([qkv_rows, grad_att], axis=1).reshape(tm_count, half * loc, -1)
@@ -205,32 +221,10 @@
 
     grad_scale = 1.0 / math.sqrt(dp_count * tm_count * rows)
 
-    def by_bits(share, taps, parts):
-        channels = share.shape[0] // taps
-        size = channels // tm_count // math.prod(parts)
-        return share.reshape((taps,) + (2,) * bits + parts + (size, share.shape[1]))
-
-    def summed(share, taps):
-        share = by_bits(share, taps, (2, 2))
-        ahead = lax.index_in_dim(share, 0, bits + 1, keepdims=False)
-        behind = lax.index_in_dim(share, 1, bits + 1, keepdims=False)
-        return jnp.concatenate(
-            [
-                sum_over_devices(ahead, bits, False, grad_scale),
-                sum_over_devices(behind, bits, True, grad_scale),
-            ],
-            axis=1,
-        )
-
-    attended_other = swap(attended, "dp", 0)
-    proj_share = (
-        dot_columns(attended, cot_half) + dot_columns(attended_other, cot_half_other)
-    ).astype(jnp.bfloat16)
-    gq_half = own_half(grad_qkv, core)
-    gq_half_other = swap(own_half(grad_qkv, 1 - core), "dp", 0)
-    qkv_share = (dot_columns(normed, gq_half) + dot_columns(normed_other, gq_half_other)).astype(
-        jnp.bfloat16
-    )
+    proj_share = share_of(all_rows(attended), cot_columns)
+    qkv_share = share_of(normeds, own_columns(grad_qkv))
+    proj_half = halve(proj_share.reshape(high, 2, -1, proj_share.shape[-1]))
+    qkv_half = halve(qkv_share.reshape(high, 2, -1, qkv_share.shape[-1]))
 
     grad_normed = dot_rows_t(grad_qkv, qkv_weight)
     correction = (
@@ -239,15 +233,15 @@
         - unit_rows * jnp.mean(grad_normed * unit_rows, axis=-1, keepdims=True)
     )
     grad_hidden = (cotangent_rows.astype(jnp.float32) + inv_std * correction).astype(jnp.bfloat16)
-    gh_half = own_half(grad_hidden, core)
-    gh_half_other = swap(own_half(grad_hidden, 1 - core), "dp", 0)
-    conv_share = (
-        dot_columns(conv_left, gh_half) + dot_columns(conv_left_other, gh_half_other)
-    ).astype(jnp.bfloat16)
-
-    proj_sum = sum_over_devices(by_bits(proj_share, 1, (2,)), bits, True, grad_scale)
-    qkv_sum = summed(qkv_share, 1)
-    conv_sum = summed(conv_share, 3)
+    conv_share = share_of(conv_lefts, own_columns(grad_hidden))
+    conv_share = jnp.transpose(
+        conv_share.reshape(3, high, 2, -1, conv_share.shape[-1]), (1, 2, 0, 3, 4)
+    ).reshape(high, 2, -1, conv_share.shape[-1])
+    conv_half = halve(conv_share)
+    qkv_sum = join(scatter_high(qkv_half, grad_scale), 1)
+    rest_sum = join(
+        scatter_high(jnp.concatenate([conv_half, proj_half], axis=1), grad_scale), 1
+    )
 
     grad_four = grad_hidden.reshape(tm_count, half, loc, width)
     rim_after = from_behind(grad_four[:, 0], "tm", -1)
@@ -262,10 +256,13 @@
         (2, 0, 1, 3, 4),
     ).reshape(latents.shape)
 
-    proj_grad = join(proj_sum[0], "dp", 0, 1)
-    qkv_grad = join(qkv_sum[0], "dp", 0, 1)
-    conv_both = join(conv_sum[:, :, None], "dp", 0, 2)
-    conv_grad = jnp.transpose(conv_both, (1, 0, 2, 3)).reshape(conv_both.shape[1], 3 * width)
+    qkv_grad = join(qkv_sum, 0)
+    rest_grad = join(rest_sum, 0)
+    size = width // tm_count
+    conv_grad = jnp.concatenate(
+        [rest_grad[tap * size : (tap + 1) * size] for tap in range(3)], axis=1
+    )
+    proj_grad = rest_grad[3 * size :]
     return (input_grad, conv_grad, qkv_grad, proj_grad)
 
 

time: 262 us -> 318 us (1.21); the launches traced: 257 us -> 317 us
  waiting for transfers between devices: 102 us -> 133 us
  matrix products: 32.2 us -> 46.1 us
  local copies, waits for them, and re-layouts: 20.7 us -> 32.4 us
  other arithmetic: 11.4 us -> 16.2 us
    ppermute x34 -> x31, waiting for transfers between devices: 81.3 us -> 133 us  [swap(): return lax.ppermute(shard, axis, [(i, i ^ mask) for i in range(devices)])]
    all_to_all x1, waiting for transfers between devices: 20.7 us -> 0.01 us  [local(): lax.all_to_all(result.reshape(tm_count, half * loc, 4 * attn_width), 'tm'...]
    dot_general x6 -> x12, matrix products: 11.5 us -> 21.8 us  [dot_columns(): lax.dot_general(left_side, right_side, (((0,), (0,)), ((), ())), preferre...]
    convert_element_type x1 -> x3, local copies, waits for them, and re-layouts: 2.97 us -> 6.46 us  [share_of(): return functools.reduce(jnp.add, [dot_columns(left, right) for left, righ...]
    dynamic_slice x7 -> x5, local copies, waits for them, and re-layouts: 4.42 us -> 7.59 us  [the longest x2 3.85 us: halve(): away = lax.dynamic_index_in_dim(share, 1 - mine, 1, keepdims=False)]
    ppermute x34 -> x31, starting transfers between devices: 36.4 us -> 35.8 us  [swap(): return lax.ppermute(shard, axis, [(i, i ^ mask) for i in range(devices)])]
  transfers between devices with their start and end apart: 37 -> 34, of which waited for: 16 -> 12; matrix products, arithmetic and copies ran while one was open for 21% -> 26% of each run, Pallas kernels for 0% -> 0%
where the time goes in v2:
time: 318 us; the launch traced here: 317 us
  waiting for transfers between devices  133 us (42%)
  starting transfers between devices  48 us (15%)
  matrix products  46.1 us (14%)
  blocking collectives  33.5 us (11%)
  local copies, waits for them, and re-layouts  32.4 us (10%)
  other arithmetic  16.2 us (5%)
  Pallas kernels  5.86 us (2%)
    ppermute x31, waiting for transfers between devices, swap(): return lax.ppermute(shard, axis, [(i, i ^ mask) for i in range(devices)])  133 us
    ppermute x31, starting transfers between devices, swap(): return lax.ppermute(shard, axis, [(i, i ^ mask) for i in range(devices)])  35.8 us
    all_to_all x1, blocking collectives, local(): lax.all_to_all(outgoing, 'tm', split_axis=0, concat_axis=0, tiled=True)  33.5 us
    dot_general x12, matrix products, dot_columns(): lax.dot_general(left_side, right_side, (((0,), (0,)), ((), ())), preferre...  21.8 us
    dot_general x5, matrix products, dot_rows_t(): lax.dot_general(left_side, right_side, (((1,), (1,)), ((), ())), preferre...  16.2 us
    dot_general x4, matrix products, dot_rows(): return jnp.dot(left_side, right_side, preferred_element_type=jnp.float32)  8.13 us
    ppermute x2, starting transfers between devices, from_behind(): return lax.ppermute(shard, axis, pairs)  6.51 us
    convert_element_type x3, local copies, waits for them, and re-layouts, share_of(): return functools.reduce(jnp.add, [dot_columns(left, right) for left, righ...  6.46 us
  transfers between devices with their start and end apart: 34, of which 12 were waited for; matrix products, arithmetic and copies ran while one was open for 26% of the time, Pallas kernels for 0%

profile of v2, /device:TPU:17, one launch (start us, length us, event | category | flops | bytes accessed | tf_op | source)
XLA Modules:
  0.0 316.7 jit_solution(2018844742361249849)
XLA Ops:
  1.7 3.1 collective-permute-start
  6.4 3.4 %fusion.9 = f32[256,1280]{1,0:T(8,128)S(1)} fusion(bf16[256,1280]{1,0:T(8,128)(2,1)S(1)} %bitcast.116, bf16[1280,3840]{1,0:T(8,128)(2,1)} %param.6), kind=kOutput, calls=%fused_computation.20 | convolution fusion | flops 838860800 | bytes 5242880 | tf_op jit(solution)/shard_map/dot_general | solution.py:34
  15.1 2.6 convolution_convert_fusion
  17.8 33.5 %all_to_all.10 = bf16[8,32,2560]{2,1,0:T(8,128)(2,1)S(1)} all-to-all(bf16[8,32,2560]{2,1,0:T(8,128)(2,1)S(1)} %bitcast.115), channel_id=1, replica_groups=mesh['dp'=4,'tm'=8] {'tm'}, dimensions={0} | all-to-all | bytes 2621440 | tf_op jit(solution)/shard_map/all_to_all | solution.py:210
  51.3 5.9 %shard_map.84 = bf16[256,2560]{1,0:T(8,128)(2,1)} custom-call(bf16[256,2560]{1,0:T(8,128)(2,1)S(1)} %bitcast.104), custom_call_target="tpu_custom_call" | custom-call | flops 1174405120 | bytes 2621440 | tf_op jit(solution)/shard_map/pallas_call | solution.py:100
  57.1 5.7 %all-to-all-start.1 = ((bf16[8,32,2560]{2,1,0:T(8,128)(2,1)}), bf16[8,32,2560]{2,1,0:T(8,128)(2,1)}, u32[]{:S(2)}, u32[]{:S(2)}) async-start(bf16[8,32,2560]{2,1,0:T(8,128)(2,1)} %bitcast.15), calls=%async_computation.1 | async-start | bytes 2621440 | tf_op jit(solution)/shard_map/all_to_all | solution.py:212
  62.9 2.5 pad_maximum_fusion
  71.7 36.2 %collective-permute-done.4 = bf16[256,3840]{1,0:T(8,128)(2,1)S(1)} collective-permute-done((bf16[256,3840]{1,0:T(8,128)(2,1)}, bf16[256,3840]{1,0:T(8,128)(2,1)S(1)}, u32[]{:S(2)}, u32[]{:S(2)}) %collective-permute-start.4) | collective-permute-done | bytes 1966112 | tf_op jit(solution)/shard_map/ppermute | solution.py:26
  107.8 5.1 %collective-permute-start.6 = (bf16[256,3840]{1,0:T(8,128)(2,1)S(1)}, bf16[256,3840]{1,0:T(8,128)(2,1)}, u32[]{:S(2)}, u32[]{:S(2)}) collective-permute-start(bf16[256,3840]{1,0:T(8,128)(2,1)S(1)} %collective-permute-done.4), channel_id=1, source_target_pairs={{0,8},{8,0},{16,24},{24,16},{1,9},{9,1},{17,25},{25,17},{2,10},{10... | collective-permute-start | bytes 5898248 | tf_op jit(solution)/shard_map/ppermute | solution.py:26
  112.9 4.4 %fusion.71 = (f32[256]{0:T(256)S(1)}, f32[256]{0:T(256)S(1)}, f32[256,1280]{1,0:T(8,128)S(1)}) fusion(f32[256]{0:T(256)S(1)} %add_rsqrt_fusion, f32[256,1280]{1,0:T(8,128)S(1)} %get-tuple-element.36, f32[256]{0:T(256)S(1)} %broadcast_multiply_fusion.2, bf16[1280,1920]{1,0:T(8,128)(2,1)} %param.7, bf16[256,2560]{1,0:T(8,128)(2,1)} %bitcast.16), kind=kOutput, calls=%fused_computation.131 | convolution fusion | flops 1259929088 | bytes 8523776 | tf_op jit(solution)/shard_map/dot_general | solution.py:38
  119.6 3.2 %fusion.59 = f32[1280,480]{0,1:T(8,128)} fusion(bf16[256,1280]{1,0:T(8,128)(2,1)} %fusion.38, bf16[256,1920]{1,0:T(8,128)(2,1)S(1)} %slice.64, s32[]{:T(128)S(6)} %select_n.125), kind=kOutput, calls=%fused_computation.95 | convolution fusion | flops 314572800 | bytes 3375108 | tf_op jit(solution)/shard_map/dot_general | solution.py:44
  122.8 4.0 %fusion.3 = f32[256,1280]{1,0:T(8,128)} fusion(bf16[256,1280]{1,0:T(8,128)(2,1)S(1)} %add_convert_fusion, bf16[1280,3840]{1,0:T(8,128)(2,1)} %param.6), kind=kOutput, calls=%fused_computation.14 | convolution fusion | flops 838860800 | bytes 5242880 | tf_op jit(solution)/shard_map/dot_general | solution.py:38
  126.8 4.0 %fusion.24 = bf16[256,1280]{1,0:T(8,128)(2,1)} fusion(bf16[256,1280]{1,0:T(8,128)(2,1)S(1)} %add_convert_fusion, bf16[1280,3840]{1,0:T(8,128)(2,1)} %param.6), kind=kOutput, calls=%fused_computation.29 | convolution fusion | flops 839188480 | bytes 4587520 | tf_op jit(solution)/shard_map/dot_general | solution.py:38
  140.3 2.5 convolution_add_fusion.2
  142.8 2.7 collective-permute-done.5
  148.7 4.4 %collective-permute-done.7 = bf16[256,320]{1,0:T(8,128)(2,1)S(1)} collective-permute-done((bf16[256,320]{1,0:T(8,128)(2,1)S(1)}, bf16[256,320]{1,0:T(8,128)(2,1)S(1)}, u32[]{:S(2)}, u32[]{:S(2)}) %collective-permute-start.7) | collective-permute-done | bytes 163872 | tf_op jit(solution)/shard_map/ppermute | solution.py:26
  153.1 3.4 %collective-permute-start.1 = (bf16[8,8,1280]{2,1,0:T(8,128)(2,1)}, bf16[8,8,1280]{2,1,0:T(8,128)(2,1)}, u32[]{:S(2)}, u32[]{:S(2)}) collective-permute-start(bf16[8,8,1280]{2,1,0:T(8,128)(2,1)} %slice_bitcast_fusion), channel_id=1, source_target_pairs={{1,0},{2,1},{3,2},{4,3},{5,4},{6,5},{7,6},{9,8},{10,9},{11,10},{12... | collective-permute-start | bytes 491528 | tf_op jit(solution)/shard_map/ppermute | solution.py:21
  156.5 2.5 fusion
  159.0 2.8 copy.53
  165.2 2.5 copy.55
  172.1 2.4 convolution_add_fusion.5
  174.6 7.7 %collective-permute-done.24 = bf16[256,480]{1,0:T(8,128)(2,1)S(1)} collective-permute-done((bf16[256,480]{1,0:T(8,128)(2,1)}, bf16[256,480]{1,0:T(8,128)(2,1)S(1)}, u32[]{:S(2)}, u32[]{:S(2)}) %collective-permute-start.24) | collective-permute-done | bytes 245792 | tf_op jit(solution)/shard_map/ppermute | solution.py:26
  186.2 5.3 %collective-permute-done.26 = bf16[256,480]{1,0:T(8,128)(2,1)S(1)} collective-permute-done((bf16[256,480]{1,0:T(8,128)(2,1)S(1)}, bf16[256,480]{1,0:T(8,128)(2,1)S(1)}, u32[]{:S(2)}, u32[]{:S(2)}) %collective-permute-start.26) | collective-permute-done | bytes 245792 | tf_op jit(solution)/shard_map/ppermute | solution.py:26
  207.0 34.7 %collective-permute-done.27 = bf16[4,160,480]{2,1,0:T(8,128)(2,1)} collective-permute-done((bf16[4,160,480]{2,1,0:T(8,128)(2,1)}, bf16[4,160,480]{2,1,0:T(8,128)(2,1)}, u32[]{:S(2)}, u32[]{:S(2)}) %collective-permute-start.27) | collective-permute-done | bytes 614432 | tf_op jit(solution)/shard_map/ppermute | solution.py:26
  248.5 2.5 copy.56
  256.4 3.0 fusion.33
  263.5 7.2 %collective-permute-done.16 = bf16[560,320]{1,0:T(8,128)(2,1)S(1)} collective-permute-done((bf16[560,320]{1,0:T(8,128)(2,1)S(1)}, bf16[560,320]{1,0:T(8,128)(2,1)S(1)}, u32[]{:S(2)}, u32[]{:S(2)}) %collective-permute-start.16) | collective-permute-done | bytes 358432 | tf_op jit(solution)/shard_map/ppermute | solution.py:26
  270.7 16.2 %collective-permute-done.17 = bf16[560,320]{1,0:T(8,128)(2,1)S(1)} collective-permute-done((bf16[560,320]{1,0:T(8,128)(2,1)S(1)}, bf16[560,320]{1,0:T(8,128)(2,1)S(1)}, u32[]{:S(2)}, u32[]{:S(2)}) %collective-permute-start.17) | collective-permute-done | bytes 358432 | tf_op jit(solution)/shard_map/ppermute | solution.py:26
  286.8 11.3 %collective-permute-done.18 = bf16[560,320]{1,0:T(8,128)(2,1)S(1)} collective-permute-done((bf16[560,320]{1,0:T(8,128)(2,1)S(1)}, bf16[560,320]{1,0:T(8,128)(2,1)S(1)}, u32[]{:S(2)}, u32[]{:S(2)}) %collective-permute-start.18) | collective-permute-done | bytes 358432 | tf_op jit(solution)/shard_map/ppermute | solution.py:26
  299.8 2.5 collective-permute-start.32
  302.3 5.4 %collective-permute-done.19 = bf16[560,320]{1,0:T(8,128)(2,1)S(1)} collective-permute-done((bf16[560,320]{1,0:T(8,128)(2,1)S(1)}, bf16[560,320]{1,0:T(8,128)(2,1)S(1)}, u32[]{:S(2)}, u32[]{:S(2)}) %collective-permute-start.19) | collective-permute-done | bytes 358432 | tf_op jit(solution)/shard_map/ppermute | solution.py:26
  308.0 3.1 collective-permute-start.20
  (158 shorter events, 79.9 us)
Async XLA Ops:
  1.7 8.8 %collective-permute-start = (bf16[8,8,1280]{2,1,0:T(8,128)(2,1)S(1)}, bf16[8,8,1280]{2,1,0:T(8,128)(2,1)S(1)}, u32[]{:S(2)}, u32[]{:S(2)}) collective-permute-start(bf16[8,8,1280]{2,1,0:T(8,128)(2,1)S(1)} %slice_bitcast_fusion.1), channel_id=1, source_target_pairs={{0,1},{1,2},{2,3},{3,4},{4,5},{5,6},{6,7},{8,9},{9,10},{10,11},{11... | collective-permute-start | bytes 491528 | tf_op jit(solution)/shard_map/ppermute | solution.py:21
  57.1 55.8 %all-to-all-start.1 = ((bf16[8,32,2560]{2,1,0:T(8,128)(2,1)}), bf16[8,32,2560]{2,1,0:T(8,128)(2,1)}, u32[]{:S(2)}, u32[]{:S(2)}) async-start(bf16[8,32,2560]{2,1,0:T(8,128)(2,1)} %bitcast.15), calls=%async_computation.1 | async-start | bytes 2621440 | tf_op jit(solution)/shard_map/all_to_all | solution.py:212
  65.4 42.4 %collective-permute-start.4 = (bf16[256,3840]{1,0:T(8,128)(2,1)}, bf16[256,3840]{1,0:T(8,128)(2,1)S(1)}, u32[]{:S(2)}, u32[]{:S(2)}) collective-permute-start(bf16[256,3840]{1,0:T(8,128)(2,1)} %pad_maximum_fusion), channel_id=1, source_target_pairs={{0,16},{8,24},{16,0},{24,8},{1,17},{9,25},{17,1},{25,9},{2,18},{10... | collective-permute-start | bytes 5898248 | tf_op jit(solution)/shard_map/ppermute | solution.py:26
  68.8 129.3 %collective-permute-start.10 = (bf16[256,320]{1,0:T(8,128)(2,1)}, bf16[256,320]{1,0:T(8,128)(2,1)}, u32[]{:S(2)}, u32[]{:S(2)}) collective-permute-start(bf16[256,320]{1,0:T(8,128)(2,1)} %get-tuple-element.29), channel_id=1, source_target_pairs={{0,8},{8,0},{16,24},{24,16},{1,9},{9,1},{17,25},{25,17},{2,10},{10... | collective-permute-start | bytes 491528 | tf_op jit(solution)/shard_map/ppermute | solution.py:26
  71.2 131.9 %collective-permute-start.12 = (bf16[256,320]{1,0:T(8,128)(2,1)}, bf16[256,320]{1,0:T(8,128)(2,1)}, u32[]{:S(2)}, u32[]{:S(2)}) collective-permute-start(bf16[256,320]{1,0:T(8,128)(2,1)} %get-tuple-element.28), channel_id=1, source_target_pairs={{0,16},{8,24},{16,0},{24,8},{1,17},{9,25},{17,1},{25,9},{2,18},{10... | collective-permute-start | bytes 491528 | tf_op jit(solution)/shard_map/ppermute | solution.py:26
  71.4 67.2 %collective-permute-start.2 = (bf16[256,3840]{1,0:T(8,128)(2,1)}, bf16[256,3840]{1,0:T(8,128)(2,1)}, u32[]{:S(2)}, u32[]{:S(2)}) collective-permute-start(bf16[256,3840]{1,0:T(8,128)(2,1)} %pad_maximum_fusion), channel_id=1, source_target_pairs={{0,8},{8,0},{16,24},{24,16},{1,9},{9,1},{17,25},{25,17},{2,10},{10... | collective-permute-start | bytes 5898248 | tf_op jit(solution)/shard_map/ppermute | solution.py:26
  107.8 40.6 %collective-permute-start.6 = (bf16[256,3840]{1,0:T(8,128)(2,1)S(1)}, bf16[256,3840]{1,0:T(8,128)(2,1)}, u32[]{:S(2)}, u32[]{:S(2)}) collective-permute-start(bf16[256,3840]{1,0:T(8,128)(2,1)S(1)} %collective-permute-done.4), channel_id=1, source_target_pairs={{0,8},{8,0},{16,24},{24,16},{1,9},{9,1},{17,25},{25,17},{2,10},{10... | collective-permute-start | bytes 5898248 | tf_op jit(solution)/shard_map/ppermute | solution.py:26
  119.5 19.5 %collective-permute-start.3 = (bf16[256,320]{1,0:T(8,128)(2,1)S(1)}, bf16[256,320]{1,0:T(8,128)(2,1)S(1)}, u32[]{:S(2)}, u32[]{:S(2)}) collective-permute-start(bf16[256,320]{1,0:T(8,128)(2,1)S(1)} %get-tuple-element.32), channel_id=1, source_target_pairs={{0,8},{8,0},{16,24},{24,16},{1,9},{9,1},{17,25},{25,17},{2,10},{10... | collective-permute-start | bytes 491528 | tf_op jit(solution)/shard_map/ppermute | solution.py:26
  138.6 31.7 %collective-permute-start.21 = (bf16[256,1280]{1,0:T(8,128)(2,1)}, bf16[256,1280]{1,0:T(8,128)(2,1)}, u32[]{:S(2)}, u32[]{:S(2)}) collective-permute-start(bf16[256,1280]{1,0:T(8,128)(2,1)} %fusion.38), channel_id=1, source_target_pairs={{0,8},{8,0},{16,24},{24,16},{1,9},{9,1},{17,25},{25,17},{2,10},{10... | collective-permute-start | bytes 1966088 | tf_op jit(solution)/shard_map/ppermute | solution.py:26
  139.0 6.5 %collective-permute-start.5 = (bf16[256,320]{1,0:T(8,128)(2,1)S(1)}, bf16[256,320]{1,0:T(8,128)(2,1)S(1)}, u32[]{:S(2)}, u32[]{:S(2)}) collective-permute-start(bf16[256,320]{1,0:T(8,128)(2,1)S(1)} %get-tuple-element.31), channel_id=1, source_target_pairs={{0,16},{8,24},{16,0},{24,8},{1,17},{9,25},{17,1},{25,9},{2,18},{10... | collective-permute-start | bytes 491528 | tf_op jit(solution)/shard_map/ppermute | solution.py:26
  145.5 7.6 %collective-permute-start.7 = (bf16[256,320]{1,0:T(8,128)(2,1)S(1)}, bf16[256,320]{1,0:T(8,128)(2,1)S(1)}, u32[]{:S(2)}, u32[]{:S(2)}) collective-permute-start(bf16[256,320]{1,0:T(8,128)(2,1)S(1)} %get-tuple-element.30), channel_id=1, source_target_pairs={{0,24},{8,16},{16,8},{24,0},{1,25},{9,17},{17,9},{25,1},{2,26},{10... | collective-permute-start | bytes 491528 | tf_op jit(solution)/shard_map/ppermute | solution.py:26
  148.4 23.0 %collective-permute-start.23 = (bf16[256,1280]{1,0:T(8,128)(2,1)}, bf16[256,1280]{1,0:T(8,128)(2,1)}, u32[]{:S(2)}, u32[]{:S(2)}) collective-permute-start(bf16[256,1280]{1,0:T(8,128)(2,1)} %fusion.38), channel_id=1, source_target_pairs={{0,16},{8,24},{16,0},{24,8},{1,17},{9,25},{17,1},{25,9},{2,18},{10... | collective-permute-start | bytes 1966088 | tf_op jit(solution)/shard_map/ppermute | solution.py:26
  153.1 14.7 %collective-permute-start.1 = (bf16[8,8,1280]{2,1,0:T(8,128)(2,1)}, bf16[8,8,1280]{2,1,0:T(8,128)(2,1)}, u32[]{:S(2)}, u32[]{:S(2)}) collective-permute-start(bf16[8,8,1280]{2,1,0:T(8,128)(2,1)} %slice_bitcast_fusion), channel_id=1, source_target_pairs={{1,0},{2,1},{3,2},{4,3},{5,4},{6,5},{7,6},{9,8},{10,9},{11,10},{12... | collective-permute-start | bytes 491528 | tf_op jit(solution)/shard_map/ppermute | solution.py:21
  170.3 34.2 %collective-permute-start.14 = (bf16[256,320]{1,0:T(8,128)(2,1)}, bf16[256,320]{1,0:T(8,128)(2,1)S(1)}, u32[]{:S(2)}, u32[]{:S(2)}) collective-permute-start(bf16[256,320]{1,0:T(8,128)(2,1)} %get-tuple-element.27), channel_id=1, source_target_pairs={{0,24},{8,16},{16,8},{24,0},{1,25},{9,17},{17,9},{25,1},{2,26},{10... | collective-permute-start | bytes 491528 | tf_op jit(solution)/shard_map/ppermute | solution.py:26
  171.4 14.7 %collective-permute-start.25 = (bf16[256,1280]{1,0:T(8,128)(2,1)}, bf16[256,1280]{1,0:T(8,128)(2,1)S(1)}, u32[]{:S(2)}, u32[]{:S(2)}) collective-permute-start(bf16[256,1280]{1,0:T(8,128)(2,1)} %collective-permute-done.23), channel_id=1, source_target_pairs={{0,8},{8,0},{16,24},{24,16},{1,9},{9,1},{17,25},{25,17},{2,10},{10... | collective-permute-start | bytes 1966088 | tf_op jit(solution)/shard_map/ppermute | solution.py:26
  171.9 10.4 %collective-permute-start.24 = (bf16[256,480]{1,0:T(8,128)(2,1)}, bf16[256,480]{1,0:T(8,128)(2,1)S(1)}, u32[]{:S(2)}, u32[]{:S(2)}) collective-permute-start(bf16[256,480]{1,0:T(8,128)(2,1)} %get-tuple-element.18), channel_id=1, source_target_pairs={{0,16},{8,24},{16,0},{24,8},{1,17},{9,25},{17,1},{25,9},{2,18},{10... | collective-permute-start | bytes 737288 | tf_op jit(solution)/shard_map/ppermute | solution.py:26
  182.3 9.2 %collective-permute-start.26 = (bf16[256,480]{1,0:T(8,128)(2,1)S(1)}, bf16[256,480]{1,0:T(8,128)(2,1)S(1)}, u32[]{:S(2)}, u32[]{:S(2)}) collective-permute-start(bf16[256,480]{1,0:T(8,128)(2,1)S(1)} %copy-done.18), channel_id=1, source_target_pairs={{0,24},{8,16},{16,8},{24,0},{1,25},{9,17},{17,9},{25,1},{2,26},{10... | collective-permute-start | bytes 737288 | tf_op jit(solution)/shard_map/ppermute | solution.py:26
  186.1 12.3 %collective-permute-start.9 = (bf16[256,640]{1,0:T(8,128)(2,1)S(1)}, bf16[256,640]{1,0:T(8,128)(2,1)}, u32[]{:S(2)}, u32[]{:S(2)}) collective-permute-start(bf16[256,640]{1,0:T(8,128)(2,1)S(1)} %copy-done.17), channel_id=1, source_target_pairs={{0,8},{8,0},{16,24},{24,16},{1,9},{9,1},{17,25},{25,17},{2,10},{10... | collective-permute-start | bytes 983048 | tf_op jit(solution)/shard_map/ppermute | solution.py:26
  191.4 9.0 %collective-permute-start.11 = (bf16[256,640]{1,0:T(8,128)(2,1)S(1)}, bf16[256,640]{1,0:T(8,128)(2,1)}, u32[]{:S(2)}, u32[]{:S(2)}) collective-permute-start(bf16[256,640]{1,0:T(8,128)(2,1)S(1)} %copy-done.17), channel_id=1, source_target_pairs={{0,16},{8,24},{16,0},{24,8},{1,17},{9,25},{17,1},{25,9},{2,18},{10... | collective-permute-start | bytes 983048 | tf_op jit(solution)/shard_map/ppermute | solution.py:26
  198.1 50.4 %collective-permute-start.8 = (bf16[4,480,320]{1,2,0:T(8,128)(2,1)}, bf16[4,480,320]{1,2,0:T(8,128)(2,1)}, u32[]{:S(2)}, u32[]{:S(2)}) collective-permute-start(bf16[4,480,320]{1,2,0:T(8,128)(2,1)} %bitcast.129), channel_id=1, source_target_pairs={{0,1},{1,0},{2,3},{3,2},{4,5},{5,4},{6,7},{7,6},{8,9},{9,8},{10,11... | collective-permute-start | bytes 3686408 | tf_op jit(solution)/shard_map/ppermute | solution.py:26
  198.4 43.3 %collective-permute-start.27 = (bf16[4,160,480]{2,1,0:T(8,128)(2,1)}, bf16[4,160,480]{2,1,0:T(8,128)(2,1)}, u32[]{:S(2)}, u32[]{:S(2)}) collective-permute-start(bf16[4,160,480]{2,1,0:T(8,128)(2,1)} %dynamic-slice_bitcast_fusion), channel_id=1, source_target_pairs={{0,1},{1,0},{2,3},{3,2},{4,5},{5,4},{6,7},{7,6},{8,9},{9,8},{10,11... | collective-permute-start | bytes 1843208 | tf_op jit(solution)/shard_map/ppermute | solution.py:26
  206.9 40.6 %collective-permute-start.15 = (bf16[4,80,320]{2,1,0:T(8,128)(2,1)S(1)}, bf16[4,80,320]{2,1,0:T(8,128)(2,1)S(1)}, u32[]{:S(2)}, u32[]{:S(2)}) collective-permute-start(bf16[4,80,320]{2,1,0:T(8,128)(2,1)S(1)} %dynamic-slice_bitcast_fusion.1), channel_id=1, source_target_pairs={{0,1},{1,0},{2,3},{3,2},{4,5},{5,4},{6,7},{7,6},{8,9},{9,8},{10,11... | collective-permute-start | bytes 614408 | tf_op jit(solution)/shard_map/ppermute | solution.py:26
  244.8 10.3 %collective-permute-start.28 = (bf16[160,480]{1,0:T(8,128)(2,1)}, bf16[160,480]{1,0:T(8,128)(2,1)S(1)}, u32[]{:S(2)}, u32[]{:S(2)}) collective-permute-start(bf16[160,480]{1,0:T(8,128)(2,1)} %get-tuple-element.24), channel_id=1, source_target_pairs={{0,2},{1,3},{2,0},{3,1},{4,6},{5,7},{6,4},{7,5},{8,10},{9,11},{10,... | collective-permute-start | bytes 460808 | tf_op jit(solution)/shard_map/ppermute | solution.py:26
  246.0 13.4 %collective-permute-start.29 = (bf16[160,480]{1,0:T(8,128)(2,1)}, bf16[160,480]{1,0:T(8,128)(2,1)S(1)}, u32[]{:S(2)}, u32[]{:S(2)}) collective-permute-start(bf16[160,480]{1,0:T(8,128)(2,1)} %get-tuple-element.26), channel_id=1, source_target_pairs={{0,4},{1,5},{2,6},{3,7},{4,0},{5,1},{6,2},{7,3},{8,12},{9,13},{10,... | collective-permute-start | bytes 460808 | tf_op jit(solution)/shard_map/ppermute | solution.py:26
  246.3 14.8 %collective-permute-start.30 = (bf16[160,480]{1,0:T(8,128)(2,1)}, bf16[160,480]{1,0:T(8,128)(2,1)}, u32[]{:S(2)}, u32[]{:S(2)}) collective-permute-start(bf16[160,480]{1,0:T(8,128)(2,1)} %get-tuple-element.25), channel_id=1, source_target_pairs={{0,6},{1,7},{2,4},{3,5},{4,2},{5,3},{6,0},{7,1},{8,14},{9,15},{10,... | collective-permute-start | bytes 460808 | tf_op jit(solution)/shard_map/ppermute | solution.py:26
  252.9 17.7 %collective-permute-start.16 = (bf16[560,320]{1,0:T(8,128)(2,1)S(1)}, bf16[560,320]{1,0:T(8,128)(2,1)S(1)}, u32[]{:S(2)}, u32[]{:S(2)}) collective-permute-start(bf16[560,320]{1,0:T(8,128)(2,1)S(1)} %get-tuple-element.6), channel_id=1, source_target_pairs={{0,2},{1,3},{2,0},{3,1},{4,6},{5,7},{6,4},{7,5},{8,10},{9,11},{10,... | collective-permute-start | bytes 1075208 | tf_op jit(solution)/shard_map/ppermute | solution.py:26
  255.1 31.7 %collective-permute-start.17 = (bf16[560,320]{1,0:T(8,128)(2,1)S(1)}, bf16[560,320]{1,0:T(8,128)(2,1)S(1)}, u32[]{:S(2)}, u32[]{:S(2)}) collective-permute-start(bf16[560,320]{1,0:T(8,128)(2,1)S(1)} %get-tuple-element.7), channel_id=1, source_target_pairs={{0,4},{1,5},{2,6},{3,7},{4,0},{5,1},{6,2},{7,3},{8,12},{9,13},{10,... | collective-permute-start | bytes 1075208 | tf_op jit(solution)/shard_map/ppermute | solution.py:26
  255.1 43.0 %collective-permute-start.18 = (bf16[560,320]{1,0:T(8,128)(2,1)S(1)}, bf16[560,320]{1,0:T(8,128)(2,1)S(1)}, u32[]{:S(2)}, u32[]{:S(2)}) collective-permute-start(bf16[560,320]{1,0:T(8,128)(2,1)S(1)} %get-tuple-element.8), channel_id=1, source_target_pairs={{0,6},{1,7},{2,4},{3,5},{4,2},{5,3},{6,0},{7,1},{8,14},{9,15},{10,... | collective-permute-start | bytes 1075208 | tf_op jit(solution)/shard_map/ppermute | solution.py:26
  262.2 37.5 %collective-permute-start.31 = (bf16[160,480]{1,0:T(8,128)(2,1)S(1)}, bf16[160,480]{1,0:T(8,128)(2,1)S(1)}, u32[]{:S(2)}, u32[]{:S(2)}) collective-permute-start(bf16[160,480]{1,0:T(8,128)(2,1)S(1)} %fusion.58), channel_id=1, source_target_pairs={{0,16},{8,24},{16,0},{24,8},{1,17},{9,25},{17,1},{25,9},{2,18},{10... | collective-permute-start | bytes 460808 | tf_op jit(solution)/shard_map/ppermute | solution.py:26
  298.4 9.3 %collective-permute-start.19 = (bf16[560,320]{1,0:T(8,128)(2,1)S(1)}, bf16[560,320]{1,0:T(8,128)(2,1)S(1)}, u32[]{:S(2)}, u32[]{:S(2)}) collective-permute-start(bf16[560,320]{1,0:T(8,128)(2,1)S(1)} %fusion.42), channel_id=1, source_target_pairs={{0,16},{8,24},{16,0},{24,8},{1,17},{9,25},{17,1},{25,9},{2,18},{10... | collective-permute-start | bytes 1075208 | tf_op jit(solution)/shard_map/ppermute | solution.py:26
  299.8 12.6 %collective-permute-start.32 = (bf16[160,960]{1,0:T(8,128)(2,1)S(1)}, bf16[160,960]{1,0:T(8,128)(2,1)S(1)}, u32[]{:S(2)}, u32[]{:S(2)}) collective-permute-start(bf16[160,960]{1,0:T(8,128)(2,1)S(1)} %pad_maximum_fusion.7), channel_id=1, source_target_pairs={{0,8},{8,0},{16,24},{24,16},{1,9},{9,1},{17,25},{25,17},{2,10},{10... | collective-permute-start | bytes 921608 | tf_op jit(solution)/shard_map/ppermute | solution.py:26
  308.0 5.6 %collective-permute-start.20 = (bf16[560,640]{1,0:T(8,128)(2,1)S(1)}, bf16[560,640]{1,0:T(8,128)(2,1)S(1)}, u32[]{:S(2)}, u32[]{:S(2)}) collective-permute-start(bf16[560,640]{1,0:T(8,128)(2,1)S(1)} %pad_maximum_fusion.3), channel_id=1, source_target_pairs={{0,8},{8,0},{16,24},{24,16},{1,9},{9,1},{17,25},{25,17},{2,10},{10... | collective-permute-start | bytes 2150408 | tf_op jit(solution)/shard_map/ppermute | solution.py:26
  (25 other events, 256.4 us)

commit v3 on v1

--- a/solution.py
+++ b/solution.py
@@ -127,17 +127,21 @@
     )
 
 
-def sum_over_devices(share, bits, y_first, scale):
+def scatter_low(share, bits, y_first):
     if y_first:
         share = halve(share, bits + 1, "dp", 1)
         share = halve(share, bits, "tm", 0)
     else:
         share = halve(share, bits, "tm", 0)
         share = halve(share, bits, "dp", 1)
+    share = jnp.moveaxis(share, 0, bits - 1)
+    return share.reshape(share.shape[: bits - 1] + (-1, share.shape[-1]))
+
+
+def scatter_high(share, bits, scale):
     for bit in range(1, bits):
-        share = halve(share, bits - bit, "tm", bit)
-    share = (share.astype(jnp.float32) * scale).astype(jnp.bfloat16)
-    return join(share, "dp", 1, 1)
+        share = halve(share, bits - 1 - bit, "tm", bit)
+    return (share.astype(jnp.float32) * scale).astype(jnp.bfloat16)
 
 
 def local(latents, conv_weight, qkv_weight, out_weight, out_cotangent):
@@ -210,17 +214,11 @@
         size = channels // tm_count // math.prod(parts)
         return share.reshape((taps,) + (2,) * bits + parts + (size, share.shape[1]))
 
-    def summed(share, taps):
+    def pieces(share, taps):
         share = by_bits(share, taps, (2, 2))
         ahead = lax.index_in_dim(share, 0, bits + 1, keepdims=False)
         behind = lax.index_in_dim(share, 1, bits + 1, keepdims=False)
-        return jnp.concatenate(
-            [
-                sum_over_devices(ahead, bits, False, grad_scale),
-                sum_over_devices(behind, bits, True, grad_scale),
-            ],
-            axis=1,
-        )
+        return [scatter_low(ahead, bits, False), scatter_low(behind, bits, True)]
 
     attended_other = swap(attended, "dp", 0)
     proj_share = (
@@ -245,10 +243,17 @@
         dot_columns(conv_left, gh_half) + dot_columns(conv_left_other, gh_half_other)
     ).astype(jnp.bfloat16)
 
-    proj_sum = sum_over_devices(by_bits(proj_share, 1, (2,)), bits, True, grad_scale)
-    qkv_sum = summed(qkv_share, 1)
-    conv_sum = summed(conv_share, 3)
-
+    proj_pieces = [scatter_low(by_bits(proj_share, 1, (2,)), bits, True)]
+    qkv_pieces = pieces(qkv_share, 1)
+    conv_pieces = pieces(conv_share, 3)
+    qkv_sum = scatter_high(jnp.concatenate(qkv_pieces, axis=bits - 1), bits, grad_scale)
+    rest_sum = scatter_high(
+        jnp.concatenate(conv_pieces + proj_pieces, axis=bits - 1), bits, grad_scale
+    )
+    qkv_both = join(join(qkv_sum[None], "dp", 1, 0), "dp", 0, 2)
+    rest_both = join(join(rest_sum[None], "dp", 1, 0), "dp", 0, 2)
+
+    grad_hidden, _ = lax.optimization_barrier((grad_hidden, conv_share))
     grad_four = grad_hidden.reshape(tm_count, half, loc, width)
     rim_after = from_behind(grad_four[:, 0], "tm", -1)
     grad_next = jnp.concatenate([grad_four[:, 1:], rim_after[:, None]], axis=1)
@@ -262,10 +267,11 @@
         (2, 0, 1, 3, 4),
     ).reshape(latents.shape)
 
-    proj_grad = join(proj_sum[0], "dp", 0, 1)
-    qkv_grad = join(qkv_sum[0], "dp", 0, 1)
-    conv_both = join(conv_sum[:, :, None], "dp", 0, 2)
-    conv_grad = jnp.transpose(conv_both, (1, 0, 2, 3)).reshape(conv_both.shape[1], 3 * width)
+    size = width // tm_count // 4
+    qkv_grad = jnp.transpose(qkv_both.reshape(2, 2, size, -1), (1, 0, 2, 3)).reshape(4 * size, -1)
+    conv_both = rest_both[:, : 6 * size].reshape(2, 2, 3, size, width)
+    conv_grad = jnp.transpose(conv_both, (1, 0, 3, 2, 4)).reshape(4 * size, 3 * width)
+    proj_grad = rest_both[:, 6 * size :].reshape(-1, width)
     return (input_grad, conv_grad, qkv_grad, proj_grad)
 
 

time: 262 us -> 253 us (0.966)
  starting transfers between devices: 49.8 us -> 37 us
  waiting for transfers between devices: 102 us -> 108 us
  matrix products: 32.2 us -> 29.3 us
    ppermute x34 -> x24, starting transfers between devices: 36.4 us -> 25.2 us  [swap(): lax.ppermute(shard, axis, [(i, i ^ 1 << bit) for i in range(devices)])]
    ppermute x34 -> x24, waiting for transfers between devices: 81.3 us -> 87.3 us  [swap(): lax.ppermute(shard, axis, [(i, i ^ 1 << bit) for i in range(devices)])]
    dot_general x5, matrix products: 13.8 us -> 10.8 us  [dot_rows_t(): lax.dot_general(left_side, right_side, (((1,), (1,)), ((), ())), preferre...]
    unnamed x36 -> x48, local copies, waits for them, and re-layouts: 4.17 us -> 7.02 us
  transfers between devices with their start and end apart: 37 -> 27, of which waited for: 16 -> 10; matrix products, arithmetic and copies ran while one was open for 21% -> 20% of each run, Pallas kernels for 0% -> 0%
where the time goes in v3:
time: 253 us; the launch traced here: 248 us
  waiting for transfers between devices  108 us (43%)
  starting transfers between devices  37 us (15%)
  blocking collectives  33.5 us (13%)
  matrix products  29.3 us (12%)
  local copies, waits for them, and re-layouts  23 us (9%)
  other arithmetic  10.1 us (4%)
  Pallas kernels  5.87 us (2%)
    ppermute x24, waiting for transfers between devices, swap(): lax.ppermute(shard, axis, [(i, i ^ 1 << bit) for i in range(devices)])  87.3 us
    all_to_all x1, blocking collectives, local(): lax.all_to_all(outgoing, 'tm', split_axis=0, concat_axis=0, tiled=True)  33.5 us
    ppermute x24, starting transfers between devices, swap(): lax.ppermute(shard, axis, [(i, i ^ 1 << bit) for i in range(devices)])  25.2 us
    all_to_all x1, waiting for transfers between devices, local(): lax.all_to_all(result.reshape(tm_count, half * loc, 4 * attn_width), 'tm'...  20.7 us
    dot_general x6, matrix products, dot_columns(): lax.dot_general(left_side, right_side, (((0,), (0,)), ((), ())), preferre...  11.6 us
    dot_general x5, matrix products, dot_rows_t(): lax.dot_general(left_side, right_side, (((1,), (1,)), ((), ())), preferre...  10.8 us
    unnamed x48, local copies, waits for them, and re-layouts  7.02 us
    dot_general x4, matrix products, dot_rows(): return jnp.dot(left_side, right_side, preferred_element_type=jnp.float32)  6.91 us
  transfers between devices with their start and end apart: 27, of which 10 were waited for; matrix products, arithmetic and copies ran while one was open for 20% of the time, Pallas kernels for 0%

profile of v3, /device:TPU:17, one launch (start us, length us, event | category | flops | bytes accessed | tf_op | source)
XLA Modules:
  0.0 248.1 jit_solution(8189511158327363241)
XLA Ops:
  1.7 3.1 %collective-permute-start = (bf16[8,8,1280]{2,1,0:T(8,128)(2,1)S(1)}, bf16[8,8,1280]{2,1,0:T(8,128)(2,1)S(1)}, u32[]{:S(2)}, u32[]{:S(2)}) collective-permute-start(bf16[8,8,1280]{2,1,0:T(8,128)(2,1)S(1)} %slice_bitcast_fusion.1), channel_id=1, source_target_pairs={{0,1},{1,2},{2,3},{3,4},{4,5},{5,6},{6,7},{8,9},{9,10},{10,11},{11... | collective-permute-start | bytes 491528 | tf_op jit(solution)/shard_map/ppermute | solution.py:21
  6.4 3.2 %fusion.6 = f32[256,1280]{1,0:T(8,128)S(1)} fusion(bf16[256,1280]{1,0:T(8,128)(2,1)S(1)} %bitcast.174, bf16[1280,3840]{1,0:T(8,128)(2,1)} %param.6), kind=kOutput, calls=%fused_computation.8 | convolution fusion | flops 838860800 | bytes 5242880 | tf_op jit(solution)/shard_map/dot_general | solution.py:34
  14.9 1.6 convolution_convert_fusion
  16.6 33.5 %all_to_all.10 = bf16[8,32,2560]{2,1,0:T(8,128)(2,1)S(1)} all-to-all(bf16[8,32,2560]{2,1,0:T(8,128)(2,1)S(1)} %bitcast.185), channel_id=1, replica_groups=mesh['dp'=4,'tm'=8] {'tm'}, dimensions={0} | all-to-all | bytes 2621440 | tf_op jit(solution)/shard_map/all_to_all | solution.py:198
  50.0 5.9 %shard_map.84 = bf16[256,2560]{1,0:T(8,128)(2,1)} custom-call(bf16[256,2560]{1,0:T(8,128)(2,1)S(1)} %bitcast.163), custom_call_target="tpu_custom_call" | custom-call | flops 1174405120 | bytes 2621440 | tf_op jit(solution)/shard_map/pallas_call | solution.py:100
  55.9 5.5 %all-to-all-start.1 = ((bf16[8,32,2560]{2,1,0:T(8,128)(2,1)}), bf16[8,32,2560]{2,1,0:T(8,128)(2,1)S(1)}, u32[]{:S(2)}, u32[]{:S(2)}) async-start(bf16[8,32,2560]{2,1,0:T(8,128)(2,1)} %bitcast.15), calls=%async_computation.1 | async-start | bytes 2621440 | tf_op jit(solution)/shard_map/all_to_all | solution.py:200
  61.4 1.7 constant_dynamic-slice_fusion.5
  63.2 1.7 collective-permute-start.9
  64.8 2.7 %pad_maximum_fusion = bf16[256,3840]{1,0:T(8,128)(2,1)} fusion(bf16[256,1280]{1,0:T(8,128)(2,1)S(1)} %bitcast.172, bf16[256,1280]{1,0:T(8,128)(2,1)} %bitcast.175, bf16[256,1280]{1,0:T(8,128)(2,1)} %bitcast.178), kind=kLoop, calls=%fused_computation.26 | loop fusion | flops 5898240 | bytes 3932160 | tf_op jit(solution)/shard_map/concatenate | solution.py:180
  68.1 20.7 %all-to-all-done.1 = bf16[8,32,2560]{2,1,0:T(8,128)(2,1)S(1)} async-done(((bf16[8,32,2560]{2,1,0:T(8,128)(2,1)}), bf16[8,32,2560]{2,1,0:T(8,128)(2,1)S(1)}, u32[]{:S(2)}, u32[]{:S(2)}) %all-to-all-start.1) | async-done | bytes 1310752 | tf_op jit(solution)/shard_map/all_to_all | solution.py:200
  88.9 4.1 %fusion.70 = (f32[256]{0:T(256)S(1)}, f32[256]{0:T(256)S(1)}, f32[256,1280]{1,0:T(8,128)S(1)}) fusion(f32[256]{0:T(256)S(1)} %add_rsqrt_fusion, f32[256,1280]{1,0:T(8,128)S(1)} %get-tuple-element.32, f32[256]{0:T(256)S(1)} %broadcast_multiply_fusion.2, bf16[1280,1920]{1,0:T(8,128)(2,1)} %param.7, bf16[256,2560]{1,0:T(8,128)(2,1)S(1)} %bitcast.168), kind=kOutput, calls=%fused_computation.140 | convolution fusion | flops 1259929088 | bytes 8523776 | tf_op jit(solution)/shard_map/dot_general | solution.py:38
  93.0 2.2 collective-permute-start.8
  98.7 1.7 fusion.60
  104.7 3.3 %add_convert_fusion = bf16[3840,640]{1,0:T(8,128)(2,1)S(1)} fusion(f32[3840,640]{1,0:T(8,128)S(1)} %fusion.60, bf16[256,3840]{1,0:T(8,128)(2,1)} %collective-permute-done.1, bf16[256,640]{1,0:T(8,128)(2,1)S(1)} %collective-permute-done.2), kind=kOutput, calls=%fused_computation | convolution fusion | flops 1263206400 | bytes 17039360 | tf_op jit(solution)/shard_map/dot_general | solution.py:44
  108.7 3.1 %collective-permute-start.3 = (bf16[8,8,1280]{2,1,0:T(8,128)(2,1)}, bf16[8,8,1280]{2,1,0:T(8,128)(2,1)}, u32[]{:S(2)}, u32[]{:S(2)}) collective-permute-start(bf16[8,8,1280]{2,1,0:T(8,128)(2,1)} %slice_bitcast_fusion), channel_id=1, source_target_pairs={{1,0},{2,1},{3,2},{4,3},{5,4},{6,5},{7,6},{9,8},{10,9},{11,10},{12... | collective-permute-start | bytes 491528 | tf_op jit(solution)/shard_map/ppermute | solution.py:21
  111.9 1.9 fusion.71
  116.6 3.9 %fusion.21 = bf16[256,1280]{1,0:T(8,128)(2,1)} fusion(bf16[256,1280]{1,0:T(8,128)(2,1)S(1)} %add_convert_fusion.3, bf16[1280,3840]{1,0:T(8,128)(2,1)} %param.6), kind=kOutput, calls=%fused_computation.17 | convolution fusion | flops 839188480 | bytes 4587520 | tf_op jit(solution)/shard_map/dot_general | solution.py:38
  120.5 3.5 %add_convert_fusion.1 = bf16[1280,960]{0,1:T(8,128)(2,1)} fusion(f32[1280,960]{0,1:T(8,128)S(1)} %fusion.47, bf16[256,1280]{1,0:T(8,128)(2,1)} %collective-permute-done.16, bf16[256,960]{1,0:T(8,128)(2,1)S(1)} %collective-permute-done.17), kind=kOutput, calls=%fused_computation.1 | convolution fusion | flops 631603200 | bytes 8519680 | tf_op jit(solution)/shard_map/dot_general | solution.py:44
  124.0 3.0 %copy.38 = bf16[1280,960]{1,0:T(8,128)(2,1)S(1)} copy(bf16[1280,960]{0,1:T(8,128)(2,1)} %add_convert_fusion.1) | data formatting | bytes 4915200 | tf_op jit(solution)/shard_map/convert_element_type | solution.py:229
  130.8 17.9 %collective-permute-done.11 = bf16[1,2,2,40,640]{4,3,2,1,0:T(8,128)(2,1)S(1)} collective-permute-done((bf16[1,2,2,40,640]{4,3,2,1,0:T(8,128)(2,1)S(1)}, bf16[1,2,2,40,640]{4,3,2,1,0:T(8,128)(2,1)S(1)}, u32[]{:S(2)}, u32[]{:S(2)}) %collective-permute-start.11) | collective-permute-done | bytes 204832 | tf_op jit(solution)/shard_map/ppermute | solution.py:26
  149.9 12.9 %collective-permute-done.18 = bf16[1,2,2,2,40,960]{5,4,2,1,3,0:T(8,128)(2,1)S(1)} collective-permute-done((bf16[1,2,2,2,40,960]{5,4,2,1,3,0:T(8,128)(2,1)S(1)}, bf16[1,2,2,2,40,960]{5,4,2,1,3,0:T(8,128)(2,1)S(1)}, u32[]{:S(2)}, u32[]{:S(2)}) %collective-permute-start.18) | collective-permute-done | bytes 614432 | tf_op jit(solution)/shard_map/ppermute | solution.py:26
  163.4 6.4 %collective-permute-done.21 = bf16[1,2,2,40,960]{4,3,2,1,0:T(8,128)(2,1)S(1)} collective-permute-done((bf16[1,2,2,40,960]{4,3,2,1,0:T(8,128)(2,1)S(1)}, bf16[1,2,2,40,960]{4,3,2,1,0:T(8,128)(2,1)S(1)}, u32[]{:S(2)}, u32[]{:S(2)}) %collective-permute-start.21) | collective-permute-done | bytes 307232 | tf_op jit(solution)/shard_map/ppermute | solution.py:26
  169.9 1.8 fusion.34
  172.1 2.7 %collective-permute-done.6 = bf16[3,2,2,2,40,640]{5,4,0,2,1,3:T(8,128)(2,1)S(1)} collective-permute-done((bf16[3,2,2,2,40,640]{5,4,0,2,1,3:T(8,128)(2,1)S(1)}, bf16[3,2,2,2,40,640]{5,4,0,2,1,3:T(8,128)(2,1)S(1)}, u32[]{:S(2)}, u32[]{:S(2)}) %collective-permute-start.6) | collective-permute-done | bytes 1228832 | tf_op jit(solution)/shard_map/ppermute | solution.py:26
  175.7 6.1 %collective-permute-done.19 = bf16[1,2,2,40,960]{4,3,2,1,0:T(8,128)(2,1)S(1)} collective-permute-done((bf16[1,2,2,40,960]{4,3,2,1,0:T(8,128)(2,1)S(1)}, bf16[1,2,2,40,960]{4,3,2,1,0:T(8,128)(2,1)S(1)}, u32[]{:S(2)}, u32[]{:S(2)}) %collective-permute-start.19) | collective-permute-done | bytes 307232 | tf_op jit(solution)/shard_map/ppermute | solution.py:26
  183.2 11.7 %collective-permute-done.5 = bf16[3,2,2,40,640]{4,3,0,2,1:T(8,128)(2,1)S(1)} collective-permute-done((bf16[3,2,2,40,640]{4,3,0,2,1:T(8,128)(2,1)S(1)}, bf16[3,2,2,40,640]{4,3,0,2,1:T(8,128)(2,1)S(1)}, u32[]{:S(2)}, u32[]{:S(2)}) %collective-permute-start.5) | collective-permute-done | bytes 614432 | tf_op jit(solution)/shard_map/ppermute | solution.py:26
  199.0 3.1 %collective-permute-start.23 = (bf16[80,960]{1,0:T(8,128)(2,1)S(1)}, bf16[80,960]{1,0:T(8,128)(2,1)S(1)}, u32[]{:S(2)}, u32[]{:S(2)}) collective-permute-start(bf16[80,960]{1,0:T(8,128)(2,1)S(1)} %dynamic-slice_bitcast_fusion.8), channel_id=1, source_target_pairs={{0,4},{1,5},{2,6},{3,7},{4,0},{5,1},{6,2},{7,3},{8,12},{9,13},{10,... | collective-permute-start | bytes 460808 | tf_op jit(solution)/shard_map/ppermute | solution.py:26
  202.1 10.1 %collective-permute-done.12 = bf16[2,280,640]{2,1,0:T(8,128)(2,1)S(1)} collective-permute-done((bf16[2,280,640]{2,1,0:T(8,128)(2,1)S(1)}, bf16[2,280,640]{2,1,0:T(8,128)(2,1)S(1)}, u32[]{:S(2)}, u32[]{:S(2)}) %collective-permute-start.12) | collective-permute-done | bytes 716832 | tf_op jit(solution)/shard_map/ppermute | solution.py:26
  212.4 4.6 %collective-permute-start.13 = (bf16[280,640]{1,0:T(8,128)(2,1)S(1)}, bf16[280,640]{1,0:T(8,128)(2,1)S(1)}, u32[]{:S(2)}, u32[]{:S(2)}) collective-permute-start(bf16[280,640]{1,0:T(8,128)(2,1)S(1)} %dynamic-slice_bitcast_fusion.4), channel_id=1, source_target_pairs={{0,4},{1,5},{2,6},{3,7},{4,0},{5,1},{6,2},{7,3},{8,12},{9,13},{10,... | collective-permute-start | bytes 1075208 | tf_op jit(solution)/shard_map/ppermute | solution.py:26
  218.5 12.6 %collective-permute-done.13 = bf16[280,640]{1,0:T(8,128)(2,1)S(1)} collective-permute-done((bf16[280,640]{1,0:T(8,128)(2,1)S(1)}, bf16[280,640]{1,0:T(8,128)(2,1)S(1)}, u32[]{:S(2)}, u32[]{:S(2)}) %collective-permute-start.13) | collective-permute-done | bytes 358432 | tf_op jit(solution)/shard_map/ppermute | solution.py:26
  233.1 6.8 %collective-permute-done.14 = bf16[1,280,640]{2,1,0:T(8,128)(2,1)S(1)} collective-permute-done((bf16[1,280,640]{2,1,0:T(8,128)(2,1)S(1)}, bf16[1,280,640]{2,1,0:T(8,128)(2,1)S(1)}, u32[]{:S(2)}, u32[]{:S(2)}) %collective-permute-start.14) | collective-permute-done | bytes 358432 | tf_op jit(solution)/shard_map/ppermute | solution.py:26
  240.1 2.2 collective-permute-start.15
  (159 shorter events, 41.5 us)
Async XLA Ops:
  1.7 8.6 %collective-permute-start = (bf16[8,8,1280]{2,1,0:T(8,128)(2,1)S(1)}, bf16[8,8,1280]{2,1,0:T(8,128)(2,1)S(1)}, u32[]{:S(2)}, u32[]{:S(2)}) collective-permute-start(bf16[8,8,1280]{2,1,0:T(8,128)(2,1)S(1)} %slice_bitcast_fusion.1), channel_id=1, source_target_pairs={{0,1},{1,2},{2,3},{3,4},{4,5},{5,6},{6,7},{8,9},{9,10},{10,11},{11... | collective-permute-start | bytes 491528 | tf_op jit(solution)/shard_map/ppermute | solution.py:21
  55.9 32.9 %all-to-all-start.1 = ((bf16[8,32,2560]{2,1,0:T(8,128)(2,1)}), bf16[8,32,2560]{2,1,0:T(8,128)(2,1)S(1)}, u32[]{:S(2)}, u32[]{:S(2)}) async-start(bf16[8,32,2560]{2,1,0:T(8,128)(2,1)} %bitcast.15), calls=%async_computation.1 | async-start | bytes 2621440 | tf_op jit(solution)/shard_map/all_to_all | solution.py:200
  63.2 37.2 %collective-permute-start.9 = (bf16[256,640]{1,0:T(8,128)(2,1)}, bf16[256,640]{1,0:T(8,128)(2,1)}, u32[]{:S(2)}, u32[]{:S(2)}) collective-permute-start(bf16[256,640]{1,0:T(8,128)(2,1)} %constant_dynamic-slice_fusion.5), channel_id=1, source_target_pairs={{0,8},{8,0},{16,24},{24,16},{1,9},{9,1},{17,25},{25,17},{2,10},{10... | collective-permute-start | bytes 983048 | tf_op jit(solution)/shard_map/ppermute | solution.py:26
  64.8 55.6 %collective-permute-start.16 = (bf16[256,1280]{1,0:T(8,128)(2,1)}, bf16[256,1280]{1,0:T(8,128)(2,1)}, u32[]{:S(2)}, u32[]{:S(2)}) collective-permute-start(bf16[256,1280]{1,0:T(8,128)(2,1)} %copy-done.12), channel_id=1, source_target_pairs={{0,8},{8,0},{16,24},{24,16},{1,9},{9,1},{17,25},{25,17},{2,10},{10... | collective-permute-start | bytes 1966088 | tf_op jit(solution)/shard_map/ppermute | solution.py:26
  67.5 37.2 %collective-permute-start.1 = (bf16[256,3840]{1,0:T(8,128)(2,1)}, bf16[256,3840]{1,0:T(8,128)(2,1)}, u32[]{:S(2)}, u32[]{:S(2)}) collective-permute-start(bf16[256,3840]{1,0:T(8,128)(2,1)} %pad_maximum_fusion), channel_id=1, source_target_pairs={{0,8},{8,0},{16,24},{24,16},{1,9},{9,1},{17,25},{25,17},{2,10},{10... | collective-permute-start | bytes 5898248 | tf_op jit(solution)/shard_map/ppermute | solution.py:26
  93.0 8.2 %collective-permute-start.8 = (bf16[256,640]{1,0:T(8,128)(2,1)S(1)}, bf16[256,640]{1,0:T(8,128)(2,1)S(1)}, u32[]{:S(2)}, u32[]{:S(2)}) collective-permute-start(bf16[256,640]{1,0:T(8,128)(2,1)S(1)} %slice.77), channel_id=1, source_target_pairs={{0,8},{8,0},{16,24},{24,16},{1,9},{9,1},{17,25},{25,17},{2,10},{10... | collective-permute-start | bytes 983048 | tf_op jit(solution)/shard_map/ppermute | solution.py:26
  95.4 25.1 %collective-permute-start.17 = (bf16[256,960]{1,0:T(8,128)(2,1)S(1)}, bf16[256,960]{1,0:T(8,128)(2,1)S(1)}, u32[]{:S(2)}, u32[]{:S(2)}) collective-permute-start(bf16[256,960]{1,0:T(8,128)(2,1)S(1)} %constant_dynamic-slice_fusion.2), channel_id=1, source_target_pairs={{0,8},{8,0},{16,24},{24,16},{1,9},{9,1},{17,25},{25,17},{2,10},{10... | collective-permute-start | bytes 1474568 | tf_op jit(solution)/shard_map/ppermute | solution.py:26
  96.0 20.6 %copy-start.9 = (bf16[256,1280]{1,0:T(8,128)(2,1)}, bf16[256,1280]{1,0:T(8,128)(2,1)S(1)}, u32[]{:S(2)}) copy-start(bf16[256,1280]{1,0:T(8,128)(2,1)S(1)} %add_convert_fusion.3) | copy-start | bytes 1966084
  100.4 4.3 %collective-permute-start.2 = (bf16[256,640]{1,0:T(8,128)(2,1)S(1)}, bf16[256,640]{1,0:T(8,128)(2,1)S(1)}, u32[]{:S(2)}, u32[]{:S(2)}) collective-permute-start(bf16[256,640]{1,0:T(8,128)(2,1)S(1)} %constant_dynamic-slice_fusion.10), channel_id=1, source_target_pairs={{0,8},{8,0},{16,24},{24,16},{1,9},{9,1},{17,25},{25,17},{2,10},{10... | collective-permute-start | bytes 983048 | tf_op jit(solution)/shard_map/ppermute | solution.py:26
  103.5 24.1 %collective-permute-start.10 = (bf16[1,2,2,2,40,640]{5,4,2,1,3,0:T(8,128)(2,1)}, bf16[1,2,2,2,40,640]{5,4,2,1,3,0:T(8,128)(2,1)S(1)}, u32[]{:S(2)}, u32[]{:S(2)}) collective-permute-start(bf16[1,2,2,2,40,640]{5,4,2,1,3,0:T(8,128)(2,1)} %bitcast.162), channel_id=1, source_target_pairs={{0,16},{8,24},{16,0},{24,8},{1,17},{9,25},{17,1},{25,9},{2,18},{10... | collective-permute-start | bytes 1228808 | tf_op jit(solution)/shard_map/ppermute | solution.py:26
  108.7 89.1 %collective-permute-start.3 = (bf16[8,8,1280]{2,1,0:T(8,128)(2,1)}, bf16[8,8,1280]{2,1,0:T(8,128)(2,1)}, u32[]{:S(2)}, u32[]{:S(2)}) collective-permute-start(bf16[8,8,1280]{2,1,0:T(8,128)(2,1)} %slice_bitcast_fusion), channel_id=1, source_target_pairs={{1,0},{2,1},{3,2},{4,3},{5,4},{6,5},{7,6},{9,8},{10,9},{11,10},{12... | collective-permute-start | bytes 491528 | tf_op jit(solution)/shard_map/ppermute | solution.py:21
  116.1 53.8 %collective-permute-start.4 = (bf16[3,2,2,2,40,640]{5,4,0,2,1,3:T(8,128)(2,1)}, bf16[3,2,2,2,40,640]{5,4,0,2,1,3:T(8,128)(2,1)}, u32[]{:S(2)}, u32[]{:S(2)}) collective-permute-start(bf16[3,2,2,2,40,640]{5,4,0,2,1,3:T(8,128)(2,1)} %bitcast.160), channel_id=1, source_target_pairs={{0,1},{1,0},{2,3},{3,2},{4,5},{5,4},{6,7},{7,6},{8,9},{9,8},{10,11... | collective-permute-start | bytes 3686408 | tf_op jit(solution)/shard_map/ppermute | solution.py:26
  127.3 21.7 %collective-permute-start.20 = (bf16[1,2,2,2,40,960]{5,4,3,2,1,0:T(8,128)(2,1)S(1)}, bf16[1,2,2,2,40,960]{5,4,3,2,1,0:T(8,128)(2,1)S(1)}, u32[]{:S(2)}, u32[]{:S(2)}) collective-permute-start(bf16[1,2,2,2,40,960]{5,4,3,2,1,0:T(8,128)(2,1)S(1)} %dynamic-slice_bitcast_fusion.1), channel_id=1, source_target_pairs={{0,16},{8,24},{16,0},{24,8},{1,17},{9,25},{17,1},{25,9},{2,18},{10... | collective-permute-start | bytes 1843208 | tf_op jit(solution)/shard_map/ppermute | solution.py:26
  127.7 21.0 %collective-permute-start.11 = (bf16[1,2,2,40,640]{4,3,2,1,0:T(8,128)(2,1)S(1)}, bf16[1,2,2,40,640]{4,3,2,1,0:T(8,128)(2,1)S(1)}, u32[]{:S(2)}, u32[]{:S(2)}) collective-permute-start(bf16[1,2,2,40,640]{4,3,2,1,0:T(8,128)(2,1)S(1)} %dynamic-slice_bitcast_fusion.7), channel_id=1, source_target_pairs={{0,1},{1,0},{2,3},{3,2},{4,5},{5,4},{6,7},{7,6},{8,9},{9,8},{10,11... | collective-permute-start | bytes 614408 | tf_op jit(solution)/shard_map/ppermute | solution.py:26
  129.0 33.8 %collective-permute-start.18 = (bf16[1,2,2,2,40,960]{5,4,2,1,3,0:T(8,128)(2,1)S(1)}, bf16[1,2,2,2,40,960]{5,4,2,1,3,0:T(8,128)(2,1)S(1)}, u32[]{:S(2)}, u32[]{:S(2)}) collective-permute-start(bf16[1,2,2,2,40,960]{5,4,2,1,3,0:T(8,128)(2,1)S(1)} %bitcast.199), channel_id=1, source_target_pairs={{0,1},{1,0},{2,3},{3,2},{4,5},{5,4},{6,7},{7,6},{8,9},{9,8},{10,11... | collective-permute-start | bytes 1843208 | tf_op jit(solution)/shard_map/ppermute | solution.py:26
  148.7 26.0 %collective-permute-start.6 = (bf16[3,2,2,2,40,640]{5,4,0,2,1,3:T(8,128)(2,1)S(1)}, bf16[3,2,2,2,40,640]{5,4,0,2,1,3:T(8,128)(2,1)S(1)}, u32[]{:S(2)}, u32[]{:S(2)}) collective-permute-start(bf16[3,2,2,2,40,640]{5,4,0,2,1,3:T(8,128)(2,1)S(1)} %bitcast.194), channel_id=1, source_target_pairs={{0,16},{8,24},{16,0},{24,8},{1,17},{9,25},{17,1},{25,9},{2,18},{10... | collective-permute-start | bytes 3686408 | tf_op jit(solution)/shard_map/ppermute | solution.py:26
  149.0 47.7 %slice-start = ((s8[9830400]{0:T(1024)(128)(4,1)}), s8[1441792]{0:T(1024)(128)(4,1)S(1)}, s32[]{:S(2)}) async-start(s8[9830400]{0:T(1024)(128)(4,1)} %bitcast.204), calls=%async_computation.2 | async-start | bytes 2883584
  149.3 20.4 %collective-permute-start.21 = (bf16[1,2,2,40,960]{4,3,2,1,0:T(8,128)(2,1)S(1)}, bf16[1,2,2,40,960]{4,3,2,1,0:T(8,128)(2,1)S(1)}, u32[]{:S(2)}, u32[]{:S(2)}) collective-permute-start(bf16[1,2,2,40,960]{4,3,2,1,0:T(8,128)(2,1)S(1)} %dynamic-slice_bitcast_fusion.5), channel_id=1, source_target_pairs={{0,1},{1,0},{2,3},{3,2},{4,5},{5,4},{6,7},{7,6},{8,9},{9,8},{10,11... | collective-permute-start | bytes 921608 | tf_op jit(solution)/shard_map/ppermute | solution.py:26
  163.1 18.7 %collective-permute-start.19 = (bf16[1,2,2,40,960]{4,3,2,1,0:T(8,128)(2,1)S(1)}, bf16[1,2,2,40,960]{4,3,2,1,0:T(8,128)(2,1)S(1)}, u32[]{:S(2)}, u32[]{:S(2)}) collective-permute-start(bf16[1,2,2,40,960]{4,3,2,1,0:T(8,128)(2,1)S(1)} %dynamic-slice_bitcast_fusion.6), channel_id=1, source_target_pairs={{0,16},{8,24},{16,0},{24,8},{1,17},{9,25},{17,1},{25,9},{2,18},{10... | collective-permute-start | bytes 921608 | tf_op jit(solution)/shard_map/ppermute | solution.py:26
  169.9 26.8 %slice-start.1 = ((s8[9830400]{0:T(1024)(128)(4,1)}), s8[4194304]{0:T(1024)(128)(4,1)S(1)}, s32[]{:S(2)}) async-start(s8[9830400]{0:T(1024)(128)(4,1)} %bitcast.204), calls=%async_computation.3 | async-start | bytes 8388608
  171.8 23.2 %collective-permute-start.5 = (bf16[3,2,2,40,640]{4,3,0,2,1:T(8,128)(2,1)S(1)}, bf16[3,2,2,40,640]{4,3,0,2,1:T(8,128)(2,1)S(1)}, u32[]{:S(2)}, u32[]{:S(2)}) collective-permute-start(bf16[3,2,2,40,640]{4,3,0,2,1:T(8,128)(2,1)S(1)} %dynamic-slice_bitcast_fusion.3), channel_id=1, source_target_pairs={{0,16},{8,24},{16,0},{24,8},{1,17},{9,25},{17,1},{25,9},{2,18},{10... | collective-permute-start | bytes 1843208 | tf_op jit(solution)/shard_map/ppermute | solution.py:26
  175.1 20.0 %collective-permute-start.7 = (bf16[3,2,2,40,640]{4,3,0,2,1:T(8,128)(2,1)S(1)}, bf16[3,2,2,40,640]{4,3,0,2,1:T(8,128)(2,1)S(1)}, u32[]{:S(2)}, u32[]{:S(2)}) collective-permute-start(bf16[3,2,2,40,640]{4,3,0,2,1:T(8,128)(2,1)S(1)} %dynamic-slice_bitcast_fusion.2), channel_id=1, source_target_pairs={{0,1},{1,0},{2,3},{3,2},{4,5},{5,4},{6,7},{7,6},{8,9},{9,8},{10,11... | collective-permute-start | bytes 1843208 | tf_op jit(solution)/shard_map/ppermute | solution.py:26
  181.9 14.9 %slice-start.2 = ((s8[9830400]{0:T(1024)(128)(4,1)}), s8[4194304]{0:T(1024)(128)(4,1)S(1)}, s32[]{:S(2)}) async-start(s8[9830400]{0:T(1024)(128)(4,1)} %bitcast.204), calls=%async_computation.4 | async-start | bytes 8388608
  181.9 17.0 %collective-permute-start.22 = (bf16[2,80,960]{2,1,0:T(8,128)(2,1)S(1)}, bf16[2,80,960]{2,1,0:T(8,128)(2,1)S(1)}, u32[]{:S(2)}, u32[]{:S(2)}) collective-permute-start(bf16[2,80,960]{2,1,0:T(8,128)(2,1)S(1)} %fusion.54), channel_id=1, source_target_pairs={{0,2},{1,3},{2,0},{3,1},{4,6},{5,7},{6,4},{7,5},{8,10},{9,11},{10,... | collective-permute-start | bytes 921608 | tf_op jit(solution)/shard_map/ppermute | solution.py:26
  195.5 16.7 %collective-permute-start.12 = (bf16[2,280,640]{2,1,0:T(8,128)(2,1)S(1)}, bf16[2,280,640]{2,1,0:T(8,128)(2,1)S(1)}, u32[]{:S(2)}, u32[]{:S(2)}) collective-permute-start(bf16[2,280,640]{2,1,0:T(8,128)(2,1)S(1)} %dynamic-slice_bitcast_fusion), channel_id=1, source_target_pairs={{0,2},{1,3},{2,0},{3,1},{4,6},{5,7},{6,4},{7,5},{8,10},{9,11},{10,... | collective-permute-start | bytes 2150408 | tf_op jit(solution)/shard_map/ppermute | solution.py:26
  199.0 19.1 %collective-permute-start.23 = (bf16[80,960]{1,0:T(8,128)(2,1)S(1)}, bf16[80,960]{1,0:T(8,128)(2,1)S(1)}, u32[]{:S(2)}, u32[]{:S(2)}) collective-permute-start(bf16[80,960]{1,0:T(8,128)(2,1)S(1)} %dynamic-slice_bitcast_fusion.8), channel_id=1, source_target_pairs={{0,4},{1,5},{2,6},{3,7},{4,0},{5,1},{6,2},{7,3},{8,12},{9,13},{10,... | collective-permute-start | bytes 460808 | tf_op jit(solution)/shard_map/ppermute | solution.py:26
  212.4 18.7 %collective-permute-start.13 = (bf16[280,640]{1,0:T(8,128)(2,1)S(1)}, bf16[280,640]{1,0:T(8,128)(2,1)S(1)}, u32[]{:S(2)}, u32[]{:S(2)}) collective-permute-start(bf16[280,640]{1,0:T(8,128)(2,1)S(1)} %dynamic-slice_bitcast_fusion.4), channel_id=1, source_target_pairs={{0,4},{1,5},{2,6},{3,7},{4,0},{5,1},{6,2},{7,3},{8,12},{9,13},{10,... | collective-permute-start | bytes 1075208 | tf_op jit(solution)/shard_map/ppermute | solution.py:26
  218.2 13.3 %collective-permute-start.24 = (bf16[1,80,960]{2,1,0:T(8,128)(2,1)S(1)}, bf16[1,80,960]{2,1,0:T(8,128)(2,1)S(1)}, u32[]{:S(2)}, u32[]{:S(2)}) collective-permute-start(bf16[1,80,960]{2,1,0:T(8,128)(2,1)S(1)} %fusion.63), channel_id=1, source_target_pairs={{0,16},{8,24},{16,0},{24,8},{1,17},{9,25},{17,1},{25,9},{2,18},{10... | collective-permute-start | bytes 460808 | tf_op jit(solution)/shard_map/ppermute | solution.py:26
  231.2 8.7 %collective-permute-start.14 = (bf16[1,280,640]{2,1,0:T(8,128)(2,1)S(1)}, bf16[1,280,640]{2,1,0:T(8,128)(2,1)S(1)}, u32[]{:S(2)}, u32[]{:S(2)}) collective-permute-start(bf16[1,280,640]{2,1,0:T(8,128)(2,1)S(1)} %fusion.50), channel_id=1, source_target_pairs={{0,16},{8,24},{16,0},{24,8},{1,17},{9,25},{17,1},{25,9},{2,18},{10... | collective-permute-start | bytes 1075208 | tf_op jit(solution)/shard_map/ppermute | solution.py:26
  231.6 10.7 %copy-start.15 = (bf16[256,1280]{1,0:T(8,128)(2,1)S(1)}, bf16[256,1280]{1,0:T(8,128)(2,1)}, u32[]{:S(2)}) copy-start(bf16[256,1280]{1,0:T(8,128)(2,1)} %fusion.21) | copy-start | bytes 1966084
  231.6 12.0 %collective-permute-start.25 = (bf16[2,80,960]{2,1,0:T(8,128)(2,1)S(1)}, bf16[2,80,960]{2,1,0:T(8,128)(2,1)S(1)}, u32[]{:S(2)}, u32[]{:S(2)}) collective-permute-start(bf16[2,80,960]{2,1,0:T(8,128)(2,1)S(1)} %pad_maximum_fusion.7), channel_id=1, source_target_pairs={{0,8},{8,0},{16,24},{24,16},{1,9},{9,1},{17,25},{25,17},{2,10},{10... | collective-permute-start | bytes 921608 | tf_op jit(solution)/shard_map/ppermute | solution.py:26
  240.1 4.5 %collective-permute-start.15 = (bf16[2,280,640]{2,1,0:T(8,128)(2,1)S(1)}, bf16[2,280,640]{2,1,0:T(8,128)(2,1)S(1)}, u32[]{:S(2)}, u32[]{:S(2)}) collective-permute-start(bf16[2,280,640]{2,1,0:T(8,128)(2,1)S(1)} %pad_maximum_fusion.3), channel_id=1, source_target_pairs={{0,8},{8,0},{16,24},{24,16},{1,9},{9,1},{17,25},{25,17},{2,10},{10... | collective-permute-start | bytes 2150408 | tf_op jit(solution)/shard_map/ppermute | solution.py:26
  (17 other events, 54.9 us)

commit v4 on v1

--- a/solution.py
+++ b/solution.py
@@ -111,33 +111,177 @@
     )(packed)
 
 
-def halve(array, position, axis, bit):
-    mine = bit_of(axis, bit)
-    away = lax.dynamic_index_in_dim(array, 1 - mine, position, keepdims=False)
-    stay = lax.dynamic_index_in_dim(array, mine, position, keepdims=False)
-    came = swap(away, axis, bit)
-    return (stay.astype(jnp.float32) + came.astype(jnp.float32)).astype(jnp.bfloat16)
-
-
-def join(array, axis, bit, position):
-    came = swap(array, axis, bit)
-    first = bit_of(axis, bit) == 0
-    return jnp.concatenate(
-        [jnp.where(first, array, came), jnp.where(first, came, array)], axis=position
-    )
-
-
-def sum_over_devices(share, bits, y_first, scale):
-    if y_first:
-        share = halve(share, bits + 1, "dp", 1)
-        share = halve(share, bits, "tm", 0)
-    else:
-        share = halve(share, bits, "tm", 0)
-        share = halve(share, bits, "dp", 1)
-    for bit in range(1, bits):
-        share = halve(share, bits - bit, "tm", bit)
-    share = (share.astype(jnp.float32) * scale).astype(jnp.bfloat16)
-    return join(share, "dp", 1, 1)
+def sum_kernel(scale, high, *refs):
+    ins, outs = refs[:3], refs[3:6]
+    scratch = [refs[6 + 6 * i : 12 + 6 * i] for i in range(3)]
+    send_sem, recv_sem = refs[24], refs[25]
+    dp, tm = lax.axis_index("dp"), lax.axis_index("tm")
+    core, my = dp % 2, dp // 2
+    mx, mz = tm % 2, tm // 2
+    x_peer = (dp, tm + 1 - 2 * mx)
+    y_peer = (dp + 2 - 4 * my, tm)
+    core_peer = (dp + 1 - 2 * core, tm)
+    z_peers = [(dp, (mz + d) % high * 2 + mx) for d in range(1, high)]
+
+    barrier = pltpu.get_barrier_semaphore()
+    for peer in [x_peer, y_peer, core_peer] + z_peers:
+        pl.semaphore_signal(
+            barrier, inc=1, device_id=peer, device_id_type=pl.DeviceIdType.MESH
+        )
+    pl.semaphore_wait(barrier, 3 + len(z_peers))
+
+    wide = ins[0].shape[-1]
+    cut = wide // 256 * 128 if wide > 256 else wide
+    low, rest = pl.ds(0, cut), pl.ds(cut, wide - cut)
+    full = slice(None)
+    units = [
+        (0, 0, True, low), (0, 1, False, low),
+        (0, 0, True, rest), (0, 1, False, rest),
+        (0, 2, True, low), (1, 0, False, full),
+        (0, 2, True, rest), (2, 0, False, full),
+    ]
+
+    def copy(unit, kind, source, target, peer):
+        return pltpu.make_async_remote_copy(
+            src_ref=source,
+            dst_ref=target,
+            send_sem=send_sem.at[unit, kind],
+            recv_sem=recv_sem.at[unit, kind],
+            device_id=peer,
+            device_id_type=pl.DeviceIdType.MESH,
+        )
+
+    def first(unit):
+        tensor, tap, x_first, cols = units[unit]
+        share, r1 = ins[tensor], scratch[tensor][0]
+        if x_first:
+            source, peer = share.at[tap, :, 1 - mx, :, :, cols], x_peer
+        else:
+            source, peer = share.at[tap, :, :, 1 - my, :, cols], y_peer
+        return [copy(unit, 0, source, r1.at[tap, :, :, :, cols], peer)]
+
+    def second(unit):
+        tensor, tap, x_first, cols = units[unit]
+        s1, r2 = scratch[tensor][1], scratch[tensor][2]
+        away, peer = (1 - my, y_peer) if x_first else (1 - mx, x_peer)
+        return [copy(unit, 1, s1.at[tap, :, away, :, cols], r2.at[tap, :, :, cols], peer)]
+
+    def third(unit):
+        tensor, tap, x_first, cols = units[unit]
+        s2, r3 = scratch[tensor][3], scratch[tensor][4]
+        return [
+            copy(
+                unit,
+                1 + d,
+                s2.at[tap, (mz + d) % high, :, cols],
+                r3.at[d - 1, tap, :, cols],
+                z_peers[d - 1],
+            )
+            for d in range(1, high)
+        ]
+
+    def fourth(unit):
+        tensor, tap, x_first, cols = units[unit]
+        place = scratch[tensor][5].at[core, tap, my, :, cols]
+        return [copy(unit, 1 + high, place, place, y_peer)]
+
+    def fifth(unit):
+        tensor, tap, x_first, cols = units[unit]
+        place = scratch[tensor][5].at[core, tap, :, :, cols]
+        return [copy(unit, 2 + high, place, place, core_peer)]
+
+    def add_first(unit):
+        tensor, tap, x_first, cols = units[unit]
+        share, r1, s1 = ins[tensor], scratch[tensor][0], scratch[tensor][1]
+        stay = share[tap, :, mx, :, :, cols] if x_first else share[tap, :, :, my, :, cols]
+        came = r1[tap, :, :, :, cols]
+        s1[tap, :, :, :, cols] = (stay.astype(jnp.float32) + came.astype(jnp.float32)).astype(
+            jnp.bfloat16
+        )
+
+    def add_second(unit):
+        tensor, tap, x_first, cols = units[unit]
+        s1, r2, s2 = scratch[tensor][1:4]
+        stay = s1[tap, :, my if x_first else mx, :, cols]
+        came = r2[tap, :, :, cols]
+        s2[tap, :, :, cols] = (stay.astype(jnp.float32) + came.astype(jnp.float32)).astype(
+            jnp.bfloat16
+        )
+
+    def add_third(unit):
+        tensor, tap, x_first, cols = units[unit]
+        s2, r3, gathered = scratch[tensor][3:6]
+        total = s2[tap, mz, :, cols].astype(jnp.float32)
+        for d in range(1, high):
+            total += r3[d - 1, tap, :, cols].astype(jnp.float32)
+        gathered[core, tap, my, :, cols] = (total * scale).astype(jnp.bfloat16)
+
+    stages = [first, second, third, fourth, fifth]
+    adds = [add_first, add_second, add_third, None]
+    steps = len(units) // 2
+    flights = {}
+
+    def start(stage, step):
+        for unit in (2 * step, 2 * step + 1):
+            flights[stage, unit] = stages[stage](unit)
+            for flight in flights[stage, unit]:
+                flight.start()
+
+    def advance(stage, step):
+        for unit in (2 * step, 2 * step + 1):
+            for flight in flights[stage, unit]:
+                flight.wait()
+            if stage < 4:
+                if adds[stage] is not None:
+                    adds[stage](unit)
+                flights[stage + 1, unit] = stages[stage + 1](unit)
+                for flight in flights[stage + 1, unit]:
+                    flight.start()
+
+    start(0, 0)
+    start(0, 1)
+    for time in range(steps + 4):
+        for stage in range(5):
+            step = time - stage
+            if 0 <= step < steps:
+                advance(stage, step)
+                if stage == 0 and step + 2 < steps:
+                    start(0, step + 2)
+    for tensor in range(3):
+        outs[tensor][...] = scratch[tensor][5][...]
+
+
+def sum_over_devices(shares, scale):
+    high = shares[0].shape[1]
+    scratch = []
+    out_shapes = []
+    for share in shares:
+        taps, _, _, _, rows, columns = share.shape
+        for shape in (
+            (taps, high, 2, rows, columns),
+            (taps, high, 2, rows, columns),
+            (taps, high, rows, columns),
+            (taps, high, rows, columns),
+            (high - 1, taps, rows, columns),
+            (2, taps, 2, rows, columns),
+        ):
+            scratch.append(pltpu.VMEM(shape, jnp.bfloat16))
+        out_shapes.append(jax.ShapeDtypeStruct((2, taps, 2, rows, columns), jnp.bfloat16))
+    semaphores = pltpu.SemaphoreType.DMA((8, high + 3))
+    size = sum(share.size for share in shares)
+    return pl.pallas_call(
+        functools.partial(sum_kernel, scale, high),
+        out_shape=out_shapes,
+        in_specs=[pl.BlockSpec(memory_space=pltpu.VMEM)] * 3,
+        out_specs=[pl.BlockSpec(memory_space=pltpu.VMEM)] * 3,
+        scratch_shapes=scratch + [semaphores, semaphores],
+        compiler_params=pltpu.CompilerParams(
+            collective_id=0, has_side_effects=True, vmem_limit_bytes=50 * 1024 * 1024
+        ),
+        cost_estimate=pl.CostEstimate(
+            flops=size, bytes_accessed=20 * size, transcendentals=0
+        ),
+    )(*shares)
 
 
 def local(latents, conv_weight, qkv_weight, out_weight, out_cotangent):
@@ -146,7 +290,6 @@
     attn_width = out_weight.shape[0]
     dp_count = lax.axis_size("dp")
     tm_count = lax.axis_size("tm")
-    bits = tm_count.bit_length() - 1
     loc = places // tm_count
     rows = half * places
     core = bit_of("dp", 0)
@@ -205,22 +348,8 @@
 
     grad_scale = 1.0 / math.sqrt(dp_count * tm_count * rows)
 
-    def by_bits(share, taps, parts):
-        channels = share.shape[0] // taps
-        size = channels // tm_count // math.prod(parts)
-        return share.reshape((taps,) + (2,) * bits + parts + (size, share.shape[1]))
-
-    def summed(share, taps):
-        share = by_bits(share, taps, (2, 2))
-        ahead = lax.index_in_dim(share, 0, bits + 1, keepdims=False)
-        behind = lax.index_in_dim(share, 1, bits + 1, keepdims=False)
-        return jnp.concatenate(
-            [
-                sum_over_devices(ahead, bits, False, grad_scale),
-                sum_over_devices(behind, bits, True, grad_scale),
-            ],
-            axis=1,
-        )
+    def by_owner(share, taps):
+        return share.reshape(taps, tm_count // 2, 2, 2, -1, share.shape[1])
 
     attended_other = swap(attended, "dp", 0)
     proj_share = (
@@ -245,9 +374,9 @@
         dot_columns(conv_left, gh_half) + dot_columns(conv_left_other, gh_half_other)
     ).astype(jnp.bfloat16)
 
-    proj_sum = sum_over_devices(by_bits(proj_share, 1, (2,)), bits, True, grad_scale)
-    qkv_sum = summed(qkv_share, 1)
-    conv_sum = summed(conv_share, 3)
+    conv_sum, qkv_sum, proj_sum = sum_over_devices(
+        [by_owner(conv_share, 3), by_owner(qkv_share, 1), by_owner(proj_share, 1)], grad_scale
+    )
 
     grad_four = grad_hidden.reshape(tm_count, half, loc, width)
     rim_after = from_behind(grad_four[:, 0], "tm", -1)
@@ -262,10 +391,13 @@
         (2, 0, 1, 3, 4),
     ).reshape(latents.shape)
 
-    proj_grad = join(proj_sum[0], "dp", 0, 1)
-    qkv_grad = join(qkv_sum[0], "dp", 0, 1)
-    conv_both = join(conv_sum[:, :, None], "dp", 0, 2)
-    conv_grad = jnp.transpose(conv_both, (1, 0, 2, 3)).reshape(conv_both.shape[1], 3 * width)
+    def assembled(gathered):
+        ordered = jnp.transpose(gathered, (2, 3, 1, 0, 4))
+        return ordered.reshape(ordered.shape[0] * ordered.shape[1], -1)
+
+    conv_grad = assembled(conv_sum)
+    qkv_grad = assembled(qkv_sum)
+    proj_grad = assembled(proj_sum)
     return (input_grad, conv_grad, qkv_grad, proj_grad)
 
 

time: 262 us -> 246 us (0.939)
  Pallas kernels: 5.86 us -> 114 us
  waiting for transfers between devices: 102 us -> 21.3 us
  starting transfers between devices: 49.8 us -> 18.1 us
  other arithmetic: 11.4 us -> 4.86 us
    pallas_call x0 -> x1, Pallas kernels: none -> 108 us  [sum_over_devices(): pl.pallas_call(functools.partial(sum_kernel, scale, high), out_shape=out_...]
    ppermute x34 -> x6, waiting for transfers between devices: 81.3 us -> 0.02 us  [swap(): lax.ppermute(shard, axis, [(i, i ^ 1 << bit) for i in range(devices)])]
    ppermute x34 -> x6, starting transfers between devices: 36.4 us -> 4.68 us  [swap(): lax.ppermute(shard, axis, [(i, i ^ 1 << bit) for i in range(devices)])]
    convert_element_type x20 -> x0, other arithmetic: 4.96 us -> none  [the longest x15 4.78 us: halve(): (stay.astype(jnp.float32) + came.astype(jnp.float32)).astype(jnp.bfloat16)]
    dot_general x5, matrix products: 13.8 us -> 10.1 us  [dot_rows_t(): lax.dot_general(left_side, right_side, (((1,), (1,)), ((), ())), preferre...]
  transfers between devices with their start and end apart: 37 -> 9, of which waited for: 16 -> 2; matrix products, arithmetic and copies ran while one was open for 21% -> 14% of each run, Pallas kernels for 0% -> 0%
where the time goes in v4:
time: 246 us; the launch traced here: 242 us
  Pallas kernels  114 us (46%)
  blocking collectives  33.5 us (14%)
  matrix products  31.6 us (13%)
  waiting for transfers between devices  21.3 us (9%)
  local copies, waits for them, and re-layouts  18.1 us (7%)
  starting transfers between devices  18.1 us (7%)
  other arithmetic  4.86 us (2%)
    pallas_call x1, Pallas kernels, sum_over_devices(): pl.pallas_call(functools.partial(sum_kernel, scale, high), out_shape=out_...  108 us
    all_to_all x1, blocking collectives, local(): lax.all_to_all(outgoing, 'tm', split_axis=0, concat_axis=0, tiled=True)  33.5 us
    all_to_all x1, waiting for transfers between devices, local(): lax.all_to_all(result.reshape(tm_count, half * loc, 4 * attn_width), 'tm'...  20.7 us
    dot_general x6, matrix products, dot_columns(): lax.dot_general(left_side, right_side, (((0,), (0,)), ((), ())), preferre...  13.6 us
    dot_general x5, matrix products, dot_rows_t(): lax.dot_general(left_side, right_side, (((1,), (1,)), ((), ())), preferre...  10.1 us
    dot_general x4, matrix products, dot_rows(): return jnp.dot(left_side, right_side, preferred_element_type=jnp.float32)  8 us
    ppermute x2, starting transfers between devices, from_behind(): return lax.ppermute(shard, axis, pairs)  7.93 us
    pallas_call x1, Pallas kernels, attention(): pl.pallas_call(functools.partial(attention_kernel, loc, width), out_shape...  5.87 us
  transfers between devices with their start and end apart: 9, of which 2 were waited for; matrix products, arithmetic and copies ran while one was open for 14% of the time, Pallas kernels for 0%

profile of v4, /device:TPU:17, one launch (start us, length us, event | category | flops | bytes accessed | tf_op | source)
XLA Modules:
  0.0 242.4 jit_solution(16553464614089240045)
XLA Ops:
  0.6 1.1 slice_bitcast_fusion.1
  1.7 3.1 %collective-permute-start = (bf16[8,8,1280]{2,1,0:T(8,128)(2,1)S(1)}, bf16[8,8,1280]{2,1,0:T(8,128)(2,1)S(1)}, u32[]{:S(2)}, u32[]{:S(2)}) collective-permute-start(bf16[8,8,1280]{2,1,0:T(8,128)(2,1)S(1)} %slice_bitcast_fusion.1), channel_id=1, source_target_pairs={{0,1},{1,2},{2,3},{3,4},{4,5},{5,6},{6,7},{8,9},{9,10},{10,11},{11... | collective-permute-start | bytes 491528 | tf_op jit(solution)/shard_map/ppermute | solution.py:21
  4.8 1.4 fusion.47
  7.5 3.2 %fusion.6 = f32[256,1280]{1,0:T(8,128)S(1)} fusion(bf16[256,1280]{1,0:T(8,128)(2,1)S(1)} %bitcast.73, bf16[1280,3840]{1,0:T(8,128)(2,1)} %param.6), kind=kOutput, calls=%fused_computation.8 | convolution fusion | flops 838860800 | bytes 5242880 | tf_op jit(solution)/shard_map/dot_general | solution.py:34
  12.5 1.0 fusion.12
  13.6 1.1 fusion.48
  15.0 1.0 fusion.33
  16.0 2.7 %convolution_convert_fusion = bf16[256,1920]{1,0:T(8,128)(2,1)S(1)} fusion(bf16[256,1280]{1,0:T(8,128)(2,1)} %fusion.33, bf16[1280,1920]{1,0:T(8,128)(2,1)S(1)} %bitcast.102), kind=kOutput, calls=%fused_computation.21 | convolution fusion | flops 1258782720 | bytes 6553600 | tf_op jit(solution)/shard_map/dot_general | solution.py:34
  18.8 33.5 %all_to_all.10 = bf16[8,32,2560]{2,1,0:T(8,128)(2,1)S(1)} all-to-all(bf16[8,32,2560]{2,1,0:T(8,128)(2,1)S(1)} %bitcast.87), channel_id=1, replica_groups=mesh['dp'=4,'tm'=8] {'tm'}, dimensions={0} | all-to-all | bytes 2621440 | tf_op jit(solution)/shard_map/all_to_all | solution.py:337
  52.3 5.9 %shard_map.84 = bf16[256,2560]{1,0:T(8,128)(2,1)} custom-call(bf16[256,2560]{1,0:T(8,128)(2,1)S(1)} %bitcast.63), custom_call_target="tpu_custom_call" | custom-call | flops 1174405120 | bytes 2621440 | tf_op jit(solution)/shard_map/pallas_call | solution.py:100
  58.1 5.5 %all-to-all-start.1 = ((bf16[8,32,2560]{2,1,0:T(8,128)(2,1)}), bf16[8,32,2560]{2,1,0:T(8,128)(2,1)S(1)}, u32[]{:S(2)}, u32[]{:S(2)}) async-start(bf16[8,32,2560]{2,1,0:T(8,128)(2,1)} %bitcast.15), calls=%async_computation.1 | async-start | bytes 2621440 | tf_op jit(solution)/shard_map/all_to_all | solution.py:339
  63.7 1.7 constant_dynamic-slice_fusion
  65.4 1.7 collective-permute-start.7
  67.1 2.7 %pad_maximum_fusion = bf16[256,3840]{1,0:T(8,128)(2,1)} fusion(bf16[256,1280]{1,0:T(8,128)(2,1)} %bitcast.77, bf16[256,1280]{1,0:T(8,128)(2,1)S(1)} %bitcast.74, bf16[256,1280]{1,0:T(8,128)(2,1)} %bitcast.80), kind=kLoop, calls=%fused_computation.22 | loop fusion | flops 5898240 | bytes 3932160 | tf_op jit(solution)/shard_map/concatenate | solution.py:319
  70.3 20.7 %all-to-all-done.1 = bf16[8,32,2560]{2,1,0:T(8,128)(2,1)S(1)} async-done(((bf16[8,32,2560]{2,1,0:T(8,128)(2,1)}), bf16[8,32,2560]{2,1,0:T(8,128)(2,1)S(1)}, u32[]{:S(2)}, u32[]{:S(2)}) %all-to-all-start.1) | async-done | bytes 1310752 | tf_op jit(solution)/shard_map/all_to_all | solution.py:339
  91.0 4.1 %fusion.46 = (f32[256]{0:T(256)S(1)}, f32[256]{0:T(256)S(1)}, f32[256,1280]{1,0:T(8,128)S(1)}) fusion(f32[256]{0:T(256)S(1)} %add_rsqrt_fusion, f32[256,1280]{1,0:T(8,128)S(1)} %get-tuple-element.16, f32[256]{0:T(256)S(1)} %broadcast_multiply_fusion.2, bf16[1280,1920]{1,0:T(8,128)(2,1)} %param.7, bf16[256,2560]{1,0:T(8,128)(2,1)S(1)} %bitcast.69), kind=kOutput, calls=%fused_computation.56 | convolution fusion | flops 1259929088 | bytes 8523776 | tf_op jit(solution)/shard_map/dot_general | solution.py:38
  95.2 1.0 copy-done.7
  96.7 3.1 %fusion = f32[256,1280]{1,0:T(8,128)S(1)} fusion(bf16[256,1280]{1,0:T(8,128)(2,1)S(1)} %add_convert_fusion.3, bf16[1280,3840]{1,0:T(8,128)(2,1)} %param.6), kind=kOutput, calls=%fused_computation.2 | convolution fusion | flops 838860800 | bytes 5242880 | tf_op jit(solution)/shard_map/dot_general | solution.py:38
  99.8 1.7 fusion.38
  101.6 2.3 fusion.34
  104.4 4.8 %collective-permute-start.1 = (bf16[8,8,1280]{2,1,0:T(8,128)(2,1)S(1)}, bf16[8,8,1280]{2,1,0:T(8,128)(2,1)S(1)}, u32[]{:S(2)}, u32[]{:S(2)}) collective-permute-start(bf16[8,8,1280]{2,1,0:T(8,128)(2,1)S(1)} %slice_bitcast_fusion), channel_id=1, source_target_pairs={{1,0},{2,1},{3,2},{4,3},{5,4},{6,5},{7,6},{9,8},{10,9},{11,10},{12... | collective-permute-start | bytes 491528 | tf_op jit(solution)/shard_map/ppermute | solution.py:21
  109.2 1.1 fusion.21
  112.0 1.7 collective-permute-start.6
  113.8 1.1 fusion.30
  115.0 1.1 copy.26
  116.2 1.4 add_convert_fusion.2
  117.7 5.6 %add_convert_fusion = bf16[3840,640]{1,0:T(8,128)(2,1)} fusion(f32[3840,640]{1,0:T(8,128)S(1)} %fusion.38, bf16[256,3840]{1,0:T(8,128)(2,1)} %collective-permute-done.2, bf16[256,640]{1,0:T(8,128)(2,1)S(1)} %collective-permute-done.3), kind=kOutput, calls=%fused_computation | convolution fusion | flops 1263206400 | bytes 17039360 | tf_op jit(solution)/shard_map/dot_general | solution.py:44
  123.3 2.0 add_convert_fusion.1
  125.3 3.6 %copy.27 = bf16[1280,960]{1,0:T(8,128)(2,1)} copy(bf16[1280,960]{0,1:T(8,128)(2,1)S(1)} %add_convert_fusion.1) | data formatting | bytes 4915200 | tf_op jit(solution)/shard_map/convert_element_type | solution.py:360
  128.9 107.9 %shard_map.85 = (bf16[2,3,2,80,640]{4,3,2,1,0:T(8,128)(2,1)S(1)}, bf16[2,1,2,80,960]{4,3,2,1,0:T(8,128)(2,1)S(1)}, bf16[2,1,2,40,640]{4,3,2,1,0:T(8,128)(2,1)S(1)}) custom-call(bf16[3,4,2,2,80,640]{5,4,3,2,1,0:T(8,128)(2,1)} %bitcast.67, bf16[1,4,2,2,80,960]{5,4,3,2,1,0:T(8,128)(2,1)} %bitcast.68, bf16[1,4,2,2,40,640]{5,4,3,2,1,0:T(8,128)(2,1)S(1)} %bitcast.62), custom_call_target="tpu_custom_call" | custom-call | flops 4096000 | bytes 81920000 | tf_op jit(solution)/shard_map/pallas_call | solution.py:272
  237.7 1.6 reshape.93
  240.0 1.5 reshape.94
  (69 shorter events, 9.2 us)
Async XLA Ops:
  0.6 10.1 %copy-start = (bf16[640,1280]{1,0:T(8,128)(2,1)S(1)}, bf16[640,1280]{1,0:T(8,128)(2,1)}, u32[]{:S(2)}) copy-start(bf16[640,1280]{1,0:T(8,128)(2,1)} %param.8) | copy-start | bytes 4915204
  1.7 9.7 %collective-permute-start = (bf16[8,8,1280]{2,1,0:T(8,128)(2,1)S(1)}, bf16[8,8,1280]{2,1,0:T(8,128)(2,1)S(1)}, u32[]{:S(2)}, u32[]{:S(2)}) collective-permute-start(bf16[8,8,1280]{2,1,0:T(8,128)(2,1)S(1)} %slice_bitcast_fusion.1), channel_id=1, source_target_pairs={{0,1},{1,2},{2,3},{3,4},{4,5},{5,6},{6,7},{8,9},{9,10},{10,11},{11... | collective-permute-start | bytes 491528 | tf_op jit(solution)/shard_map/ppermute | solution.py:21
  6.3 1.1 copy-start.8
  6.4 7.1 %copy-start.2 = (bf16[1,8,4,8,1280]{4,3,2,1,0:T(8,128)(2,1)}, bf16[1,8,4,8,1280]{4,3,2,1,0:T(8,128)(2,1)S(1)}, u32[]{:S(2)}) copy-start(bf16[1,8,4,8,1280]{4,3,2,1,0:T(8,128)(2,1)S(1)} %copy.24) | copy-start | bytes 1966084
  7.5 4.0 %copy-start.6 = (bf16[4,8,8,1280]{3,2,0,1:T(8,128)(2,1)}, bf16[4,8,8,1280]{3,2,0,1:T(8,128)(2,1)S(1)}, u32[]{:S(2)}) copy-start(bf16[4,8,8,1280]{3,2,0,1:T(8,128)(2,1)S(1)} %copy.21) | copy-start | bytes 1966084
  7.5 5.0 %copy-start.9 = (bf16[1280,3840]{1,0:T(8,128)(2,1)S(1)}, bf16[1280,3840]{1,0:T(8,128)(2,1)}, u32[]{:S(2)}) copy-start(bf16[1280,3840]{1,0:T(8,128)(2,1)} %param.6) | copy-start | bytes 29491204
  11.6 3.1 %copy-start.4 = (bf16[8,4,8,1280]{3,2,1,0:T(8,128)(2,1)}, bf16[8,4,8,1280]{3,2,1,0:T(8,128)(2,1)S(1)}, u32[]{:S(2)}) copy-start(bf16[8,4,8,1280]{3,2,1,0:T(8,128)(2,1)S(1)} %copy.22) | copy-start | bytes 1966084
  12.5 3.5 %slice-start.3 = ((s8[4915200]{0:T(1024)(128)(4,1)}), s8[4194304]{0:T(1024)(128)(4,1)S(1)}, s32[]{:S(2)}) async-start(s8[4915200]{0:T(1024)(128)(4,1)} %bitcast.101), calls=%async_computation.5 | async-start | bytes 8388608
  13.5 2.5 %slice-start.4 = ((s8[4915200]{0:T(1024)(128)(4,1)}), s8[720896]{0:T(1024)(128)(4,1)S(1)}, s32[]{:S(2)}) async-start(s8[4915200]{0:T(1024)(128)(4,1)} %bitcast.101), calls=%async_computation.6 | async-start | bytes 1441792
  58.1 32.9 %all-to-all-start.1 = ((bf16[8,32,2560]{2,1,0:T(8,128)(2,1)}), bf16[8,32,2560]{2,1,0:T(8,128)(2,1)S(1)}, u32[]{:S(2)}, u32[]{:S(2)}) async-start(bf16[8,32,2560]{2,1,0:T(8,128)(2,1)} %bitcast.15), calls=%async_computation.1 | async-start | bytes 2621440 | tf_op jit(solution)/shard_map/all_to_all | solution.py:339
  65.4 50.8 %collective-permute-start.7 = (bf16[256,640]{1,0:T(8,128)(2,1)}, bf16[256,640]{1,0:T(8,128)(2,1)}, u32[]{:S(2)}, u32[]{:S(2)}) collective-permute-start(bf16[256,640]{1,0:T(8,128)(2,1)} %constant_dynamic-slice_fusion), channel_id=1, source_target_pairs={{0,8},{8,0},{16,24},{24,16},{1,9},{9,1},{17,25},{25,17},{2,10},{10... | collective-permute-start | bytes 983048 | tf_op jit(solution)/shard_map/ppermute | solution.py:26
  67.0 56.2 %collective-permute-start.4 = (bf16[256,1280]{1,0:T(8,128)(2,1)}, bf16[256,1280]{1,0:T(8,128)(2,1)}, u32[]{:S(2)}, u32[]{:S(2)}) collective-permute-start(bf16[256,1280]{1,0:T(8,128)(2,1)} %fusion.33), channel_id=1, source_target_pairs={{0,8},{8,0},{16,24},{24,16},{1,9},{9,1},{17,25},{25,17},{2,10},{10... | collective-permute-start | bytes 1966088 | tf_op jit(solution)/shard_map/ppermute | solution.py:26
  69.8 47.9 %collective-permute-start.2 = (bf16[256,3840]{1,0:T(8,128)(2,1)}, bf16[256,3840]{1,0:T(8,128)(2,1)}, u32[]{:S(2)}, u32[]{:S(2)}) collective-permute-start(bf16[256,3840]{1,0:T(8,128)(2,1)} %pad_maximum_fusion), channel_id=1, source_target_pairs={{0,8},{8,0},{16,24},{24,16},{1,9},{9,1},{17,25},{25,17},{2,10},{10... | collective-permute-start | bytes 5898248 | tf_op jit(solution)/shard_map/ppermute | solution.py:26
  95.1 1.1 copy-start.7
  96.6 3.1 %copy-start.3 = (bf16[1,8,4,8,1280]{4,3,2,1,0:T(8,128)(2,1)S(1)}, bf16[1,8,4,8,1280]{4,3,2,1,0:T(8,128)(2,1)}, u32[]{:S(2)}) copy-start(bf16[1,8,4,8,1280]{4,3,2,1,0:T(8,128)(2,1)} %copy-done.2) | copy-start | bytes 1966084
  96.6 3.1 %copy-start.5 = (bf16[8,4,8,1280]{3,2,1,0:T(8,128)(2,1)S(1)}, bf16[8,4,8,1280]{3,2,1,0:T(8,128)(2,1)}, u32[]{:S(2)}) copy-start(bf16[8,4,8,1280]{3,2,1,0:T(8,128)(2,1)} %copy-done.4) | copy-start | bytes 1966084
  99.8 9.4 %slice-start = ((s8[9830400]{0:T(1024)(128)(4,1)}), s8[1441792]{0:T(1024)(128)(4,1)S(1)}, s32[]{:S(2)}) async-start(s8[9830400]{0:T(1024)(128)(4,1)} %bitcast.99), calls=%async_computation.2 | async-start | bytes 2883584
  99.8 9.4 %slice-start.1 = ((s8[9830400]{0:T(1024)(128)(4,1)}), s8[4194304]{0:T(1024)(128)(4,1)S(1)}, s32[]{:S(2)}) async-start(s8[9830400]{0:T(1024)(128)(4,1)} %bitcast.99), calls=%async_computation.3 | async-start | bytes 8388608
  101.6 7.6 %slice-start.2 = ((s8[9830400]{0:T(1024)(128)(4,1)}), s8[4194304]{0:T(1024)(128)(4,1)S(1)}, s32[]{:S(2)}) async-start(s8[9830400]{0:T(1024)(128)(4,1)} %bitcast.99), calls=%async_computation.4 | async-start | bytes 8388608
  104.4 7.7 %collective-permute-start.1 = (bf16[8,8,1280]{2,1,0:T(8,128)(2,1)S(1)}, bf16[8,8,1280]{2,1,0:T(8,128)(2,1)S(1)}, u32[]{:S(2)}, u32[]{:S(2)}) collective-permute-start(bf16[8,8,1280]{2,1,0:T(8,128)(2,1)S(1)} %slice_bitcast_fusion), channel_id=1, source_target_pairs={{1,0},{2,1},{3,2},{4,3},{5,4},{6,5},{7,6},{9,8},{10,9},{11,10},{12... | collective-permute-start | bytes 491528 | tf_op jit(solution)/shard_map/ppermute | solution.py:21
  110.4 7.2 %collective-permute-start.3 = (bf16[256,640]{1,0:T(8,128)(2,1)S(1)}, bf16[256,640]{1,0:T(8,128)(2,1)S(1)}, u32[]{:S(2)}, u32[]{:S(2)}) collective-permute-start(bf16[256,640]{1,0:T(8,128)(2,1)S(1)} %constant_dynamic-slice_fusion.2), channel_id=1, source_target_pairs={{0,8},{8,0},{16,24},{24,16},{1,9},{9,1},{17,25},{25,17},{2,10},{10... | collective-permute-start | bytes 983048 | tf_op jit(solution)/shard_map/ppermute | solution.py:26
  112.0 4.2 %collective-permute-start.6 = (bf16[256,640]{1,0:T(8,128)(2,1)S(1)}, bf16[256,640]{1,0:T(8,128)(2,1)S(1)}, u32[]{:S(2)}, u32[]{:S(2)}) collective-permute-start(bf16[256,640]{1,0:T(8,128)(2,1)S(1)} %slice.51), channel_id=1, source_target_pairs={{0,8},{8,0},{16,24},{24,16},{1,9},{9,1},{17,25},{25,17},{2,10},{10... | collective-permute-start | bytes 983048 | tf_op jit(solution)/shard_map/ppermute | solution.py:26
  116.2 7.1 %collective-permute-start.5 = (bf16[256,960]{1,0:T(8,128)(2,1)S(1)}, bf16[256,960]{1,0:T(8,128)(2,1)S(1)}, u32[]{:S(2)}, u32[]{:S(2)}) collective-permute-start(bf16[256,960]{1,0:T(8,128)(2,1)S(1)} %constant_dynamic-slice_fusion.1), channel_id=1, source_target_pairs={{0,8},{8,0},{16,24},{24,16},{1,9},{9,1},{17,25},{25,17},{2,10},{10... | collective-permute-start | bytes 1474568 | tf_op jit(solution)/shard_map/ppermute | solution.py:26
  239.4 3.0 %copy-start.1 = (bf16[640,1280]{1,0:T(8,128)(2,1)S(1)}, bf16[640,1280]{1,0:T(8,128)(2,1)}, u32[]{:S(2)}) copy-start(bf16[640,1280]{1,0:T(8,128)(2,1)} %param.8) | copy-start | bytes 4915204

commit v5 on v4

--- a/solution.py
+++ b/solution.py
@@ -135,10 +135,10 @@
     low, rest = pl.ds(0, cut), pl.ds(cut, wide - cut)
     full = slice(None)
     units = [
-        (0, 0, True, low), (0, 1, False, low),
-        (0, 0, True, rest), (0, 1, False, rest),
-        (0, 2, True, low), (1, 0, False, full),
-        (0, 2, True, rest), (2, 0, False, full),
+        (0, 0, False, low), (0, 1, True, low),
+        (0, 0, False, rest), (1, 0, True, full),
+        (0, 2, False, rest), (0, 1, True, rest),
+        (0, 2, False, low), (2, 0, True, full),
     ]
 
     def copy(unit, kind, source, target, peer):

time: 246 us -> 246 us (level)
  no operation moved by 1% of the time
where the time goes in v5:
time: 246 us; the launch traced here: 242 us
  Pallas kernels  113 us (46%)
  blocking collectives  33.5 us (14%)
  matrix products  31.6 us (13%)
  waiting for transfers between devices  21.3 us (9%)
  local copies, waits for them, and re-layouts  18.1 us (7%)
  starting transfers between devices  18.1 us (7%)
  other arithmetic  4.86 us (2%)
    pallas_call x1, Pallas kernels, sum_over_devices(): pl.pallas_call(functools.partial(sum_kernel, scale, high), out_shape=out_...  108 us
    all_to_all x1, blocking collectives, local(): lax.all_to_all(outgoing, 'tm', split_axis=0, concat_axis=0, tiled=True)  33.5 us
    all_to_all x1, waiting for transfers between devices, local(): lax.all_to_all(result.reshape(tm_count, half * loc, 4 * attn_width), 'tm'...  20.7 us
    dot_general x6, matrix products, dot_columns(): lax.dot_general(left_side, right_side, (((0,), (0,)), ((), ())), preferre...  13.6 us
    dot_general x5, matrix products, dot_rows_t(): lax.dot_general(left_side, right_side, (((1,), (1,)), ((), ())), preferre...  10.1 us
    dot_general x4, matrix products, dot_rows(): return jnp.dot(left_side, right_side, preferred_element_type=jnp.float32)  8 us
    ppermute x2, starting transfers between devices, from_behind(): return lax.ppermute(shard, axis, pairs)  7.93 us
    pallas_call x1, Pallas kernels, attention(): pl.pallas_call(functools.partial(attention_kernel, loc, width), out_shape...  5.87 us
  transfers between devices with their start and end apart: 9, of which 2 were waited for; matrix products, arithmetic and copies ran while one was open for 14% of the time, Pallas kernels for 0%

profile of v5, /device:TPU:17, one launch (start us, length us, event | category | flops | bytes accessed | tf_op | source)
XLA Modules:
  0.0 242.0 jit_solution(7597031300651761095)
XLA Ops:
  0.6 1.1 slice_bitcast_fusion.1
  1.7 3.1 %collective-permute-start = (bf16[8,8,1280]{2,1,0:T(8,128)(2,1)S(1)}, bf16[8,8,1280]{2,1,0:T(8,128)(2,1)S(1)}, u32[]{:S(2)}, u32[]{:S(2)}) collective-permute-start(bf16[8,8,1280]{2,1,0:T(8,128)(2,1)S(1)} %slice_bitcast_fusion.1), channel_id=1, source_target_pairs={{0,1},{1,2},{2,3},{3,4},{4,5},{5,6},{6,7},{8,9},{9,10},{10,11},{11... | collective-permute-start | bytes 491528 | tf_op jit(solution)/shard_map/ppermute | solution.py:21
  4.8 1.4 fusion.47
  7.5 3.2 %fusion.6 = f32[256,1280]{1,0:T(8,128)S(1)} fusion(bf16[256,1280]{1,0:T(8,128)(2,1)S(1)} %bitcast.73, bf16[1280,3840]{1,0:T(8,128)(2,1)} %param.6), kind=kOutput, calls=%fused_computation.8 | convolution fusion | flops 838860800 | bytes 5242880 | tf_op jit(solution)/shard_map/dot_general | solution.py:34
  12.5 1.0 fusion.12
  13.6 1.1 fusion.48
  15.0 1.0 fusion.33
  16.0 2.7 %convolution_convert_fusion = bf16[256,1920]{1,0:T(8,128)(2,1)S(1)} fusion(bf16[256,1280]{1,0:T(8,128)(2,1)} %fusion.33, bf16[1280,1920]{1,0:T(8,128)(2,1)S(1)} %bitcast.102), kind=kOutput, calls=%fused_computation.21 | convolution fusion | flops 1258782720 | bytes 6553600 | tf_op jit(solution)/shard_map/dot_general | solution.py:34
  18.8 33.5 %all_to_all.10 = bf16[8,32,2560]{2,1,0:T(8,128)(2,1)S(1)} all-to-all(bf16[8,32,2560]{2,1,0:T(8,128)(2,1)S(1)} %bitcast.87), channel_id=1, replica_groups=mesh['dp'=4,'tm'=8] {'tm'}, dimensions={0} | all-to-all | bytes 2621440 | tf_op jit(solution)/shard_map/all_to_all | solution.py:337
  52.3 5.9 %shard_map.84 = bf16[256,2560]{1,0:T(8,128)(2,1)} custom-call(bf16[256,2560]{1,0:T(8,128)(2,1)S(1)} %bitcast.63), custom_call_target="tpu_custom_call" | custom-call | flops 1174405120 | bytes 2621440 | tf_op jit(solution)/shard_map/pallas_call | solution.py:100
  58.1 5.5 %all-to-all-start.1 = ((bf16[8,32,2560]{2,1,0:T(8,128)(2,1)}), bf16[8,32,2560]{2,1,0:T(8,128)(2,1)S(1)}, u32[]{:S(2)}, u32[]{:S(2)}) async-start(bf16[8,32,2560]{2,1,0:T(8,128)(2,1)} %bitcast.15), calls=%async_computation.1 | async-start | bytes 2621440 | tf_op jit(solution)/shard_map/all_to_all | solution.py:339
  63.7 1.7 constant_dynamic-slice_fusion
  65.4 1.7 collective-permute-start.7
  67.1 2.7 %pad_maximum_fusion = bf16[256,3840]{1,0:T(8,128)(2,1)} fusion(bf16[256,1280]{1,0:T(8,128)(2,1)} %bitcast.77, bf16[256,1280]{1,0:T(8,128)(2,1)S(1)} %bitcast.74, bf16[256,1280]{1,0:T(8,128)(2,1)} %bitcast.80), kind=kLoop, calls=%fused_computation.22 | loop fusion | flops 5898240 | bytes 3932160 | tf_op jit(solution)/shard_map/concatenate | solution.py:319
  70.3 20.7 %all-to-all-done.1 = bf16[8,32,2560]{2,1,0:T(8,128)(2,1)S(1)} async-done(((bf16[8,32,2560]{2,1,0:T(8,128)(2,1)}), bf16[8,32,2560]{2,1,0:T(8,128)(2,1)S(1)}, u32[]{:S(2)}, u32[]{:S(2)}) %all-to-all-start.1) | async-done | bytes 1310752 | tf_op jit(solution)/shard_map/all_to_all | solution.py:339
  91.0 4.1 %fusion.46 = (f32[256]{0:T(256)S(1)}, f32[256]{0:T(256)S(1)}, f32[256,1280]{1,0:T(8,128)S(1)}) fusion(f32[256]{0:T(256)S(1)} %add_rsqrt_fusion, f32[256,1280]{1,0:T(8,128)S(1)} %get-tuple-element.16, f32[256]{0:T(256)S(1)} %broadcast_multiply_fusion.2, bf16[1280,1920]{1,0:T(8,128)(2,1)} %param.7, bf16[256,2560]{1,0:T(8,128)(2,1)S(1)} %bitcast.69), kind=kOutput, calls=%fused_computation.56 | convolution fusion | flops 1259929088 | bytes 8523776 | tf_op jit(solution)/shard_map/dot_general | solution.py:38
  95.2 1.0 copy-done.7
  96.7 3.1 %fusion = f32[256,1280]{1,0:T(8,128)S(1)} fusion(bf16[256,1280]{1,0:T(8,128)(2,1)S(1)} %add_convert_fusion.3, bf16[1280,3840]{1,0:T(8,128)(2,1)} %param.6), kind=kOutput, calls=%fused_computation.2 | convolution fusion | flops 838860800 | bytes 5242880 | tf_op jit(solution)/shard_map/dot_general | solution.py:38
  99.8 1.7 fusion.38
  101.6 2.3 fusion.34
  104.4 4.8 %collective-permute-start.1 = (bf16[8,8,1280]{2,1,0:T(8,128)(2,1)S(1)}, bf16[8,8,1280]{2,1,0:T(8,128)(2,1)S(1)}, u32[]{:S(2)}, u32[]{:S(2)}) collective-permute-start(bf16[8,8,1280]{2,1,0:T(8,128)(2,1)S(1)} %slice_bitcast_fusion), channel_id=1, source_target_pairs={{1,0},{2,1},{3,2},{4,3},{5,4},{6,5},{7,6},{9,8},{10,9},{11,10},{12... | collective-permute-start | bytes 491528 | tf_op jit(solution)/shard_map/ppermute | solution.py:21
  109.2 1.1 fusion.21
  112.0 1.7 collective-permute-start.6
  113.8 1.1 fusion.30
  115.0 1.1 copy.26
  116.2 1.4 add_convert_fusion.2
  117.7 5.6 %add_convert_fusion = bf16[3840,640]{1,0:T(8,128)(2,1)} fusion(f32[3840,640]{1,0:T(8,128)S(1)} %fusion.38, bf16[256,3840]{1,0:T(8,128)(2,1)} %collective-permute-done.2, bf16[256,640]{1,0:T(8,128)(2,1)S(1)} %collective-permute-done.3), kind=kOutput, calls=%fused_computation | convolution fusion | flops 1263206400 | bytes 17039360 | tf_op jit(solution)/shard_map/dot_general | solution.py:44
  123.3 2.0 add_convert_fusion.1
  125.3 3.6 %copy.27 = bf16[1280,960]{1,0:T(8,128)(2,1)} copy(bf16[1280,960]{0,1:T(8,128)(2,1)S(1)} %add_convert_fusion.1) | data formatting | bytes 4915200 | tf_op jit(solution)/shard_map/convert_element_type | solution.py:360
  128.9 107.6 %shard_map.85 = (bf16[2,3,2,80,640]{4,3,2,1,0:T(8,128)(2,1)S(1)}, bf16[2,1,2,80,960]{4,3,2,1,0:T(8,128)(2,1)S(1)}, bf16[2,1,2,40,640]{4,3,2,1,0:T(8,128)(2,1)S(1)}) custom-call(bf16[3,4,2,2,80,640]{5,4,3,2,1,0:T(8,128)(2,1)} %bitcast.67, bf16[1,4,2,2,80,960]{5,4,3,2,1,0:T(8,128)(2,1)} %bitcast.68, bf16[1,4,2,2,40,640]{5,4,3,2,1,0:T(8,128)(2,1)S(1)} %bitcast.62), custom_call_target="tpu_custom_call" | custom-call | flops 4096000 | bytes 81920000 | tf_op jit(solution)/shard_map/pallas_call | solution.py:272
  237.4 1.6 reshape.93
  239.7 1.5 reshape.94
  (69 shorter events, 9.2 us)
Async XLA Ops:
  0.6 10.1 %copy-start = (bf16[640,1280]{1,0:T(8,128)(2,1)S(1)}, bf16[640,1280]{1,0:T(8,128)(2,1)}, u32[]{:S(2)}) copy-start(bf16[640,1280]{1,0:T(8,128)(2,1)} %param.8) | copy-start | bytes 4915204
  1.7 9.7 %collective-permute-start = (bf16[8,8,1280]{2,1,0:T(8,128)(2,1)S(1)}, bf16[8,8,1280]{2,1,0:T(8,128)(2,1)S(1)}, u32[]{:S(2)}, u32[]{:S(2)}) collective-permute-start(bf16[8,8,1280]{2,1,0:T(8,128)(2,1)S(1)} %slice_bitcast_fusion.1), channel_id=1, source_target_pairs={{0,1},{1,2},{2,3},{3,4},{4,5},{5,6},{6,7},{8,9},{9,10},{10,11},{11... | collective-permute-start | bytes 491528 | tf_op jit(solution)/shard_map/ppermute | solution.py:21
  6.3 1.1 copy-start.8
  6.4 7.1 %copy-start.2 = (bf16[1,8,4,8,1280]{4,3,2,1,0:T(8,128)(2,1)}, bf16[1,8,4,8,1280]{4,3,2,1,0:T(8,128)(2,1)S(1)}, u32[]{:S(2)}) copy-start(bf16[1,8,4,8,1280]{4,3,2,1,0:T(8,128)(2,1)S(1)} %copy.24) | copy-start | bytes 1966084
  7.5 4.0 %copy-start.6 = (bf16[4,8,8,1280]{3,2,0,1:T(8,128)(2,1)}, bf16[4,8,8,1280]{3,2,0,1:T(8,128)(2,1)S(1)}, u32[]{:S(2)}) copy-start(bf16[4,8,8,1280]{3,2,0,1:T(8,128)(2,1)S(1)} %copy.21) | copy-start | bytes 1966084
  7.5 5.0 %copy-start.9 = (bf16[1280,3840]{1,0:T(8,128)(2,1)S(1)}, bf16[1280,3840]{1,0:T(8,128)(2,1)}, u32[]{:S(2)}) copy-start(bf16[1280,3840]{1,0:T(8,128)(2,1)} %param.6) | copy-start | bytes 29491204
  11.6 3.1 %copy-start.4 = (bf16[8,4,8,1280]{3,2,1,0:T(8,128)(2,1)}, bf16[8,4,8,1280]{3,2,1,0:T(8,128)(2,1)S(1)}, u32[]{:S(2)}) copy-start(bf16[8,4,8,1280]{3,2,1,0:T(8,128)(2,1)S(1)} %copy.22) | copy-start | bytes 1966084
  12.5 3.5 %slice-start.3 = ((s8[4915200]{0:T(1024)(128)(4,1)}), s8[4194304]{0:T(1024)(128)(4,1)S(1)}, s32[]{:S(2)}) async-start(s8[4915200]{0:T(1024)(128)(4,1)} %bitcast.101), calls=%async_computation.5 | async-start | bytes 8388608
  13.5 2.5 %slice-start.4 = ((s8[4915200]{0:T(1024)(128)(4,1)}), s8[720896]{0:T(1024)(128)(4,1)S(1)}, s32[]{:S(2)}) async-start(s8[4915200]{0:T(1024)(128)(4,1)} %bitcast.101), calls=%async_computation.6 | async-start | bytes 1441792
  58.1 32.9 %all-to-all-start.1 = ((bf16[8,32,2560]{2,1,0:T(8,128)(2,1)}), bf16[8,32,2560]{2,1,0:T(8,128)(2,1)S(1)}, u32[]{:S(2)}, u32[]{:S(2)}) async-start(bf16[8,32,2560]{2,1,0:T(8,128)(2,1)} %bitcast.15), calls=%async_computation.1 | async-start | bytes 2621440 | tf_op jit(solution)/shard_map/all_to_all | solution.py:339
  65.4 50.8 %collective-permute-start.7 = (bf16[256,640]{1,0:T(8,128)(2,1)}, bf16[256,640]{1,0:T(8,128)(2,1)}, u32[]{:S(2)}, u32[]{:S(2)}) collective-permute-start(bf16[256,640]{1,0:T(8,128)(2,1)} %constant_dynamic-slice_fusion), channel_id=1, source_target_pairs={{0,8},{8,0},{16,24},{24,16},{1,9},{9,1},{17,25},{25,17},{2,10},{10... | collective-permute-start | bytes 983048 | tf_op jit(solution)/shard_map/ppermute | solution.py:26
  67.0 56.2 %collective-permute-start.4 = (bf16[256,1280]{1,0:T(8,128)(2,1)}, bf16[256,1280]{1,0:T(8,128)(2,1)}, u32[]{:S(2)}, u32[]{:S(2)}) collective-permute-start(bf16[256,1280]{1,0:T(8,128)(2,1)} %fusion.33), channel_id=1, source_target_pairs={{0,8},{8,0},{16,24},{24,16},{1,9},{9,1},{17,25},{25,17},{2,10},{10... | collective-permute-start | bytes 1966088 | tf_op jit(solution)/shard_map/ppermute | solution.py:26
  69.8 47.9 %collective-permute-start.2 = (bf16[256,3840]{1,0:T(8,128)(2,1)}, bf16[256,3840]{1,0:T(8,128)(2,1)}, u32[]{:S(2)}, u32[]{:S(2)}) collective-permute-start(bf16[256,3840]{1,0:T(8,128)(2,1)} %pad_maximum_fusion), channel_id=1, source_target_pairs={{0,8},{8,0},{16,24},{24,16},{1,9},{9,1},{17,25},{25,17},{2,10},{10... | collective-permute-start | bytes 5898248 | tf_op jit(solution)/shard_map/ppermute | solution.py:26
  95.1 1.1 copy-start.7
  96.6 3.1 %copy-start.3 = (bf16[1,8,4,8,1280]{4,3,2,1,0:T(8,128)(2,1)S(1)}, bf16[1,8,4,8,1280]{4,3,2,1,0:T(8,128)(2,1)}, u32[]{:S(2)}) copy-start(bf16[1,8,4,8,1280]{4,3,2,1,0:T(8,128)(2,1)} %copy-done.2) | copy-start | bytes 1966084
  96.6 3.1 %copy-start.5 = (bf16[8,4,8,1280]{3,2,1,0:T(8,128)(2,1)S(1)}, bf16[8,4,8,1280]{3,2,1,0:T(8,128)(2,1)}, u32[]{:S(2)}) copy-start(bf16[8,4,8,1280]{3,2,1,0:T(8,128)(2,1)} %copy-done.4) | copy-start | bytes 1966084
  99.8 9.4 %slice-start = ((s8[9830400]{0:T(1024)(128)(4,1)}), s8[1441792]{0:T(1024)(128)(4,1)S(1)}, s32[]{:S(2)}) async-start(s8[9830400]{0:T(1024)(128)(4,1)} %bitcast.99), calls=%async_computation.2 | async-start | bytes 2883584
  99.8 9.4 %slice-start.1 = ((s8[9830400]{0:T(1024)(128)(4,1)}), s8[4194304]{0:T(1024)(128)(4,1)S(1)}, s32[]{:S(2)}) async-start(s8[9830400]{0:T(1024)(128)(4,1)} %bitcast.99), calls=%async_computation.3 | async-start | bytes 8388608
  101.6 7.6 %slice-start.2 = ((s8[9830400]{0:T(1024)(128)(4,1)}), s8[4194304]{0:T(1024)(128)(4,1)S(1)}, s32[]{:S(2)}) async-start(s8[9830400]{0:T(1024)(128)(4,1)} %bitcast.99), calls=%async_computation.4 | async-start | bytes 8388608
  104.4 7.7 %collective-permute-start.1 = (bf16[8,8,1280]{2,1,0:T(8,128)(2,1)S(1)}, bf16[8,8,1280]{2,1,0:T(8,128)(2,1)S(1)}, u32[]{:S(2)}, u32[]{:S(2)}) collective-permute-start(bf16[8,8,1280]{2,1,0:T(8,128)(2,1)S(1)} %slice_bitcast_fusion), channel_id=1, source_target_pairs={{1,0},{2,1},{3,2},{4,3},{5,4},{6,5},{7,6},{9,8},{10,9},{11,10},{12... | collective-permute-start | bytes 491528 | tf_op jit(solution)/shard_map/ppermute | solution.py:21
  110.4 7.2 %collective-permute-start.3 = (bf16[256,640]{1,0:T(8,128)(2,1)S(1)}, bf16[256,640]{1,0:T(8,128)(2,1)S(1)}, u32[]{:S(2)}, u32[]{:S(2)}) collective-permute-start(bf16[256,640]{1,0:T(8,128)(2,1)S(1)} %constant_dynamic-slice_fusion.2), channel_id=1, source_target_pairs={{0,8},{8,0},{16,24},{24,16},{1,9},{9,1},{17,25},{25,17},{2,10},{10... | collective-permute-start | bytes 983048 | tf_op jit(solution)/shard_map/ppermute | solution.py:26
  112.0 4.2 %collective-permute-start.6 = (bf16[256,640]{1,0:T(8,128)(2,1)S(1)}, bf16[256,640]{1,0:T(8,128)(2,1)S(1)}, u32[]{:S(2)}, u32[]{:S(2)}) collective-permute-start(bf16[256,640]{1,0:T(8,128)(2,1)S(1)} %slice.51), channel_id=1, source_target_pairs={{0,8},{8,0},{16,24},{24,16},{1,9},{9,1},{17,25},{25,17},{2,10},{10... | collective-permute-start | bytes 983048 | tf_op jit(solution)/shard_map/ppermute | solution.py:26
  116.2 7.1 %collective-permute-start.5 = (bf16[256,960]{1,0:T(8,128)(2,1)S(1)}, bf16[256,960]{1,0:T(8,128)(2,1)S(1)}, u32[]{:S(2)}, u32[]{:S(2)}) collective-permute-start(bf16[256,960]{1,0:T(8,128)(2,1)S(1)} %constant_dynamic-slice_fusion.1), channel_id=1, source_target_pairs={{0,8},{8,0},{16,24},{24,16},{1,9},{9,1},{17,25},{25,17},{2,10},{10... | collective-permute-start | bytes 1474568 | tf_op jit(solution)/shard_map/ppermute | solution.py:26
  239.0 3.0 %copy-start.1 = (bf16[640,1280]{1,0:T(8,128)(2,1)S(1)}, bf16[640,1280]{1,0:T(8,128)(2,1)}, u32[]{:S(2)}) copy-start(bf16[640,1280]{1,0:T(8,128)(2,1)} %param.8) | copy-start | bytes 4915204
